TPU v7x, 32 devices: a whole 2x2x4 slice. The times are simulated.
32 devices in a mesh: parts: 2 (over x), row: 8 (over z, core), col: 2 (over y).
Axes of the slice: x: 2, y: 2, z: 4, core: 2. Of those that a mesh axis runs over, the one named last changes fastest.
Arguments:
- pair_features_map: bfloat16 [64, 1024, 512], P(None, ('parts', 'row'), 'col'), parts along dimension 1, may hold values from -6 to 6
- labels: int32 [1024, 512], P(('parts', 'row', 'col')), parts along dimension 0, may hold values from 0 to 36, as said below
- lengths: int32 [2], P('parts'), parts along dimension 0, may hold values from 256 to 512
- conv_weight: bfloat16 [3, 3, 64, 64], replicated, may hold values from -0.25 to 0.25
- conv_bias: float32 [64], replicated, may hold values from -3 to 3
- head_weight: bfloat16 [37, 64], replicated, may hold values from -2.390625 to 2.390625
- head_bias: float32 [37], replicated, may hold values from -4 to 4
Outputs:
- pair_gradient: bfloat16 [64, 1024, 512], P(None, ('parts', 'row'), 'col'), parts along dimension 1
- grad_conv_weight: float32 [6, 3, 64, 64], P('parts'), parts along dimension 0
- grad_conv_bias: float32 [128], P('parts'), parts along dimension 0
- grad_head_weight: float32 [74, 64], P('parts'), parts along dimension 0
- grad_head_bias: float32 [74], P('parts'), parts along dimension 0
- loss: float32 [2], P('parts'), parts along dimension 0
There are 2 independent parts, one for each index of `parts`. A program takes and returns all parts, laid end to end along the dimension named above; an argument that names none is the same for every part. Nothing has to cross between parts.
Inputs may be any that keep to these rules, and one draw needn't show every extreme that they name: labels[i, j] equals labels[j, i] for every pair.
All inputs are finite; a program needn't handle non-finite values.
Results may differ from a plain program's by a relative error of at most 0.0067.
Values may be sent and summed in bfloat16 or wider, within the bound.
No kernel may reach another device: no remote copies, remote signals or barrier semaphores. Data moves between devices by JAX's collectives and lax.ppermute only.
A program may use at most 128 MiB of HBM per device.

v0:
```python
import jax
import jax.numpy as jnp
from jax import lax
from jax.sharding import PartitionSpec as P

DILATION_STEP = 4


def with_halo(cells, sides, width):
    for axis, dim in sides:
        count = lax.axis_size(axis)
        ends = count - 1
        head = lax.slice_in_dim(cells, 0, width, axis=dim)
        tail = lax.slice_in_dim(cells, cells.shape[dim] - width, cells.shape[dim], axis=dim)
        cells = jnp.concatenate(
            [
                lax.ppermute(tail, axis, [(i, (i + 1) % count) for i in range(ends)]),
                cells,
                lax.ppermute(head, axis, [((i + 1) % count, i) for i in range(ends)]),
            ],
            axis=dim,
        )
    return cells


def tile_to_band(field):
    channels, patch_rows, patch_columns = field.shape
    width = lax.axis_size("col")
    split = field.reshape(channels, width, patch_rows // width, patch_columns)
    moved = lax.all_to_all(split, "col", split_axis=1, concat_axis=3, tiled=True)
    return moved.reshape(channels, patch_rows // width, width * patch_columns)


def band_to_tile(field):
    channels, band_rows, length_cols = field.shape
    width = lax.axis_size("col")
    split = field.reshape(channels, band_rows, width, length_cols // width)
    moved = lax.all_to_all(split, "col", split_axis=2, concat_axis=1, tiled=True)
    return moved.reshape(channels, width * band_rows, length_cols // width)


def reorder_back(moved, channels, band_rows, length_cols):
    return jnp.transpose(moved, (0, 3, 2, 1)).reshape(channels, band_rows, length_cols)


def mirror_features(field):
    channels, band_rows, length_cols = field.shape
    bands = lax.axis_size(("row", "col"))
    blocks = field.reshape(channels, band_rows, bands, band_rows)
    moved = lax.all_to_all(blocks, ("row", "col"), split_axis=2, concat_axis=2, tiled=True)
    return reorder_back(moved, channels, band_rows, length_cols)


def per_device(pair_features_map, labels, lengths, conv_weight, conv_bias, head_weight, head_bias):
    channels, patch_rows, patch_columns = pair_features_map.shape
    nbins = head_weight.shape[0]
    bordered_input = with_halo(pair_features_map, (("row", 1), ("col", 2)), DILATION_STEP)
    before_activation = (
        jnp.zeros((channels, patch_rows, patch_columns), jnp.float32) + conv_bias[:, None, None]
    )
    for offset_row in range(3):
        for offset_column in range(3):
            sliding_patch = bordered_input[
                :,
                DILATION_STEP * offset_row : DILATION_STEP * offset_row + patch_rows,
                DILATION_STEP * offset_column : DILATION_STEP * offset_column + patch_columns,
            ]
            before_activation = before_activation + jnp.einsum(
                "oc,cij->oij",
                conv_weight[offset_row, offset_column],
                sliding_patch,
                preferred_element_type=jnp.float32,
            )
    hidden_tile = jnp.where(
        before_activation > 0, before_activation, jnp.expm1(jnp.minimum(before_activation, 0.0))
    ).astype(jnp.bfloat16)
    hidden = tile_to_band(hidden_tile)
    band_rows, length_cols = (hidden.shape[1], hidden.shape[2])
    hidden_mirror = mirror_features(hidden)
    direct = jnp.einsum("kc,cij->kij", head_weight, hidden, preferred_element_type=jnp.float32)
    opposite = jnp.einsum(
        "kc,cij->kij", head_weight, hidden_mirror, preferred_element_type=jnp.float32
    )
    logits = 0.5 * (direct + opposite) + head_bias[:, None, None]
    band = lax.axis_index(("row", "col"))
    row_ids = band * band_rows + lax.broadcasted_iota(jnp.int32, (band_rows, length_cols), 0)
    col_ids = lax.broadcasted_iota(jnp.int32, (band_rows, length_cols), 1)
    extent = lengths[0]
    valid = ((row_ids < extent) & (col_ids < extent)).astype(jnp.float32)
    count = (extent * extent).astype(jnp.float32)
    onehot = (lax.broadcasted_iota(jnp.int32, (nbins, 1, 1), 0) == labels[None]).astype(jnp.float32)
    lse = jnp.log(jnp.sum(jnp.exp(logits), axis=0))
    picked = jnp.sum(onehot * logits, axis=0)
    loss_local = jnp.sum(valid * (lse - picked))
    dlogits = (valid[None] * (jnp.exp(logits - lse[None]) - onehot) / count).astype(jnp.bfloat16)
    head_grad = jnp.einsum("kij,cij->kc", dlogits, hidden, preferred_element_type=jnp.float32)
    head_bias_grad = jnp.sum(dlogits.astype(jnp.float32), axis=(1, 2))
    tile_grad = band_to_tile(dlogits)
    back = jnp.einsum("kc,kij->cij", head_weight, tile_grad, preferred_element_type=jnp.float32)
    slope = jnp.where(before_activation > 0, 1.0, jnp.exp(jnp.minimum(before_activation, 0.0)))
    preact_gradient = (back * slope).astype(jnp.bfloat16)
    preact_gradient_bordered = with_halo(preact_gradient, (("row", 1), ("col", 2)), DILATION_STEP)
    grad_field = jnp.zeros((channels, patch_rows, patch_columns), jnp.float32)
    tap_rows = []
    for offset_row in range(3):
        tap_cols = []
        for offset_column in range(3):
            sliding_patch = bordered_input[
                :,
                DILATION_STEP * offset_row : DILATION_STEP * offset_row + patch_rows,
                DILATION_STEP * offset_column : DILATION_STEP * offset_column + patch_columns,
            ]
            tap_cols.append(
                jnp.einsum(
                    "oij,cij->oc",
                    preact_gradient,
                    sliding_patch,
                    preferred_element_type=jnp.float32,
                )
            )
            row_begin = DILATION_STEP * (2 - offset_row)
            column_begin = DILATION_STEP * (2 - offset_column)
            source = preact_gradient_bordered[
                :, row_begin : row_begin + patch_rows, column_begin : column_begin + patch_columns
            ]
            grad_field = grad_field + jnp.einsum(
                "oc,oij->cij",
                conv_weight[offset_row, offset_column],
                source,
                preferred_element_type=jnp.float32,
            )
        tap_rows.append(jnp.stack(tap_cols))
    conv_grad = jnp.stack(tap_rows)
    conv_bias_grad = jnp.sum(preact_gradient.astype(jnp.float32), axis=(1, 2))
    conv_grad, conv_bias_grad, head_grad, head_bias_grad, loss_total = lax.psum(
        (conv_grad, conv_bias_grad, head_grad, head_bias_grad, loss_local), ("row", "col")
    )
    loss = (loss_total / count).reshape(1)
    return (
        grad_field.astype(jnp.bfloat16),
        conv_grad,
        conv_bias_grad,
        head_grad,
        head_bias_grad,
        loss,
    )


def solution(mesh):
    return jax.shard_map(
        per_device,
        mesh=mesh,
        in_specs=(
            P(None, ("parts", "row"), "col"),
            P(("parts", "row", "col"), None),
            P("parts"),
            P(),
            P(),
            P(),
            P(),
        ),
        out_specs=(
            P(None, ("parts", "row"), "col"),
            P("parts", None, None, None),
            P("parts"),
            P("parts", None),
            P("parts"),
            P("parts"),
        ),
        check_vma=False,
    )
```

profile of v0, /device:TPU:0, one launch (start us, length us, event | category | flops | bytes accessed | tf_op | source)
XLA Modules:
  0.0 410.8 jit_solution(8611053157606536604)
XLA Ops:
  13.8 4.4 %fusion.60 = f32[64,64,256]{2,0,1:T(8,128)} fusion(bf16[3,3,64,64]{3,2,1,0:T(8,128)(2,1)} %param.10, bf16[64,64,256]{2,1,0:T(8,128)(2,1)S(1)} %copy-done.10), kind=kOutput, calls=%fused_computation.100 | convolution fusion | flops 134217728 | bytes 6307840 | tf_op jit(solution)/shard_map/oc,cij->oij/dot_general | solution.py:68
  25.1 4.9 %collective-permute-start.2 = (bf16[64,72,4]{1,0,2:T(8,128)(2,1)}, bf16[64,72,4]{1,0,2:T(8,128)(2,1)}, u32[]{:S(2)}, u32[]{:S(2)}) collective-permute-start(bf16[64,72,4]{1,0,2:T(8,128)(2,1)} %copy.58), channel_id=1, source_target_pairs={{0,1},{2,3},{4,5},{6,7},{8,9},{10,11},{12,13},{14,15},{16,17},{18,... | collective-permute-start | bytes 110600 | tf_op jit(solution)/shard_map/ppermute | solution.py:17
  33.7 4.3 %fusion.41 = f32[64,256,64]{1,2,0:T(8,128)} fusion(bf16[64,64,256]{2,0,1:T(8,128)(2,1)} %copy-done.7, bf16[64,4,256]{2,0,1:T(8,128)(2,1)} %copy-done.23, bf16[3,3,64,64]{3,2,1,0:T(8,128)(2,1)} %param.10), kind=kOutput, calls=%fused_computation.67 | convolution fusion | flops 138412032 | bytes 6438912 | tf_op jit(solution)/shard_map/oc,cij->oij/dot_general | solution.py:68
  58.1 3.9 fusion.56
  65.9 13.3 %fusion = (bf16[64,64,256]{2,0,1:T(8,128)(2,1)S(1)}, f32[64,64,256]{2,0,1:T(8,128)}) fusion(bf16[64,72,4]{2,0,1:T(8,128)(2,1)S(1)} %copy.62, bf16[64,72,256]{2,0,1:T(8,128)(2,1)S(1)} %constant_dynamic-update-slice_fusion, bf16[3,3,64,64]{3,2,1,0:T(8,128)(2,1)} %param.10, f32[64,256,64]{1,2,0:T(8,128)} %fusion.43, f32[64,256,64]{1,2,0:T(8,128)} %fusion.47, ...), kind=kOutput, calls=%fused_computation.6 | convolution fusion | flops 152043520 | bytes 42258688 | tf_op jit(solution)/shard_map/oc,cij->oij/dot_general | solution.py:68
  80.4 29.7 %all_to_all.35 = bf16[64,2,32,256]{3,2,0,1:T(8,128)(2,1)} all-to-all(bf16[64,2,32,256]{3,2,0,1:T(8,128)(2,1)S(1)} %copy.65), channel_id=1, replica_groups=mesh['parts'=2,'row'=8,'col'=2] {'col'}, dimensions={1} | all-to-all | bytes 4194304 | tf_op jit(solution)/shard_map/all_to_all | solution.py:30
  110.1 5.0 %copy.66 = bf16[64,2,32,256]{0,3,1,2:T(8,128)(2,1)} copy(bf16[64,2,32,256]{3,2,0,1:T(8,128)(2,1)} %all_to_all.35) | data formatting | bytes 4194304 | tf_op jit(solution)/shard_map/all_to_all | solution.py:30
  115.0 5.3 %copy.126 = bf16[64,32,16,32]{0,3,1,2:T(8,128)(2,1)} copy(bf16[64,32,16,32]{0,3,2,1:T(8,128)(2,1)} %bitcast.202) | data formatting | bytes 4194304 | tf_op jit(solution)/shard_map/reshape;reshape | solution.py:49
  120.3 7.5 %reshape.99 = bf16[16,2,32768]{2,1,0:T(2,128)(2,1)} reshape(bf16[16,32,32,64]{3,2,1,0:T(8,128)(2,1)} %bitcast.205) | data formatting | bytes 4194304
  127.9 6.9 %all-to-all-start.1 = ((bf16[16,2,32768]{2,1,0:T(2,128)(2,1)}), bf16[16,2,32768]{2,1,0:T(2,128)(2,1)}, u32[]{:S(2)}, u32[]{:S(2)}) async-start(bf16[16,2,32768]{2,1,0:T(2,128)(2,1)} %reshape.99), calls=%async_computation.1 | async-start | bytes 4194304 | tf_op jit(solution)/shard_map/all_to_all | solution.py:50
  136.7 6.1 %fusion.93 = f32[32,512,37]{1,2,0:T(8,128)} fusion(bf16[64,32,512]{0,2,1:T(8,128)(2,1)} %bitcast.203, bf16[37,64]{1,0:T(8,128)(2,1)S(1)} %copy-done), kind=kOutput, calls=%fused_computation.133 | convolution fusion | flops 77594624 | bytes 4526720 | tf_op jit(solution)/shard_map/kc,cij->kij/dot_general | solution.py:80
  142.9 34.0 %all-to-all-done.1 = bf16[16,2,32768]{2,1,0:T(2,128)(2,1)} async-done(((bf16[16,2,32768]{2,1,0:T(2,128)(2,1)}), bf16[16,2,32768]{2,1,0:T(2,128)(2,1)}, u32[]{:S(2)}, u32[]{:S(2)}) %all-to-all-start.1) | async-done | bytes 2097184 | tf_op jit(solution)/shard_map/all_to_all | solution.py:50
  176.9 7.4 %reshape.100 = bf16[16,32,32,64]{3,2,1,0:T(8,128)(2,1)} reshape(bf16[16,2,32768]{2,1,0:T(2,128)(2,1)} %all-to-all-done.1) | data formatting | bytes 4194304
  184.3 7.9 %fusion.10 = (f32[32,512]{1,0:T(8,128)S(1)}, f32[32,512]{1,0:T(8,128)S(1)}, f32[32,512,37]{1,2,0:T(8,128)S(1)}) fusion(s32[32,512]{1,0:T(8,128)} %param.8, f32[37]{0:T(128)} %param.13, f32[32,512,37]{1,2,0:T(8,128)} %fusion.93, bf16[37,64]{1,0:T(8,128)(2,1)S(1)} %copy-done, bf16[64,32,512]{0,1,2:T(8,128)(2,1)} %bitcast.207), kind=kOutput, calls=%fused_computation.32 | convolution fusion | flops 81805312 | bytes 7148308 | tf_op jit(solution)/shard_map/kc,cij->kij/dot_general | solution.py:81
  201.5 4.5 %all-to-all-start.2 = ((bf16[37,32,2,256]{3,1,0,2:T(8,128)(2,1)}), bf16[37,32,2,256]{3,1,0,2:T(8,128)(2,1)}, u32[]{:S(2)}, u32[]{:S(2)}) async-start(bf16[37,32,2,256]{3,1,0,2:T(8,128)(2,1)} %copy.72), calls=%async_computation.2 | async-start | bytes 2424832 | tf_op jit(solution)/shard_map/all_to_all | solution.py:38
  206.2 4.1 convolution_bitcast_fusion.7
  210.3 10.8 %all-to-all-done.2 = bf16[37,32,2,256]{3,1,0,2:T(8,128)(2,1)} async-done(((bf16[37,32,2,256]{3,1,0,2:T(8,128)(2,1)}), bf16[37,32,2,256]{3,1,0,2:T(8,128)(2,1)}, u32[]{:S(2)}, u32[]{:S(2)}) %all-to-all-start.2) | async-done | bytes 1212448 | tf_op jit(solution)/shard_map/all_to_all | solution.py:38
  223.1 4.2 %convert_reduce_fusion = (f32[64]{0:T(128)}, bf16[64,64,256]{2,0,1:T(8,128)(2,1)S(1)}) fusion(f32[64,64,256]{2,0,1:T(8,128)} %get-tuple-element.45, bf16[37,64,256]{2,0,1:T(8,128)(2,1)S(1)} %bitcast.208, bf16[37,64]{1,0:T(8,128)(2,1)S(1)} %copy-done), kind=kOutput, calls=%fused_computation.17 | convolution fusion | flops 84934592 | bytes 7508864 | tf_op jit(solution)/shard_map/kc,kij->cij/dot_general | solution.py:99
  243.0 4.4 %collective-permute-start.4 = (bf16[64,4,256]{2,0,1:T(8,128)(2,1)S(1)}, bf16[64,4,256]{2,0,1:T(8,128)(2,1)S(1)}, u32[]{:S(2)}, u32[]{:S(2)}) collective-permute-start(bf16[64,4,256]{2,0,1:T(8,128)(2,1)S(1)} %get-tuple-element.39), channel_id=1, source_target_pairs={{0,2},{2,4},{4,6},{6,8},{8,10},{10,12},{12,14},{1,3},{3,5},{5,7},{... | collective-permute-start | bytes 393224 | tf_op jit(solution)/shard_map/ppermute | solution.py:17
  249.0 62.7 %all-reduce = (f32[64]{0:T(128)}, f32[37,64]{1,0:T(8,128)}, f32[37]{0:T(128)}, f32[]{:T(128)}) all-reduce(f32[64]{0:T(128)S(1)} %copy-done.30, f32[37,64]{1,0:T(8,128)S(1)} %copy-done.26, f32[37]{0:T(128)S(1)} %get-tuple-element.30, f32[]{:T(128)} %get-tuple-element.42), channel_id=1, replica_groups=mesh['parts'=2,'row'=8,'col'=2] {'row','col'}, use_global_device_ids=true, to_apply=%region_3.4 | all-reduce | flops 2470 | bytes 19760 | tf_op jit(solution)/shard_map/psum | solution.py:135
  324.1 5.9 %collective-permute-start.7 = (bf16[64,72,4]{1,0,2:T(8,128)(2,1)}, bf16[64,72,4]{1,0,2:T(8,128)(2,1)}, u32[]{:S(2)}, u32[]{:S(2)}) collective-permute-start(bf16[64,72,4]{1,0,2:T(8,128)(2,1)} %copy.78), channel_id=1, source_target_pairs={{0,1},{2,3},{4,5},{6,7},{8,9},{10,11},{12,13},{14,15},{16,17},{18,... | collective-permute-start | bytes 110600 | tf_op jit(solution)/shard_map/ppermute | solution.py:17
  343.5 6.5 %maximum_maximum_fusion = (bf16[64,72,260]{2,0,1:T(8,128)(2,1)S(1)}, bf16[64,72,260]{2,0,1:T(8,128)(2,1)S(1)}) fusion(bf16[64,4,256]{2,0,1:T(8,128)(2,1)S(1)} %copy-done.16, bf16[64,64,256]{2,0,1:T(8,128)(2,1)S(1)} %copy-done.3, bf16[64,4,256]{2,0,1:T(8,128)(2,1)S(1)} %copy-done.18, bf16[64,72,4]{2,0,1:T(8,128)(2,1)} %copy.79, bf16[64,72,4]{2,0,1:T(8,128)(2,1)S(1)} %copy.75), kind=kLoop, calls=%fused_computation.23 | loop fusion | flops 19169280 | bytes 7225344 | tf_op jit(solution)/shard_map/concatenate | solution.py:15
  364.3 10.8 %fusion.24 = bf16[64,64,256]{2,0,1:T(8,128)(2,1)S(1)} fusion(f32[64,256,64]{1,2,0:T(8,128)} %fusion.16, f32[64,256,64]{1,2,0:T(8,128)} %fusion.29, f32[64,256,64]{1,2,0:T(8,128)} %fusion.31, f32[64,256,64]{1,2,0:T(8,128)S(1)} %copy-done.12, f32[64,256,64]{1,2,0:T(8,128)} %fusion.33, f32[64,256,64]{1,2,0:T(8,128)} %fusion.35, f32[64,256,64]{1,2,0:T(8,128)} %fusion.37, ...), kind=kOutput, calls=%fused_computation.50 | convolution fusion | flops 143654912 | bytes 37765120 | tf_op jit(solution)/shard_map/oc,oij->cij/dot_general | solution.py:126
  377.5 23.2 %all-reduce.3.cloned.1.call-done = f32[3,3,64,64]{3,2,1,0:T(8,128)} async-done(((f32[3,3,64,64]{3,2,1,0:T(8,128)}), f32[3,3,64,64]{3,2,1,0:T(8,128)}) %all-reduce.3.cloned.1.call-update) | async-done | bytes 147472 | tf_op jit(solution)/shard_map/psum | solution.py:135
  (132 shorter events, 115.8 us)
Async XLA Ops:
  7.2 129.6 %copy-start = (bf16[37,64]{1,0:T(8,128)(2,1)S(1)}, bf16[37,64]{1,0:T(8,128)(2,1)}, u32[]{:S(2)}) copy-start(bf16[37,64]{1,0:T(8,128)(2,1)} %param.12) | copy-start | bytes 14212
  7.2 6.6 %copy-start.10 = (bf16[64,64,256]{2,1,0:T(8,128)(2,1)S(1)}, bf16[64,64,256]{2,1,0:T(8,128)(2,1)}, u32[]{:S(2)}) copy-start(bf16[64,64,256]{2,1,0:T(8,128)(2,1)} %param.7) | copy-start | bytes 6291460
  10.1 8.1 %copy-start.7 = (bf16[64,64,256]{2,0,1:T(8,128)(2,1)}, bf16[64,64,256]{2,0,1:T(8,128)(2,1)S(1)}, u32[]{:S(2)}) copy-start(bf16[64,64,256]{2,0,1:T(8,128)(2,1)S(1)} %copy.55) | copy-start | bytes 6291460
  10.2 8.1 %collective-permute-start = (bf16[64,4,256]{2,0,1:T(8,128)(2,1)S(1)}, bf16[64,4,256]{2,0,1:T(8,128)(2,1)S(1)}, u32[]{:S(2)}, u32[]{:S(2)}) collective-permute-start(bf16[64,4,256]{2,0,1:T(8,128)(2,1)S(1)} %get-tuple-element.40), channel_id=1, source_target_pairs={{0,2},{2,4},{4,6},{6,8},{8,10},{10,12},{12,14},{1,3},{3,5},{5,7},{... | collective-permute-start | bytes 393224 | tf_op jit(solution)/shard_map/ppermute | solution.py:17
  12.5 6.9 %collective-permute-start.1 = (bf16[64,4,256]{2,0,1:T(8,128)(2,1)S(1)}, bf16[64,4,256]{2,0,1:T(8,128)(2,1)S(1)}, u32[]{:S(2)}, u32[]{:S(2)}) collective-permute-start(bf16[64,4,256]{2,0,1:T(8,128)(2,1)S(1)} %get-tuple-element.41), channel_id=1, source_target_pairs={{2,0},{4,2},{6,4},{8,6},{10,8},{12,10},{14,12},{3,1},{5,3},{7,5},{... | collective-permute-start | bytes 393224 | tf_op jit(solution)/shard_map/ppermute | solution.py:19
  25.1 16.2 %collective-permute-start.2 = (bf16[64,72,4]{1,0,2:T(8,128)(2,1)}, bf16[64,72,4]{1,0,2:T(8,128)(2,1)}, u32[]{:S(2)}, u32[]{:S(2)}) collective-permute-start(bf16[64,72,4]{1,0,2:T(8,128)(2,1)} %copy.58), channel_id=1, source_target_pairs={{0,1},{2,3},{4,5},{6,7},{8,9},{10,11},{12,13},{14,15},{16,17},{18,... | collective-permute-start | bytes 110600 | tf_op jit(solution)/shard_map/ppermute | solution.py:17
  32.0 19.4 %collective-permute-start.3 = (bf16[64,72,4]{1,0,2:T(8,128)(2,1)}, bf16[64,72,4]{1,0,2:T(8,128)(2,1)}, u32[]{:S(2)}, u32[]{:S(2)}) collective-permute-start(bf16[64,72,4]{1,0,2:T(8,128)(2,1)} %copy.61), channel_id=1, source_target_pairs={{1,0},{3,2},{5,4},{7,6},{9,8},{11,10},{13,12},{15,14},{17,16},{19,... | collective-permute-start | bytes 110600 | tf_op jit(solution)/shard_map/ppermute | solution.py:19
  127.9 49.0 %all-to-all-start.1 = ((bf16[16,2,32768]{2,1,0:T(2,128)(2,1)}), bf16[16,2,32768]{2,1,0:T(2,128)(2,1)}, u32[]{:S(2)}, u32[]{:S(2)}) async-start(bf16[16,2,32768]{2,1,0:T(2,128)(2,1)} %reshape.99), calls=%async_computation.1 | async-start | bytes 4194304 | tf_op jit(solution)/shard_map/all_to_all | solution.py:50
  184.3 7.9 %copy-start.29 = (pred[32]{0:T(512)(128)(4,1)S(1)}, pred[32]{0:T(512)(128)(4,1)}, u32[]{:S(2)}) copy-start(pred[32]{0:T(512)(128)(4,1)} %copy-done.28) | copy-start | bytes 100
  184.3 8.6 %copy-start.25 = (f32[32,512]{1,0:T(8,128)S(1)}, f32[32,512]{1,0:T(8,128)}, u32[]{:S(2)}) copy-start(f32[32,512]{1,0:T(8,128)} %and_convert_fusion) | copy-start | bytes 196612
  184.3 8.6 %copy-start.27 = (s32[32,512]{1,0:T(8,128)S(1)}, s32[32,512]{1,0:T(8,128)}, u32[]{:S(2)}) copy-start(s32[32,512]{1,0:T(8,128)} %param.8) | copy-start | bytes 196612
  201.5 19.6 %all-to-all-start.2 = ((bf16[37,32,2,256]{3,1,0,2:T(8,128)(2,1)}), bf16[37,32,2,256]{3,1,0,2:T(8,128)(2,1)}, u32[]{:S(2)}, u32[]{:S(2)}) async-start(bf16[37,32,2,256]{3,1,0,2:T(8,128)(2,1)} %copy.72), calls=%async_computation.2 | async-start | bytes 2424832 | tf_op jit(solution)/shard_map/all_to_all | solution.py:38
  206.0 194.7 %all-reduce.3.cloned.1.call-start = ((), (), s32[]{:S(2)}) async-start(), calls=%async_computation.3 | async-start | bytes 589824 | tf_op jit(solution)/shard_map/psum | solution.py:135
  227.3 20.9 %copy-start.2 = (bf16[64,64,256]{2,0,1:T(8,128)(2,1)}, bf16[64,64,256]{2,0,1:T(8,128)(2,1)S(1)}, u32[]{:S(2)}) copy-start(bf16[64,64,256]{2,0,1:T(8,128)(2,1)S(1)} %get-tuple-element.48) | copy-start | bytes 6291460
  238.1 9.4 %copy-start.9 = (bf16[64,64,256]{2,0,1:T(8,128)(2,1)S(1)}, bf16[64,64,256]{2,0,1:T(8,128)(2,1)}, u32[]{:S(2)}) copy-start(bf16[64,64,256]{2,0,1:T(8,128)(2,1)} %copy-done.7) | copy-start | bytes 6291460
  238.1 9.4 %copy-start.24 = (bf16[64,4,256]{2,0,1:T(8,128)(2,1)S(1)}, bf16[64,4,256]{2,0,1:T(8,128)(2,1)}, u32[]{:S(2)}) copy-start(bf16[64,4,256]{2,0,1:T(8,128)(2,1)} %copy-done.23) | copy-start | bytes 393220
  241.7 71.4 %collective-permute-start.5 = (bf16[64,4,256]{2,0,1:T(8,128)(2,1)S(1)}, bf16[64,4,256]{2,0,1:T(8,128)(2,1)S(1)}, u32[]{:S(2)}, u32[]{:S(2)}) collective-permute-start(bf16[64,4,256]{2,0,1:T(8,128)(2,1)S(1)} %get-tuple-element.38), channel_id=1, source_target_pairs={{2,0},{4,2},{6,4},{8,6},{10,8},{12,10},{14,12},{3,1},{5,3},{7,5},{... | collective-permute-start | bytes 393224 | tf_op jit(solution)/shard_map/ppermute | solution.py:19
  243.0 70.1 %collective-permute-start.4 = (bf16[64,4,256]{2,0,1:T(8,128)(2,1)S(1)}, bf16[64,4,256]{2,0,1:T(8,128)(2,1)S(1)}, u32[]{:S(2)}, u32[]{:S(2)}) collective-permute-start(bf16[64,4,256]{2,0,1:T(8,128)(2,1)S(1)} %get-tuple-element.39), channel_id=1, source_target_pairs={{0,2},{2,4},{4,6},{6,8},{8,10},{10,12},{12,14},{1,3},{3,5},{5,7},{... | collective-permute-start | bytes 393224 | tf_op jit(solution)/shard_map/ppermute | solution.py:17
  318.0 12.0 %copy-start.3 = (bf16[64,64,256]{2,0,1:T(8,128)(2,1)S(1)}, bf16[64,64,256]{2,0,1:T(8,128)(2,1)}, u32[]{:S(2)}) copy-start(bf16[64,64,256]{2,0,1:T(8,128)(2,1)} %copy-done.2) | copy-start | bytes 6291460
  318.0 12.0 %copy-start.15 = (bf16[64,4,256]{2,0,1:T(8,128)(2,1)S(1)}, bf16[64,4,256]{2,0,1:T(8,128)(2,1)}, u32[]{:S(2)}) copy-start(bf16[64,4,256]{2,0,1:T(8,128)(2,1)} %copy-done.14) | copy-start | bytes 393220
  320.8 16.2 %collective-permute-start.6 = (bf16[64,72,4]{1,0,2:T(8,128)(2,1)S(1)}, bf16[64,72,4]{1,0,2:T(8,128)(2,1)}, u32[]{:S(2)}, u32[]{:S(2)}) collective-permute-start(bf16[64,72,4]{1,0,2:T(8,128)(2,1)S(1)} %copy.74), channel_id=1, source_target_pairs={{1,0},{3,2},{5,4},{7,6},{9,8},{11,10},{13,12},{15,14},{17,16},{19,... | collective-permute-start | bytes 110600 | tf_op jit(solution)/shard_map/ppermute | solution.py:19
  324.1 9.4 %copy-start.18 = (bf16[64,4,256]{2,0,1:T(8,128)(2,1)S(1)}, bf16[64,4,256]{2,0,1:T(8,128)(2,1)}, u32[]{:S(2)}) copy-start(bf16[64,4,256]{2,0,1:T(8,128)(2,1)} %copy-done.17) | copy-start | bytes 393220
  324.1 15.7 %collective-permute-start.7 = (bf16[64,72,4]{1,0,2:T(8,128)(2,1)}, bf16[64,72,4]{1,0,2:T(8,128)(2,1)}, u32[]{:S(2)}, u32[]{:S(2)}) collective-permute-start(bf16[64,72,4]{1,0,2:T(8,128)(2,1)} %copy.78), channel_id=1, source_target_pairs={{0,1},{2,3},{4,5},{6,7},{8,9},{10,11},{12,13},{14,15},{16,17},{18,... | collective-permute-start | bytes 110600 | tf_op jit(solution)/shard_map/ppermute | solution.py:17
  364.3 38.2 %copy-start.1 = (bf16[37,64]{1,0:T(8,128)(2,1)S(1)}, bf16[37,64]{1,0:T(8,128)(2,1)}, u32[]{:S(2)}) copy-start(bf16[37,64]{1,0:T(8,128)(2,1)} %param.12) | copy-start | bytes 14212
  (19 other events, 57.2 us)
Sparse Core Ops, SparseCore 0:
  313.2 87.4 all-reduce.2
where the time goes:
time: 418 us; the launch traced here: 411 us
  matrix products  113 us (27%)
  blocking collectives  92.3 us (22%)
  local copies, waits for them, and re-layouts  72.9 us (17%)
  waiting for transfers between devices  68.1 us (16%)
  starting transfers between devices  34.7 us (8%)
  between operations  17.4 us (4%)
  other arithmetic  12.7 us (3%)
    psum x1, blocking collectives, per_device(): lax.psum((conv_grad, conv_bias_grad, head_grad, head_bias_grad, loss_loca...  62.7 us
    dot_general x9, matrix products, per_device(): jnp.einsum('oc,cij->oij', conv_weight[offset_row, offset_column], sliding...  44.2 us
    dot_general x9, matrix products, per_device(): jnp.einsum('oc,oij->cij', conv_weight[offset_row, offset_column], source,...  35.5 us
    all_to_all x1, waiting for transfers between devices, mirror_features(): lax.all_to_all(blocks, ('row', 'col'), split_axis=2, concat_axis=2, tiled...  34 us
    all_to_all x1, blocking collectives, tile_to_band(): lax.all_to_all(split, 'col', split_axis=1, concat_axis=3, tiled=True)  29.7 us
    unnamed x71, local copies, waits for them, and re-layouts  27.2 us
    psum x1, waiting for transfers between devices, per_device(): lax.psum((conv_grad, conv_bias_grad, head_grad, head_bias_grad, loss_loca...  23.2 us
    ppermute x4, starting transfers between devices, with_halo(): lax.ppermute(tail, axis, [(i, (i + 1) % count) for i in range(ends)])  17.6 us
  transfers between devices with their start and end apart: 11, of which 3 were waited for; matrix products, arithmetic and copies ran while one was open for 23% of the time, Pallas kernels for 0%

commit v1 on v0

v1 whole, which is shorter than its diff:
```python
import functools

import jax
import jax.numpy as jnp
from jax import lax
from jax.experimental import pallas as pl
from jax.experimental.pallas import tpu as pltpu
from jax.sharding import PartitionSpec as P

DIL = 4
ROWS = ("row", "col")
F32 = jnp.float32
BF16 = jnp.bfloat16


def col_exchange(to_left, to_right):
    count = lax.axis_size("col")
    if count == 2:
        at_zero = lax.axis_index("col") == 0
        got = lax.ppermute(jnp.where(at_zero, to_right, to_left), "col", [(0, 1), (1, 0)])
        none = jnp.zeros_like(got)
        return jnp.where(at_zero, none, got), jnp.where(at_zero, got, none)
    from_left = lax.ppermute(to_right, "col", [(i, i + 1) for i in range(count - 1)])
    from_right = lax.ppermute(to_left, "col", [(i + 1, i) for i in range(count - 1)])
    return from_left, from_right


def row_exchange(head, tail):
    count = lax.axis_size("row")
    above = lax.ppermute(tail, "row", [(i, i + 1) for i in range(count - 1)])
    below = lax.ppermute(head, "row", [(i + 1, i) for i in range(count - 1)])
    return above, below


def side_lanes(left, right):
    gap = jnp.zeros(left.shape[:-1] + (128 - 2 * DIL,), left.dtype)
    return jnp.concatenate([left, gap, right], axis=-1)


def take(ref, start, count, stride, tiles):
    step = ref.shape[0] // tiles
    return jnp.concatenate(
        [ref[pl.ds(start + step * u, count, stride=stride), :] for u in range(tiles)], axis=1
    )


def put(ref, start, stride, value):
    tiles = value.shape[1] // 128
    step = ref.shape[0] // tiles
    for u in range(tiles):
        ref[pl.ds(start + step * u, value.shape[0], stride=stride), :] = value[
            :, 128 * u : 128 * (u + 1)
        ]


def shifted(row, side):
    width = row.shape[1]
    lane = lax.broadcasted_iota(jnp.int32, side.shape, 1)
    before = pltpu.roll(row, DIL, 1)
    after = pltpu.roll(row, width - DIL, 1)
    first = jnp.where(lane < DIL, side, before[:, :128])
    last = jnp.where(lane >= 128 - DIL, side, after[:, width - 128 :])
    if width > 128:
        first = jnp.concatenate([first, before[:, 128:]], axis=1)
        last = jnp.concatenate([after[:, : width - 128], last], axis=1)
    return jnp.concatenate([first.astype(BF16), row.astype(BF16), last.astype(BF16)], axis=0)


def forward_kernel(scal, x, top, bot, side, w, bias, hw, xs, hid, slope, direct, *rest, rows, q):
    sends = rest[:q]
    main, sides, bordered, turned = rest[q:]
    step = pl.program_id(0)
    channels = w.shape[0]
    high = rows + 2 * DIL
    nb = hw.shape[0]
    tiles = x.shape[2] // 128

    @pl.when(step == 0)
    def _():
        def fill(c, _):
            base = pl.multiple_of(c * high, 8)
            body = x[c].astype(F32)
            rim = jnp.concatenate([top[c].astype(F32), bot[c].astype(F32)], axis=0)
            for u in range(tiles):
                at = base + u * channels * high
                lanes = slice(128 * u, 128 * (u + 1))
                main[pl.ds(at, rows), :] = body[:, lanes]
                main[pl.ds(at + rows, 2 * DIL), :] = rim[:, lanes]
            sides[pl.ds(base, high), :] = side[c].astype(F32)
            return 0

        lax.fori_loop(0, channels, fill, 0, unroll=4)

    for ii in range(8):
        i = step * 8 + ii
        at = jnp.where(i < DIL, i + rows, jnp.where(i < rows + DIL, i - DIL, i))
        row = take(main, at, channels, high, tiles)
        edge = sides[pl.ds(i, channels, stride=high), :]
        three = shifted(row, edge)
        bordered[i] = three
        xs[ii] = three

    @pl.when(step > 0)
    def _():
        for ii in range(8):
            i = (step - 1) * 8 + ii
            window = jnp.concatenate([bordered[i + DIL * a] for a in range(3)], axis=0)
            pre = jnp.dot(w[...], window, preferred_element_type=F32) + bias[...]
            grown = jnp.exp(jnp.minimum(pre, 0.0))
            h = jnp.where(pre > 0, pre, grown - 1.0).astype(BF16)
            hid[ii] = h
            slope[ii] = jnp.where(pre > 0, 1.0, grown).astype(BF16)
            put(direct, i, rows, jnp.dot(hw[...], h, preferred_element_type=F32))

    @pl.when(step == pl.num_programs(0) - 1)
    def _():
        for m in range(sends[0].shape[0]):
            for u in range(tiles):
                at = nb * rows * u + 2 * rows * m
                pair = direct[at : at + 2 * rows, :].T.astype(BF16)
                turned[2 * u, m] = pair[:rows]
                turned[2 * u + 1, m] = pair[rows:]
        for t in range(q):
            sends[t][...] = turned[scal[0] ^ t]


def middle_kernel(scal, hb, *rest, q, nbins):
    direct, labels, hid, slope, hwt = rest[:5]
    got = rest[5 : 5 + q]
    dpre, small, dl, hacc, bacc, cacc, lacc = rest[5 + q :]
    step = pl.program_id(0)
    tiles, nb = direct.shape[:2]
    channels = hwt.shape[0]

    @pl.when(step == 0)
    def _():
        hacc[...] = jnp.zeros_like(hacc)
        bacc[...] = jnp.zeros_like(bacc)
        cacc[...] = jnp.zeros_like(cacc)
        lacc[...] = jnp.zeros_like(lacc)
        dl[...] = jnp.zeros_like(dl)

    extent = scal[3]
    lane = lax.broadcasted_iota(jnp.int32, (8, 128), 1)
    row_ids = scal[1] + step * 8 + lax.broadcasted_iota(jnp.int32, (8, 128), 0)
    low = lane < 64
    area = (extent * extent).astype(F32)
    for u in range(tiles):
        lanes = slice(128 * u, 128 * (u + 1))
        col_ids = scal[2] + 128 * u + lane
        valid = jnp.where((row_ids < extent) & (col_ids < extent), 1.0, 0.0)
        wanted = labels[:, lanes]
        logits = []
        for m in range((nbins + 1) // 2):
            parts = [got[t][m].astype(F32) for t in range(q)]
            bit = 1
            while bit < q:
                swap = (scal[0] & bit) != 0
                parts = [jnp.where(swap, parts[s ^ bit], parts[s]) for s in range(q)]
                bit *= 2
            one, two = parts[2 * u], parts[2 * u + 1]
            mirror = (
                jnp.where(low, one, pltpu.roll(two, 64, 1)),
                jnp.where(low, pltpu.roll(one, 64, 1), two),
            )
            for k in range(2 * m, min(2 * m + 2, nbins)):
                logits.append(0.5 * (direct[u, k] + mirror[k - 2 * m]) + hb[k])
        peak = functools.reduce(jnp.maximum, logits)
        picked = functools.reduce(
            lambda a, b: a + b,
            [jnp.where(wanted == k, logits[k], 0.0) for k in range(nbins)],
        )
        powers = [jnp.exp(v - peak) for v in logits]
        total = functools.reduce(lambda a, b: a + b, powers)
        lacc[...] += valid * (peak + jnp.log(total) - picked)
        inverse = 1.0 / total
        scale = valid / area
        for k in range(nbins):
            d = (powers[k] * inverse - jnp.where(wanted == k, 1.0, 0.0)) * scale
            d = d.astype(BF16).astype(F32)
            at = 8 * (nb * u + k)
            dl[at : at + 8, :] = d
            bacc[8 * k : 8 * k + 8, :] += d

    for ii in range(8):
        d = take(dl, ii, nb, 8, tiles).astype(BF16)
        back = jnp.dot(hwt[...], d, preferred_element_type=F32)
        p = (back * slope[ii].astype(F32)).astype(BF16)
        dpre[ii] = p
        cacc[...] += p.astype(F32)
        hacc[0:nb, 0:channels] += lax.dot_general(
            d, hid[ii], (((1,), (1,)), ((), ())), preferred_element_type=F32
        )

    @pl.when(step == pl.num_programs(0) - 1)
    def _():
        spot = lax.broadcasted_iota(jnp.int32, small.shape, 1)
        sums = jnp.sum(bacc[...].reshape(nb, 8, 128), axis=1)
        sums = jnp.sum(sums, axis=1, keepdims=True)
        sums = jnp.concatenate([sums, jnp.zeros((channels - nb, 1), F32)], axis=0)
        biases = jnp.sum(cacc[...], axis=1, keepdims=True)
        loss = jnp.sum(jnp.sum(lacc[...], axis=1, keepdims=True), axis=0, keepdims=True)
        small[...] = jnp.where(
            spot < channels,
            hacc[...],
            jnp.where(spot == channels, sums, jnp.where(spot == channels + 1, biases, loss)),
        )


def weight_kernel(xs, dpre, small, out, acc, padded, *, rows):
    step = pl.program_id(0)
    channels = dpre.shape[1]
    wide = 3 * channels

    @pl.when(step == 0)
    def _():
        acc[...] = jnp.zeros_like(acc)
        padded[0:8] = jnp.zeros((8,) + padded.shape[1:], BF16)
        padded[8 : 8 + rows] = dpre[...]
        padded[8 + rows : 16 + rows] = jnp.zeros((8,) + padded.shape[1:], BF16)

    left = []
    for ii in range(8):
        i = step * 8 + ii + 8
        left.append(jnp.concatenate([padded[i - DIL * a] for a in range(3)], axis=0))
    left = jnp.concatenate(left, axis=1)
    right = jnp.concatenate([xs[ii] for ii in range(8)], axis=1)
    acc[...] += lax.dot_general(
        left, right, (((1,), (1,)), ((), ())), preferred_element_type=F32
    )

    @pl.when(step == pl.num_programs(0) - 1)
    def _():
        half = wide // 2
        out[0:wide, :] = acc[:, 0:128]
        out[wide : wide + half, 0:64] = acc[0:half, 128:192]
        out[wide : wide + half, 64:128] = acc[half:wide, 128:192]
        out[wide + half :, :] = small[...]


def backward_kernel(dpre, top, bot, side, w, out, bordered, turned, *, rows):
    step = pl.program_id(0)
    channels = w.shape[0]

    def place(i, row):
        bordered[i] = shifted(row.astype(F32), side[i].astype(F32))

    @pl.when(step == 0)
    def _():
        for ii in range(DIL):
            place(ii, top[ii])
            place(ii + DIL, dpre[ii])

    @pl.when((step > 0) & (step < pl.num_programs(0) - 1))
    def _():
        for ii in range(8):
            i = step * 8 + ii
            place(i, dpre[i - DIL])

    @pl.when(step == pl.num_programs(0) - 1)
    def _():
        for ii in range(DIL):
            place(rows + ii, dpre[rows - DIL + ii])
            place(rows + DIL + ii, bot[ii])

    @pl.when(step > 0)
    def _():
        for ii in range(8):
            i = (step - 1) * 8 + ii
            window = jnp.concatenate([bordered[i + DIL * a] for a in range(3)], axis=0)
            put(turned, ii, 8, jnp.dot(w[...], window, preferred_element_type=F32))
        for u in range(out.shape[2] // 128):
            at = 8 * channels * u
            block = turned[at : at + 8 * channels, :].reshape(channels, 8, 128)
            out[:, :, 128 * u : 128 * (u + 1)] = block.astype(BF16)


def full(shape):
    return pl.BlockSpec(shape, lambda *_: (0,) * len(shape))


def total_over_tiles(value):
    for axis in ("col", "row"):
        count = lax.axis_size(axis)
        if count & (count - 1):
            value = lax.psum(value, axis)
            continue
        bit = 1
        while bit < count:
            value = value + lax.ppermute(value, axis, [(i, i ^ bit) for i in range(count)])
            bit *= 2
    return value


def per_device(x, labels, lengths, conv_weight, conv_bias, head_weight, head_bias):
    channels, rows, width = x.shape
    nbins = head_weight.shape[0]
    nrow, ncol = lax.axis_size("row"), lax.axis_size("col")
    q = width // rows
    assert rows == 64 and q * rows == width and q & (q - 1) == 0 and q * ncol == nrow
    nb = -(-nbins // 8) * 8
    pairs = (nbins + 1) // 2
    high = rows + 2 * DIL
    groups = rows // 8
    tiles = width // 128
    r, c = lax.axis_index("row"), lax.axis_index("col")
    limit = pltpu.CompilerParams(vmem_limit_bytes=56 * 1024 * 1024)

    scal = jnp.stack([r % q, r * rows, c * width, lengths[0]]).astype(jnp.int32)
    w_fwd = conv_weight.transpose(2, 0, 1, 3).reshape(channels, 9 * channels)
    w_bwd = conv_weight[::-1, ::-1].transpose(3, 0, 1, 2).reshape(channels, 9 * channels)
    hw = jnp.pad(head_weight, ((0, nb - nbins), (0, 0)))

    top, bot = row_exchange(x[:, :DIL, :], x[:, rows - DIL :, :])
    tall = [top, x, bot]
    to_left = jnp.concatenate([v[:, :, :DIL] for v in tall], axis=1)
    to_right = jnp.concatenate([v[:, :, width - DIL :] for v in tall], axis=1)
    flat = (channels, high * DIL)
    left, right = col_exchange(to_left.reshape(flat), to_right.reshape(flat))
    side = side_lanes(
        left.reshape(channels, high, DIL), right.reshape(channels, high, DIL)
    )

    band = labels.shape[0]
    mine = labels.astype(BF16).reshape(band, ncol, width)
    strips = jnp.zeros((ncol, band, width), BF16)
    for d in range(ncol):
        piece = lax.dynamic_index_in_dim(mine, (c + d) % ncol, axis=1, keepdims=False)
        if d:
            piece = lax.ppermute(piece, "col", [(i, (i + d) % ncol) for i in range(ncol)])
        strips = lax.dynamic_update_index_in_dim(strips, piece, (c - d) % ncol, axis=0)
    tile_labels = strips.reshape(rows, width).astype(jnp.int32)

    outs = pl.pallas_call(
        functools.partial(forward_kernel, rows=rows, q=q),
        grid_spec=pltpu.PrefetchScalarGridSpec(
            num_scalar_prefetch=1,
            grid=(groups + 1,),
            in_specs=[
                full((channels, rows, width)),
                full((channels, DIL, width)),
                full((channels, DIL, width)),
                full((channels, high, 128)),
                full((channels, 9 * channels)),
                full((channels, 1)),
                full((nb, channels)),
            ],
            out_specs=[
                pl.BlockSpec((8, 3 * channels, width), lambda g, s: (g, 0, 0)),
                pl.BlockSpec((8, channels, width), lambda g, s: (jnp.maximum(g - 1, 0), 0, 0)),
                pl.BlockSpec((8, channels, width), lambda g, s: (jnp.maximum(g - 1, 0), 0, 0)),
                full((tiles * nb * rows, 128)),
            ]
            + [full((pairs, rows, 128))] * q,
            scratch_shapes=[
                pltpu.VMEM((tiles * channels * high, 128), F32),
                pltpu.VMEM((channels * high, 128), F32),
                pltpu.VMEM((high, 3 * channels, width), BF16),
                pltpu.VMEM((q, pairs, rows, 128), BF16),
            ],
        ),
        out_shape=[
            jax.ShapeDtypeStruct((high, 3 * channels, width), BF16),
            jax.ShapeDtypeStruct((rows, channels, width), BF16),
            jax.ShapeDtypeStruct((rows, channels, width), BF16),
            jax.ShapeDtypeStruct((tiles * nb * rows, 128), F32),
        ]
        + [jax.ShapeDtypeStruct((pairs, rows, 128), BF16)] * q,
        compiler_params=limit,
        name="forward",
    )(scal, x, top, bot, side, w_fwd, conv_bias[:, None], hw)
    xs, hid, slope, direct = outs[:4]

    got = []
    for t in range(q):
        perm = [
            (i * ncol + j, (q * j + (i % q ^ t)) * ncol + i // q)
            for i in range(nrow)
            for j in range(ncol)
        ]
        got.append(lax.ppermute(outs[4 + t], ROWS, perm))

    dpre, small = pl.pallas_call(
        functools.partial(middle_kernel, q=q, nbins=nbins),
        grid_spec=pltpu.PrefetchScalarGridSpec(
            num_scalar_prefetch=2,
            grid=(groups,),
            in_specs=[
                pl.BlockSpec((tiles, nb, 8, 128), lambda g, *_: (0, 0, g, 0)),
                pl.BlockSpec((8, width), lambda g, *_: (g, 0)),
                pl.BlockSpec((8, channels, width), lambda g, *_: (g, 0, 0)),
                pl.BlockSpec((8, channels, width), lambda g, *_: (g, 0, 0)),
                full((channels, nb)),
            ]
            + [pl.BlockSpec((pairs, 8, 128), lambda g, *_: (0, g, 0))] * q,
            out_specs=[
                pl.BlockSpec((8, channels, width), lambda g, *_: (g, 0, 0)),
                full((channels, 128)),
            ],
            scratch_shapes=[
                pltpu.VMEM((tiles * nb * 8, 128), F32),
                pltpu.VMEM((channels, 128), F32),
                pltpu.VMEM((nb * 8, 128), F32),
                pltpu.VMEM((channels, width), F32),
                pltpu.VMEM((8, 128), F32),
            ],
        ),
        out_shape=[
            jax.ShapeDtypeStruct((rows, channels, width), BF16),
            jax.ShapeDtypeStruct((channels, 128), F32),
        ],
        compiler_params=limit,
        name="middle",
    )(scal, head_bias, direct.reshape(tiles, nb, rows, 128), tile_labels, hid, slope, hw.T, *got)

    above, below = row_exchange(dpre[:DIL], dpre[rows - DIL :])
    tall = [above, dpre, below]
    to_left = jnp.concatenate([v[:, :, :DIL] for v in tall], axis=0)
    to_right = jnp.concatenate([v[:, :, width - DIL :] for v in tall], axis=0)
    flat = (high, channels * DIL)
    left, right = col_exchange(to_left.reshape(flat), to_right.reshape(flat))
    side = side_lanes(
        left.reshape(high, channels, DIL), right.reshape(high, channels, DIL)
    )

    wide = 3 * channels
    sums = pl.pallas_call(
        functools.partial(weight_kernel, rows=rows),
        grid=(groups + 1,),
        in_specs=[
            pl.BlockSpec((8, wide, width), lambda g: (g, 0, 0)),
            full((rows, channels, width)),
            full((channels, 128)),
        ],
        out_specs=full((wide + wide // 2 + channels, 128)),
        out_shape=jax.ShapeDtypeStruct((wide + wide // 2 + channels, 128), F32),
        scratch_shapes=[
            pltpu.VMEM((wide, wide), F32),
            pltpu.VMEM((rows + 16, channels, width), BF16),
        ],
        compiler_params=limit,
        name="weights",
    )(xs, dpre, small)
    sums = total_over_tiles(sums)

    pair_gradient = pl.pallas_call(
        functools.partial(backward_kernel, rows=rows),
        grid=(groups + 1,),
        in_specs=[
            full((rows, channels, width)),
            full((DIL, channels, width)),
            full((DIL, channels, width)),
            full((high, channels, 128)),
            full((channels, 9 * channels)),
        ],
        out_specs=pl.BlockSpec(
            (channels, 8, width), lambda g: (0, jnp.maximum(g - 1, 0), 0)
        ),
        out_shape=jax.ShapeDtypeStruct((channels, rows, width), BF16),
        scratch_shapes=[
            pltpu.VMEM((high, wide, width), BF16),
            pltpu.VMEM((tiles * channels * 8, 128), F32),
        ],
        compiler_params=limit,
        name="backward",
    )(dpre, above, below, side, w_bwd)

    half = wide // 2
    tail = sums[wide : wide + half]
    taps = jnp.concatenate(
        [sums[:wide], jnp.concatenate([tail[:, :64], tail[:, 64:]], axis=0)], axis=1
    )
    conv_grad = taps.reshape(3, channels, 3, channels).transpose(0, 2, 1, 3)
    rest = sums[wide + half :]
    area = (lengths[0] * lengths[0]).astype(F32)
    return (
        pair_gradient,
        conv_grad,
        rest[:, channels + 1],
        rest[:nbins, :channels],
        rest[:nbins, channels],
        (rest[0, channels + 2] / area).reshape(1),
    )


def solution(mesh):
    return jax.shard_map(
        per_device,
        mesh=mesh,
        in_specs=(
            P(None, ("parts", "row"), "col"),
            P(("parts", "row", "col"), None),
            P("parts"),
            P(),
            P(),
            P(),
            P(),
        ),
        out_specs=(
            P(None, ("parts", "row"), "col"),
            P("parts", None, None, None),
            P("parts"),
            P("parts", None),
            P("parts"),
            P("parts"),
        ),
        check_vma=False,
    )
```

time: 418 us -> 174 us (0.42); the launches traced: 411 us -> 173 us
  matrix products: 113 us -> 0 us
  blocking collectives: 92.3 us -> 0 us
  Pallas kernels: 0 us -> 53.4 us
  waiting for transfers between devices: 68.1 us -> 18.2 us
  local copies, waits for them, and re-layouts: 72.9 us -> 28.6 us
  starting transfers between devices: 34.7 us -> 63.2 us
  between operations: 17.4 us -> 3.61 us
  other arithmetic: 12.7 us -> 6.01 us
    dot_general x31 -> x0, matrix products: 113 us -> none  [the longest x9 44.2 us: per_device(): jnp.einsum('oc,cij->oij', conv_weight[offset_row, offset_column], sliding...]
    psum x1 -> x0, blocking collectives: 62.7 us -> none  [per_device(): lax.psum((conv_grad, conv_bias_grad, head_grad, head_bias_grad, loss_loca...]
    pallas_call x0 -> x4, Pallas kernels: none -> 53.4 us  [the longest x1 24.2 us: per_device(): pl.pallas_call(functools.partial(forward_kernel, rows=rows, q=q), grid_sp...]
    all_to_all x2 -> x0, waiting for transfers between devices: 44.8 us -> none  [the longest x1 34 us: mirror_features(): lax.all_to_all(blocks, ('row', 'col'), split_axis=2, concat_axis=2, tiled...]
    ppermute x8 -> x15, starting transfers between devices: 23.1 us -> 63.2 us  [the longest x4 47.2 us: total_over_tiles(): lax.ppermute(value, axis, [(i, i ^ bit) for i in range(count)])]
    all_to_all x1 -> x0, blocking collectives: 29.7 us -> none  [tile_to_band(): lax.all_to_all(split, 'col', split_axis=1, concat_axis=3, tiled=True)]
    unnamed x71 -> x30, local copies, waits for them, and re-layouts: 27.2 us -> 2.79 us
    psum x1 -> x0, waiting for transfers between devices: 23.2 us -> none  [per_device(): lax.psum((conv_grad, conv_bias_grad, head_grad, head_bias_grad, loss_loca...]
  transfers between devices with their start and end apart: 11 -> 15, of which waited for: 3 -> 5; matrix products, arithmetic and copies ran while one was open for 23% -> 16% of each run, Pallas kernels for 0% -> 25%
where the time goes in v1:
time: 174 us; the launch traced here: 173 us
  starting transfers between devices  63.2 us (36%)
  Pallas kernels  53.4 us (31%)
  local copies, waits for them, and re-layouts  28.6 us (16%)
  waiting for transfers between devices  18.2 us (10%)
  other arithmetic  6.01 us (3%)
  between operations  3.61 us (2%)
    ppermute x4, starting transfers between devices, total_over_tiles(): lax.ppermute(value, axis, [(i, i ^ bit) for i in range(count)])  47.2 us
    pallas_call x1, Pallas kernels, per_device(): pl.pallas_call(functools.partial(forward_kernel, rows=rows, q=q), grid_sp...  24.2 us
    ppermute x4, waiting for transfers between devices, per_device(): got.append(lax.ppermute(outs[4 + t], ROWS, perm))  16 us
    pallas_call x1, Pallas kernels, per_device(): pl.pallas_call(functools.partial(middle_kernel, q=q, nbins=nbins), grid_s...  10.1 us
    pallas_call x1, Pallas kernels, per_device(): pl.pallas_call(functools.partial(backward_kernel, rows=rows), grid=(group...  9.69 us
    pallas_call x1, Pallas kernels, per_device(): pl.pallas_call(functools.partial(weight_kernel, rows=rows), grid=(groups...  9.39 us
    ppermute x4, starting transfers between devices, per_device(): got.append(lax.ppermute(outs[4 + t], ROWS, perm))  5.88 us
    slice x6, local copies, waits for them, and re-layouts, per_device(): to_left = jnp.concatenate([v[:, :, :DIL] for v in tall], axis=0)  4.63 us
  transfers between devices with their start and end apart: 15, of which 5 were waited for; matrix products, arithmetic and copies ran while one was open for 16% of the time, Pallas kernels for 25%

profile of v1, /device:TPU:0, one launch (start us, length us, event | category | flops | bytes accessed | tf_op | source)
XLA Modules:
  0.0 172.9 jit_solution(9754244611485277251)
XLA Ops:
  1.8 2.4 %collective-permute-start = (bf16[64,4,256]{2,1,0:T(4,128)(2,1)S(1)}, bf16[64,4,256]{2,1,0:T(4,128)(2,1)S(1)}, u32[]{:S(2)}, u32[]{:S(2)}) collective-permute-start(bf16[64,4,256]{2,1,0:T(4,128)(2,1)S(1)} %get-tuple-element.51), channel_id=1, source_target_pairs={{0,2},{2,4},{4,6},{6,8},{8,10},{10,12},{12,14},{1,3},{3,5},{5,7},{... | collective-permute-start | bytes 393224 | tf_op jit(solution)/shard_map/ppermute | solution.py:30
  4.1 1.3 collective-permute-start.1
  6.4 2.4 %collective-permute-start.3 = (bf16[32,256]{1,0:T(8,128)(2,1)S(1)}, bf16[32,256]{1,0:T(8,128)(2,1)S(1)}, u32[]{:S(2)}, u32[]{:S(2)}) collective-permute-start(bf16[32,256]{1,0:T(8,128)(2,1)S(1)} %bitcast.43), channel_id=1, source_target_pairs={{0,1},{1,0},{2,3},{3,2},{4,5},{5,4},{6,7},{7,6},{8,9},{9,8},{10,11... | collective-permute-start | bytes 49160 | tf_op jit(solution)/shard_map/ppermute | solution.py:330
  8.9 2.0 %fusion.2 = (bf16[64,64,4]{2,1,0:T(8,128)(2,1)S(1)}, bf16[64,64,4]{2,1,0:T(8,128)(2,1)S(1)}) fusion(bf16[64,64,256]{2,1,0:T(8,128)(2,1)} %x.3), kind=kLoop, calls=%fused_computation.21 | loop fusion | bytes 131072 | tf_op jit(solution)/shard_map/slice | solution.py:316
  19.4 1.3 collective-permute-done.2
  22.2 1.7 %pad_maximum_fusion.side = bf16[64,72,128]{2,1,0:T(8,128)(2,1)} fusion(bf16[64,72,4]{2,1,0:T(8,128)(2,1)S(1)} %copy.53, bf16[64,72,4]{2,1,0:T(8,128)(2,1)S(1)} %copy.52, bf16[128]{0:T(256)(128)(2,1)S(1)} %pad.18.clone), kind=kLoop, calls=%fused_computation | loop fusion | flops 3538944 | bytes 1253632 | tf_op jit(solution)/shard_map/concatenate | solution.py:37
  23.9 24.2 %forward.1 = (bf16[72,192,256]{2,1,0:T(8,128)(2,1)}, bf16[64,64,256]{2,1,0:T(8,128)(2,1)}, bf16[64,64,256]{2,1,0:T(8,128)(2,1)}, f32[5120,128]{1,0:T(8,128)}, bf...) custom-call(s32[4]{0:T(128)} %pad_add_fusion.scal, ...), custom_call_target="tpu_custom_call" | custom-call | tf_op jit(solution)/shard_map/forward/pallas_call | solution.py:334
  48.1 1.6 collective-permute-start.4
  50.8 3.0 %collective-permute-start.6 = (bf16[19,64,128]{2,1,0:T(8,128)(2,1)}, bf16[19,64,128]{2,1,0:T(8,128)(2,1)S(1)}, u32[]{:S(2)}, u32[]{:S(2)}) collective-permute-start(bf16[19,64,128]{2,1,0:T(8,128)(2,1)} %get-tuple-element.21), channel_id=1, source_target_pairs={{0,4},{1,12},{2,6},{3,14},{4,0},{5,8},{6,2},{7,10},{8,5},{9,13},{1... | collective-permute-start | bytes 933896 | tf_op jit(solution)/shard_map/ppermute | solution.py:381
  54.6 8.7 %collective-permute-done.6.rest_7_ = bf16[19,64,128]{2,1,0:T(8,128)(2,1)S(1)} collective-permute-done((bf16[19,64,128]{2,1,0:T(8,128)(2,1)}, bf16[19,64,128]{2,1,0:T(8,128)(2,1)S(1)}, u32[]{:S(2)}, u32[]{:S(2)}) %collective-permute-start.6) | collective-permute-done | bytes 311328 | tf_op jit(solution)/shard_map/ppermute | solution.py:381
  63.3 7.3 %collective-permute-done.7.rest_8_ = bf16[19,64,128]{2,1,0:T(8,128)(2,1)S(1)} collective-permute-done((bf16[19,64,128]{2,1,0:T(8,128)(2,1)}, bf16[19,64,128]{2,1,0:T(8,128)(2,1)S(1)}, u32[]{:S(2)}, u32[]{:S(2)}) %collective-permute-start.7) | collective-permute-done | bytes 311328 | tf_op jit(solution)/shard_map/ppermute | solution.py:381
  71.4 10.1 %middle.1 = (bf16[64,64,256]{2,1,0:T(8,128)(2,1)}, f32[64,128]{1,0:T(8,128)}) custom-call(s32[4]{0:T(128)} %pad_add_fusion.scal, f32[37]{0:T(128)} %hb.1, f32[2,40,64,128]{3,2,1,0:T(8,128)} %bitcast.32, s32[64,256]{1,0:T(8,128)} %bitcast_convert_fusion.rest_1_, bf16[64,64,256]{2,1,0:T(8,128)(2,1)} %get-tuple-element.17.rest_2_, ...), custom_call_target="tpu_custom_call" | custom-call | tf_op jit(solution)/shard_map/middle/pallas_call | solution.py:383
  82.5 2.1 %collective-permute-start.8 = (bf16[4,64,256]{2,1,0:T(8,128)(2,1)S(1)}, bf16[4,64,256]{2,1,0:T(8,128)(2,1)S(1)}, u32[]{:S(2)}, u32[]{:S(2)}) collective-permute-start(bf16[4,64,256]{2,1,0:T(8,128)(2,1)S(1)} %get-tuple-element.47), channel_id=1, source_target_pairs={{0,2},{2,4},{4,6},{6,8},{8,10},{10,12},{12,14},{1,3},{3,5},{5,7},{... | collective-permute-start | bytes 393224 | tf_op jit(solution)/shard_map/ppermute | solution.py:30
  84.6 2.0 %fusion = (bf16[64,64,4]{2,1,0:T(8,128)(2,1)S(1)}, bf16[64,64,4]{2,1,0:T(8,128)(2,1)S(1)}) fusion(bf16[64,64,256]{2,1,0:T(8,128)(2,1)} %get-tuple-element.23.dpre), kind=kLoop, calls=%fused_computation.19 | loop fusion | bytes 131072 | tf_op jit(solution)/shard_map/slice | solution.py:418
  86.6 9.4 %weights.1 = f32[352,128]{1,0:T(8,128)} custom-call(bf16[72,192,256]{2,1,0:T(8,128)(2,1)} %get-tuple-element.24.xs, bf16[64,64,256]{2,1,0:T(8,128)(2,1)} %get-tuple-element.23.dpre, f32[64,128]{1,0:T(8,128)} %get-tuple-element.25.small), custom_call_target="tpu_custom_call" | custom-call | tf_op jit(solution)/shard_map/weights/pallas_call | solution.py:427
  96.0 27.6 %collective-permute-start.11 = (f32[352,128]{1,0:T(8,128)}, f32[352,128]{1,0:T(8,128)S(1)}, u32[]{:S(2)}, u32[]{:S(2)}) collective-permute-start(f32[352,128]{1,0:T(8,128)} %weights.1), channel_id=1, source_target_pairs={{0,1},{1,0},{2,3},{3,2},{4,5},{5,4},{6,7},{7,6},{8,9},{9,8},{10,11... | collective-permute-start | bytes 540680 | tf_op jit(solution)/shard_map/ppermute | solution.py:290
  126.1 1.5 collective-permute-start.9
  127.7 12.2 %collective-permute-start.12 = (f32[352,128]{1,0:T(8,128)S(1)}, f32[352,128]{1,0:T(8,128)S(1)}, u32[]{:S(2)}, u32[]{:S(2)}) collective-permute-start(f32[352,128]{1,0:T(8,128)S(1)} %add.52), channel_id=1, source_target_pairs={{0,2},{2,0},{4,6},{6,4},{8,10},{10,8},{12,14},{14,12},{1,3},{3,1},... | collective-permute-start | bytes 540680 | tf_op jit(solution)/shard_map/ppermute | solution.py:290
  144.2 3.4 %collective-permute-start.13 = (f32[352,128]{1,0:T(8,128)S(1)}, f32[352,128]{1,0:T(8,128)S(1)}, u32[]{:S(2)}, u32[]{:S(2)}) collective-permute-start(f32[352,128]{1,0:T(8,128)S(1)} %add.53), channel_id=1, source_target_pairs={{0,4},{2,6},{4,0},{6,2},{8,12},{10,14},{12,8},{14,10},{1,5},{3,7},... | collective-permute-start | bytes 540680 | tf_op jit(solution)/shard_map/ppermute | solution.py:290
  147.6 1.9 %copy.66 = bf16[72,64,4]{2,1,0:T(8,128)(2,1)S(1)} copy(bf16[72,64,4]{0,2,1:T(4,128)(2,1)S(1)} %bitcast.40) | data formatting | bytes 73728 | tf_op jit(solution)/shard_map/reshape | solution.py:423
  149.5 1.9 %copy.67 = bf16[72,64,4]{2,1,0:T(8,128)(2,1)S(1)} copy(bf16[72,64,4]{0,2,1:T(4,128)(2,1)S(1)} %bitcast.39) | data formatting | bytes 73728 | tf_op jit(solution)/shard_map/reshape | solution.py:423
  152.0 4.1 %collective-permute-start.14 = (f32[352,128]{1,0:T(8,128)S(1)}, f32[352,128]{1,0:T(8,128)S(1)}, u32[]{:S(2)}, u32[]{:S(2)}) collective-permute-start(f32[352,128]{1,0:T(8,128)S(1)} %add.54), channel_id=1, source_target_pairs={{0,8},{2,10},{4,12},{6,14},{8,0},{10,2},{12,4},{14,6},{1,9},{3,11}... | collective-permute-start | bytes 540680 | tf_op jit(solution)/shard_map/ppermute | solution.py:290
  156.1 1.8 %pad_maximum_fusion.1.side = bf16[72,64,128]{2,1,0:T(8,128)(2,1)} fusion(bf16[72,64,4]{2,1,0:T(8,128)(2,1)S(1)} %copy.67, bf16[72,64,4]{2,1,0:T(8,128)(2,1)S(1)} %copy.66, bf16[128]{0:T(256)(128)(2,1)S(1)} %pad.18.clone), kind=kLoop, calls=%fused_computation.1 | loop fusion | flops 3538944 | bytes 1253632 | tf_op jit(solution)/shard_map/concatenate | solution.py:37
  157.8 9.7 %backward.1 = bf16[64,64,256]{2,1,0:T(8,128)(2,1)} custom-call(bf16[64,64,256]{2,1,0:T(8,128)(2,1)} %get-tuple-element.23.dpre, bf16[4,64,256]{2,1,0:T(8,128)(2,1)} %copy-done.4, bf16[4,64,256]{2,1,0:T(8,128)(2,1)} %copy-done.5, bf16[72,64,128]{2,1,0:T(8,128)(2,1)} %pad_maximum_fusion.1.side, bf16[64,576]{1,0:T(8,128)(2,1)} %copy.68.w), custom_call_target="tpu_custom_call" | custom-call | tf_op jit(solution)/shard_map/backward/pallas_call | solution.py:446
  (99 shorter events, 25.7 us)
Async XLA Ops:
  1.8 11.7 %collective-permute-start = (bf16[64,4,256]{2,1,0:T(4,128)(2,1)S(1)}, bf16[64,4,256]{2,1,0:T(4,128)(2,1)S(1)}, u32[]{:S(2)}, u32[]{:S(2)}) collective-permute-start(bf16[64,4,256]{2,1,0:T(4,128)(2,1)S(1)} %get-tuple-element.51), channel_id=1, source_target_pairs={{0,2},{2,4},{4,6},{6,8},{8,10},{10,12},{12,14},{1,3},{3,5},{5,7},{... | collective-permute-start | bytes 393224 | tf_op jit(solution)/shard_map/ppermute | solution.py:30
  4.1 10.0 %collective-permute-start.1 = (bf16[64,4,256]{2,1,0:T(4,128)(2,1)S(1)}, bf16[64,4,256]{2,1,0:T(4,128)(2,1)S(1)}, u32[]{:S(2)}, u32[]{:S(2)}) collective-permute-start(bf16[64,4,256]{2,1,0:T(4,128)(2,1)S(1)} %get-tuple-element.50), channel_id=1, source_target_pairs={{2,0},{4,2},{6,4},{8,6},{10,8},{12,10},{14,12},{3,1},{5,3},{7,5},{... | collective-permute-start | bytes 393224 | tf_op jit(solution)/shard_map/ppermute | solution.py:31
  6.4 47.5 %collective-permute-start.3 = (bf16[32,256]{1,0:T(8,128)(2,1)S(1)}, bf16[32,256]{1,0:T(8,128)(2,1)S(1)}, u32[]{:S(2)}, u32[]{:S(2)}) collective-permute-start(bf16[32,256]{1,0:T(8,128)(2,1)S(1)} %bitcast.43), channel_id=1, source_target_pairs={{0,1},{1,0},{2,3},{3,2},{4,5},{5,4},{6,7},{7,6},{8,9},{9,8},{10,11... | collective-permute-start | bytes 49160 | tf_op jit(solution)/shard_map/ppermute | solution.py:330
  11.6 7.0 %copy-start.11 = (f32[64]{0:T(128)S(1)}, f32[64]{0:T(128)}, u32[]{:S(2)}) copy-start(f32[64]{0:T(128)} %param.11) | copy-start | bytes 772
  13.5 8.7 %copy-start.2 = (bf16[64,4,256]{2,1,0:T(4,128)(2,1)}, bf16[64,4,256]{2,1,0:T(4,128)(2,1)S(1)}, u32[]{:S(2)}) copy-start(bf16[64,4,256]{2,1,0:T(4,128)(2,1)S(1)} %collective-permute-done.top) | copy-start | bytes 393220
  14.2 8.0 %copy-start.3 = (bf16[64,4,256]{2,1,0:T(4,128)(2,1)}, bf16[64,4,256]{2,1,0:T(4,128)(2,1)S(1)}, u32[]{:S(2)}) copy-start(bf16[64,4,256]{2,1,0:T(4,128)(2,1)S(1)} %collective-permute-done.1.bot) | copy-start | bytes 393220
  16.3 4.4 %collective-permute-start.2 = (bf16[64,288]{0,1:T(8,128)(2,1)S(1)}, bf16[64,288]{0,1:T(8,128)(2,1)S(1)}, u32[]{:S(2)}, u32[]{:S(2)}) collective-permute-start(bf16[64,288]{0,1:T(8,128)(2,1)S(1)} %bitcast.41), channel_id=1, source_target_pairs={{0,1},{1,0},{2,3},{3,2},{4,5},{5,4},{6,7},{7,6},{8,9},{9,8},{10,11... | collective-permute-start | bytes 110600 | tf_op jit(solution)/shard_map/ppermute | solution.py:20
  48.1 6.5 %collective-permute-start.4 = (bf16[19,64,128]{2,1,0:T(8,128)(2,1)}, bf16[19,64,128]{2,1,0:T(8,128)(2,1)S(1)}, u32[]{:S(2)}, u32[]{:S(2)}) collective-permute-start(bf16[19,64,128]{2,1,0:T(8,128)(2,1)} %get-tuple-element.19), channel_id=1, source_target_pairs={{0,0},{1,8},{2,2},{3,10},{4,4},{5,12},{6,6},{7,14},{8,1},{9,9},{10... | collective-permute-start | bytes 933896 | tf_op jit(solution)/shard_map/ppermute | solution.py:381
  49.7 4.9 %collective-permute-start.5 = (bf16[19,64,128]{2,1,0:T(8,128)(2,1)}, bf16[19,64,128]{2,1,0:T(8,128)(2,1)S(1)}, u32[]{:S(2)}, u32[]{:S(2)}) collective-permute-start(bf16[19,64,128]{2,1,0:T(8,128)(2,1)} %get-tuple-element.20), channel_id=1, source_target_pairs={{0,2},{1,10},{2,0},{3,8},{4,6},{5,14},{6,4},{7,12},{8,3},{9,11},{1... | collective-permute-start | bytes 933896 | tf_op jit(solution)/shard_map/ppermute | solution.py:381
  50.8 12.5 %collective-permute-start.6 = (bf16[19,64,128]{2,1,0:T(8,128)(2,1)}, bf16[19,64,128]{2,1,0:T(8,128)(2,1)S(1)}, u32[]{:S(2)}, u32[]{:S(2)}) collective-permute-start(bf16[19,64,128]{2,1,0:T(8,128)(2,1)} %get-tuple-element.21), channel_id=1, source_target_pairs={{0,4},{1,12},{2,6},{3,14},{4,0},{5,8},{6,2},{7,10},{8,5},{9,13},{1... | collective-permute-start | bytes 933896 | tf_op jit(solution)/shard_map/ppermute | solution.py:381
  53.8 16.8 %collective-permute-start.7 = (bf16[19,64,128]{2,1,0:T(8,128)(2,1)}, bf16[19,64,128]{2,1,0:T(8,128)(2,1)S(1)}, u32[]{:S(2)}, u32[]{:S(2)}) collective-permute-start(bf16[19,64,128]{2,1,0:T(8,128)(2,1)} %get-tuple-element.22), channel_id=1, source_target_pairs={{0,6},{1,14},{2,4},{3,12},{4,2},{5,10},{6,0},{7,8},{8,7},{9,15},{1... | collective-permute-start | bytes 933896 | tf_op jit(solution)/shard_map/ppermute | solution.py:381
  54.6 16.0 %copy-start.6 = (bf16[19,64,128]{2,1,0:T(8,128)(2,1)}, bf16[19,64,128]{2,1,0:T(8,128)(2,1)S(1)}, u32[]{:S(2)}) copy-start(bf16[19,64,128]{2,1,0:T(8,128)(2,1)S(1)} %collective-permute-done.4.rest_5_) | copy-start | bytes 933892
  54.6 16.0 %copy-start.7 = (bf16[19,64,128]{2,1,0:T(8,128)(2,1)}, bf16[19,64,128]{2,1,0:T(8,128)(2,1)S(1)}, u32[]{:S(2)}) copy-start(bf16[19,64,128]{2,1,0:T(8,128)(2,1)S(1)} %collective-permute-done.5.rest_6_) | copy-start | bytes 933892
  63.3 7.3 %copy-start.8 = (bf16[19,64,128]{2,1,0:T(8,128)(2,1)}, bf16[19,64,128]{2,1,0:T(8,128)(2,1)S(1)}, u32[]{:S(2)}) copy-start(bf16[19,64,128]{2,1,0:T(8,128)(2,1)S(1)} %collective-permute-done.6.rest_7_) | copy-start | bytes 933892
  82.5 45.1 %collective-permute-start.8 = (bf16[4,64,256]{2,1,0:T(8,128)(2,1)S(1)}, bf16[4,64,256]{2,1,0:T(8,128)(2,1)S(1)}, u32[]{:S(2)}, u32[]{:S(2)}) collective-permute-start(bf16[4,64,256]{2,1,0:T(8,128)(2,1)S(1)} %get-tuple-element.47), channel_id=1, source_target_pairs={{0,2},{2,4},{4,6},{6,8},{8,10},{10,12},{12,14},{1,3},{3,5},{5,7},{... | collective-permute-start | bytes 393224 | tf_op jit(solution)/shard_map/ppermute | solution.py:30
  96.0 31.7 %copy-start = (f32[352,128]{1,0:T(8,128)S(1)}, f32[352,128]{1,0:T(8,128)}, u32[]{:S(2)}) copy-start(f32[352,128]{1,0:T(8,128)} %weights.1) | copy-start | bytes 540676
  96.0 31.7 %collective-permute-start.11 = (f32[352,128]{1,0:T(8,128)}, f32[352,128]{1,0:T(8,128)S(1)}, u32[]{:S(2)}, u32[]{:S(2)}) collective-permute-start(f32[352,128]{1,0:T(8,128)} %weights.1), channel_id=1, source_target_pairs={{0,1},{1,0},{2,3},{3,2},{4,5},{5,4},{6,7},{7,6},{8,9},{9,8},{10,11... | collective-permute-start | bytes 540680 | tf_op jit(solution)/shard_map/ppermute | solution.py:290
  126.1 14.3 %collective-permute-start.9 = (bf16[4,64,256]{2,1,0:T(8,128)(2,1)S(1)}, bf16[4,64,256]{2,1,0:T(8,128)(2,1)S(1)}, u32[]{:S(2)}, u32[]{:S(2)}) collective-permute-start(bf16[4,64,256]{2,1,0:T(8,128)(2,1)S(1)} %get-tuple-element.46), channel_id=1, source_target_pairs={{2,0},{4,2},{6,4},{8,6},{10,8},{12,10},{14,12},{3,1},{5,3},{7,5},{... | collective-permute-start | bytes 393224 | tf_op jit(solution)/shard_map/ppermute | solution.py:31
  127.6 21.9 %copy-start.4 = (bf16[4,64,256]{2,1,0:T(8,128)(2,1)}, bf16[4,64,256]{2,1,0:T(8,128)(2,1)S(1)}, u32[]{:S(2)}) copy-start(bf16[4,64,256]{2,1,0:T(8,128)(2,1)S(1)} %collective-permute-done.8.top) | copy-start | bytes 393220
  127.7 16.4 %collective-permute-start.12 = (f32[352,128]{1,0:T(8,128)S(1)}, f32[352,128]{1,0:T(8,128)S(1)}, u32[]{:S(2)}, u32[]{:S(2)}) collective-permute-start(f32[352,128]{1,0:T(8,128)S(1)} %add.52), channel_id=1, source_target_pairs={{0,2},{2,0},{4,6},{6,4},{8,10},{10,8},{12,14},{14,12},{1,3},{3,1},... | collective-permute-start | bytes 540680 | tf_op jit(solution)/shard_map/ppermute | solution.py:290
  140.4 11.1 %copy-start.5 = (bf16[4,64,256]{2,1,0:T(8,128)(2,1)}, bf16[4,64,256]{2,1,0:T(8,128)(2,1)S(1)}, u32[]{:S(2)}) copy-start(bf16[4,64,256]{2,1,0:T(8,128)(2,1)S(1)} %collective-permute-done.9.bot) | copy-start | bytes 393220
  143.0 4.5 %collective-permute-start.10 = (bf16[72,256]{0,1:T(8,128)(2,1)S(1)}, bf16[72,256]{0,1:T(8,128)(2,1)S(1)}, u32[]{:S(2)}, u32[]{:S(2)}) collective-permute-start(bf16[72,256]{0,1:T(8,128)(2,1)S(1)} %bitcast.42), channel_id=1, source_target_pairs={{0,1},{1,0},{2,3},{3,2},{4,5},{5,4},{6,7},{7,6},{8,9},{9,8},{10,11... | collective-permute-start | bytes 110600 | tf_op jit(solution)/shard_map/ppermute | solution.py:20
  144.2 7.8 %collective-permute-start.13 = (f32[352,128]{1,0:T(8,128)S(1)}, f32[352,128]{1,0:T(8,128)S(1)}, u32[]{:S(2)}, u32[]{:S(2)}) collective-permute-start(f32[352,128]{1,0:T(8,128)S(1)} %add.53), channel_id=1, source_target_pairs={{0,4},{2,6},{4,0},{6,2},{8,12},{10,14},{12,8},{14,10},{1,5},{3,7},... | collective-permute-start | bytes 540680 | tf_op jit(solution)/shard_map/ppermute | solution.py:290
  152.0 15.5 %collective-permute-start.14 = (f32[352,128]{1,0:T(8,128)S(1)}, f32[352,128]{1,0:T(8,128)S(1)}, u32[]{:S(2)}, u32[]{:S(2)}) collective-permute-start(f32[352,128]{1,0:T(8,128)S(1)} %add.54), channel_id=1, source_target_pairs={{0,8},{2,10},{4,12},{6,14},{8,0},{10,2},{12,4},{14,6},{1,9},{3,11}... | collective-permute-start | bytes 540680 | tf_op jit(solution)/shard_map/ppermute | solution.py:290
  (3 other events, 9.4 us)

commit v2 on v0

v2 whole, which is shorter than its diff:
```python
import functools

import jax
import jax.numpy as jnp
from jax import lax
from jax.experimental import pallas as pl
from jax.experimental.pallas import tpu as pltpu
from jax.sharding import PartitionSpec as P

DIL = 4
ROWS = ("row", "col")
F32 = jnp.float32
BF16 = jnp.bfloat16
VM = pl.BlockSpec(memory_space=pltpu.VMEM)
SM = pl.BlockSpec(memory_space=pltpu.SMEM)
MIB = 1024 * 1024


def grant(mib):
    return pltpu.CompilerParams(vmem_limit_bytes=mib * MIB)


def cost(us):
    return pl.CostEstimate(flops=int(us * 1.1e9), transcendentals=0, bytes_accessed=0)


def call(body, name, out_shape, args, us, smem=0, scratch=(), aliases=None, mib=4):
    return pl.pallas_call(
        body,
        out_shape=out_shape,
        in_specs=[SM] * smem + [VM] * (len(args) - smem),
        out_specs=jax.tree.map(lambda _: VM, out_shape),
        scratch_shapes=list(scratch),
        input_output_aliases=aliases or {},
        compiler_params=grant(mib),
        cost_estimate=cost(us),
        name=name,
    )(*args)


def shape(dims, dtype=BF16):
    return jax.ShapeDtypeStruct(dims, dtype)


def pairs_of(tiles):
    return jnp.concatenate(tiles, axis=1)


def prep_kernel(x, out, head, tail, main):
    some, rows, width = x.shape
    tiles, _, channels, _ = out.shape
    step = pl.program_id(0)

    for cc in range(some):
        body = x[cc].astype(F32)
        for u in range(tiles):
            at = pl.multiple_of((u * channels + step * some + cc) * rows, 8)
            main[pl.ds(at, rows), :] = body[:, 128 * u : 128 * (u + 1)]

    @pl.when(step == pl.num_programs(0) - 1)
    def _():
        def turn(i, _):
            for u in range(tiles):
                at = u * channels * rows + i
                out[u, i] = main[pl.ds(at, channels, stride=rows), :].astype(BF16)
            return 0

        lax.fori_loop(0, rows, turn, 0, unroll=8)
        for u in range(tiles):
            head[u] = out[u, :DIL]
            tail[u] = out[u, rows - DIL :]


def edges_kernel(scal, field, above, below, *sides, ncol):
    tiles, rows, channels, _ = field.shape
    lane = lax.broadcasted_iota(jnp.int32, (channels, 128), 1) // DIL
    if ncol == 2:
        first = scal[4] == 0
        picks = [(jnp.where(first, tiles - 1, 0), jnp.where(first, DIL, 0))]
    else:
        picks = [(0, 0), (tiles - 1, DIL)]
    per = 128 // DIL
    for (tile, extra), out in zip(picks, sides):

        def add(slot, row, acc):
            moved = pltpu.roll(row.astype(F32), lax.rem(slot * DIL + extra, 128), 1)
            return jnp.where(lane == slot, moved, acc)

        for part in range(out.shape[0]):
            acc = jnp.zeros((channels, 128), F32)
            start = part * per - DIL
            if part == 0:
                for ii in range(DIL):
                    acc = add(ii, above[tile, ii], acc)
                start = 0
            stop = min((part + 1) * per - DIL, rows)

            def body(i, acc):
                return add(i + DIL - part * per, field[tile, i], acc)

            acc = lax.fori_loop(start, stop, body, acc, unroll=4)
            if part == out.shape[0] - 1:
                for ii in range(DIL):
                    acc = add(rows + DIL + ii - part * per, below[tile, ii], acc)
            out[part] = acc.astype(BF16)


def border_kernel(scal, field, above, below, *rest, ncol):
    sides, (out, lefts, rights) = rest[:-3], rest[-3:]
    tiles, rows, channels, _ = field.shape
    for p in range(lefts.shape[0]):
        if ncol == 2:
            first = scal[4] == 0
            v = sides[0][p].astype(F32)
            lefts[p] = jnp.where(first, 0.0, v)
            rights[p] = jnp.where(first, v, 0.0)
        else:
            lefts[p] = sides[0][p].astype(F32)
            rights[p] = sides[1][p].astype(F32)
    lane = lax.broadcasted_iota(jnp.int32, (channels, 128), 1)
    per = 128 // DIL

    def place(i, row):
        part, at = i // per, lax.rem(i, per) * DIL
        left = pltpu.roll(lefts[part], lax.rem(128 - at, 128), 1)
        right = pltpu.roll(rights[part], lax.rem(256 - DIL - at, 128), 1)
        row = [v.astype(F32) for v in row]
        whole = pairs_of(row)
        before = pltpu.roll(whole, DIL, 1)
        after = pltpu.roll(whole, whole.shape[1] - DIL, 1)
        for u in range(tiles):
            b = before[:, 128 * u : 128 * (u + 1)]
            a = after[:, 128 * u : 128 * (u + 1)]
            if u == 0:
                b = jnp.where(lane < DIL, left, b)
            if u == tiles - 1:
                a = jnp.where(lane >= 128 - DIL, right, a)
            out[u, i] = jnp.concatenate(
                [b.astype(BF16), row[u].astype(BF16), a.astype(BF16)], axis=0
            )

    for i in range(DIL):
        place(i, [above[u, i] for u in range(tiles)])
        place(i + rows + DIL, [below[u, i] for u in range(tiles)])

    def body(i, _):
        place(i + DIL, [field[u, i] for u in range(tiles)])
        return 0

    lax.fori_loop(0, rows, body, 0, unroll=4)


def forward_kernel(scal, xs, w, bias, hw, hid, slope, direct, one, two, *, stage):
    rows, channels, _ = hid.shape
    nb = hw.shape[0]
    rq = scal[0]
    u = (rq >> 1) ^ stage

    def window(i):
        return jnp.concatenate([xs[u, i + DIL * a] for a in range(3)], axis=0)

    def conv(g, _):
        for p in range(4):
            i = g * 8 + 2 * p
            pre = jnp.dot(
                w[...], pairs_of([window(i), window(i + 1)]), preferred_element_type=F32
            )
            pre = pre + bias[...]
            grown = jnp.exp(jnp.minimum(pre, 0.0))
            h = jnp.where(pre > 0, pre, grown - 1.0).astype(BF16)
            s = jnp.where(pre > 0, 1.0, grown).astype(BF16)
            for e in range(2):
                hid[i + e] = h[:, 128 * e : 128 * (e + 1)]
                slope[i + e] = s[:, 128 * e : 128 * (e + 1)]
        return 0

    lax.fori_loop(0, rows // 8, conv, 0)

    def head(g, _):
        for p in range(4):
            i = g * 8 + 2 * p
            d = jnp.dot(hw[...], pairs_of([hid[i], hid[i + 1]]), preferred_element_type=F32)
            for e in range(2):
                direct[pl.ds(i + e, nb, stride=rows), :] = d[:, 128 * e : 128 * (e + 1)]
        return 0

    lax.fori_loop(0, rows // 8, head, 0)

    flip = (rq & 1) == 1
    for m in range(one.shape[0]):
        turned = direct[2 * rows * m : 2 * rows * (m + 1), :].T.astype(BF16)
        low, high = turned[:rows].astype(F32), turned[rows:].astype(F32)
        one[m] = jnp.where(flip, high, low).astype(BF16)
        two[m] = jnp.where(flip, low, high).astype(BF16)


def middle_kernel(scal, hb, direct, labels, hid, slope, hwt, one, two, *rest, stage, last, nbins):
    if stage:
        before, rest = rest[1], rest[2:]
    dpre, small, *ends, dl, hacc, bacc, cacc, lacc = rest
    nb, rows, _ = direct.shape
    channels = hwt.shape[0]
    rq, extent = scal[0], scal[3]
    u = (rq >> 1) ^ stage
    flip = (rq & 1) == 1
    for ref in (hacc, bacc, cacc, lacc):
        ref[...] = jnp.zeros_like(ref)
    dl[nbins * rows :, :] = jnp.zeros((dl.shape[0] - nbins * rows, 128), F32)

    lane = lax.broadcasted_iota(jnp.int32, (8, 128), 1)
    low = lane < 64
    col_ids = scal[2] + 128 * u + lane
    area = (extent * extent).astype(F32)

    def softmax(g, _):
        base = pl.multiple_of(g * 8, 8)
        row_ids = scal[1] + base + lax.broadcasted_iota(jnp.int32, (8, 128), 0)
        valid = jnp.where((row_ids < extent) & (col_ids < extent), 1.0, 0.0)
        wanted = labels[u, pl.ds(base, 8), :]
        logits = []
        for m in range((nbins + 1) // 2):
            a = one[m, pl.ds(base, 8), :].astype(F32)
            b = two[m, pl.ds(base, 8), :].astype(F32)
            a, b = jnp.where(flip, b, a), jnp.where(flip, a, b)
            mirror = (
                jnp.where(low, a, pltpu.roll(b, 64, 1)),
                jnp.where(low, pltpu.roll(a, 64, 1), b),
            )
            for k in range(2 * m, min(2 * m + 2, nbins)):
                logits.append(
                    0.5 * (direct[k, pl.ds(base, 8), :] + mirror[k - 2 * m]) + hb[k]
                )
        peak = functools.reduce(jnp.maximum, logits)
        picked = functools.reduce(
            lambda a, b: a + b,
            [jnp.where(wanted == k, logits[k], 0.0) for k in range(nbins)],
        )
        powers = [jnp.exp(v - peak) for v in logits]
        total = functools.reduce(lambda a, b: a + b, powers)
        lacc[...] += valid * (peak + jnp.log(total) - picked)
        inverse = 1.0 / total
        scale = valid / area
        for k in range(nbins):
            d = (powers[k] * inverse - jnp.where(wanted == k, 1.0, 0.0)) * scale
            d = d.astype(BF16).astype(F32)
            dl[pl.ds(k * rows + base, 8), :] = d
            bacc[8 * k : 8 * k + 8, :] += d
        return 0

    lax.fori_loop(0, rows // 8, softmax, 0)

    def back(g, _):
        for p in range(4):
            i = g * 8 + 2 * p
            d = pairs_of(
                [dl[pl.ds(i + e, nb, stride=rows), :].astype(BF16) for e in range(2)]
            )
            h = pairs_of([hid[i], hid[i + 1]])
            s = pairs_of([slope[i], slope[i + 1]])
            v = jnp.dot(hwt[...], d, preferred_element_type=F32) * s.astype(F32)
            v = v.astype(BF16)
            dpre[u, i] = v[:, :128]
            dpre[u, i + 1] = v[:, 128:]
            cacc[...] += v[:, :128].astype(F32) + v[:, 128:].astype(F32)
            hacc[0:nb, 0:channels] += lax.dot_general(
                d, h, (((1,), (1,)), ((), ())), preferred_element_type=F32
            )
        return 0

    lax.fori_loop(0, rows // 8, back, 0)

    spot = lax.broadcasted_iota(jnp.int32, small.shape, 1)
    sums = jnp.sum(bacc[...].reshape(nb, 8, 128), axis=1)
    sums = jnp.sum(sums, axis=1, keepdims=True)
    sums = jnp.concatenate([sums, jnp.zeros((channels - nb, 1), F32)], axis=0)
    biases = jnp.sum(cacc[...], axis=1, keepdims=True)
    loss = jnp.sum(jnp.sum(lacc[...], axis=1, keepdims=True), axis=0, keepdims=True)
    value = jnp.where(
        spot < channels,
        hacc[...],
        jnp.where(spot == channels, sums, jnp.where(spot == channels + 1, biases, loss)),
    )
    small[...] = value + before[...] if stage else value
    if last:
        for v in range(dpre.shape[0]):
            ends[0][v] = dpre[v, :DIL]
            ends[1][v] = dpre[v, rows - DIL :]


def weight_kernel(xs, dpre, small, out, acc, padded):
    tiles, rows, channels, _ = dpre.shape
    wide = 3 * channels
    acc[...] = jnp.zeros_like(acc)
    for u in range(tiles):
        padded[u, 0:8] = jnp.zeros((8, channels, 128), BF16)
        padded[u, 8 : 8 + rows] = dpre[u]
        padded[u, 8 + rows : 16 + rows] = jnp.zeros((8, channels, 128), BF16)

    def body(g, _):
        left, right = [], []
        for ii in range(8):
            i = g * 8 + ii
            for u in range(tiles):
                left.append(
                    jnp.concatenate([padded[u, i + 8 - DIL * a] for a in range(3)], axis=0)
                )
                right.append(xs[u, i])
        acc[...] += lax.dot_general(
            pairs_of(left), pairs_of(right), (((1,), (1,)), ((), ())),
            preferred_element_type=F32,
        )
        return 0

    lax.fori_loop(0, rows // 8 + 1, body, 0)
    half = wide // 2
    out[0:wide, :] = acc[:, 0:128]
    out[wide : wide + half, 0:64] = acc[0:half, 128:192]
    out[wide : wide + half, 64:128] = acc[half:wide, 128:192]
    out[wide + half :, :] = small[...]


def backward_kernel(ds, w, out, turned):
    step = pl.program_id(0)
    channels, _, width = out.shape
    tiles = width // 128
    for ii in range(8):
        i = step * 8 + ii
        window = pairs_of(
            [
                jnp.concatenate([ds[u, i + DIL * a] for a in range(3)], axis=0)
                for u in range(tiles)
            ]
        )
        v = jnp.dot(w[...], window, preferred_element_type=F32)
        for u in range(tiles):
            turned[pl.ds(u * channels * 8 + ii, channels, stride=8), :] = v[
                :, 128 * u : 128 * (u + 1)
            ]
    for u in range(tiles):
        at = 8 * channels * u
        block = turned[at : at + 8 * channels, :].reshape(channels, 8, 128)
        out[:, :, 128 * u : 128 * (u + 1)] = block.astype(BF16)


def side_columns(field, above, below, scal):
    parts = -(-(field.shape[1] + 2 * DIL) * DIL // 128)
    ncol = lax.axis_size("col")
    return call(
        functools.partial(edges_kernel, ncol=ncol),
        "edges",
        [shape((parts, field.shape[2], 128))] * (1 if ncol == 2 else 2),
        (scal, field, above, below),
        us=1.5,
        smem=1,
    )


def with_border(field, above, below, sides, scal):
    tiles, rows, channels, _ = field.shape
    ncol = lax.axis_size("col")
    if ncol == 2:
        got = [lax.ppermute(sides[0], "col", [(0, 1), (1, 0)])]
    else:
        to_left, to_right = sides
        got = [
            lax.ppermute(to_right, "col", [(i, i + 1) for i in range(ncol - 1)]),
            lax.ppermute(to_left, "col", [(i + 1, i) for i in range(ncol - 1)]),
        ]
    return call(
        functools.partial(border_kernel, ncol=ncol),
        "border",
        shape((tiles, rows + 2 * DIL, 3 * channels, 128)),
        (scal, field, above, below, *got),
        us=4,
        smem=1,
        scratch=[pltpu.VMEM(got[0].shape, F32)] * 2,
    )


def row_halo(head, tail):
    count = lax.axis_size("row")
    above = lax.ppermute(tail, "row", [(i, i + 1) for i in range(count - 1)])
    below = lax.ppermute(head, "row", [(i + 1, i) for i in range(count - 1)])
    return above, below


def total_over_tiles(value):
    nrow, ncol = lax.axis_size("row"), lax.axis_size("col")
    if ncol == 2 and nrow % 2 == 0 and nrow <= 8 and value.shape[0] % 32 == 0:
        r, c = lax.axis_index("row"), lax.axis_index("col")
        me = (r % 2) * 2 + c
        parts = value.reshape(4, value.shape[0] // 4, value.shape[1])

        def near(v, d):
            perm = [
                (i * 2 + j, (i ^ (d >> 1)) * 2 + (j ^ (d & 1)))
                for i in range(nrow)
                for j in range(2)
            ]
            return lax.ppermute(v, ROWS, perm)

        own = lax.dynamic_index_in_dim(parts, me, 0, False)
        for d in (1, 2, 3):
            own = own + near(lax.dynamic_index_in_dim(parts, me ^ d, 0, False), d)
        summed = own
        for d in range(1, nrow // 2):
            perm = [(i, (i + 2 * d) % nrow) for i in range(nrow)]
            summed = summed + lax.ppermute(own, "row", perm)
        got = [summed] + [near(summed, d) for d in (1, 2, 3)]
        return got, jnp.stack([me, me ^ 1, me ^ 2, me ^ 3]).astype(jnp.int32)
    for axis, count in (("col", ncol), ("row", nrow)):
        if count & (count - 1):
            value = lax.psum(value, axis)
            continue
        bit = 1
        while bit < count:
            value = value + lax.ppermute(value, axis, [(i, i ^ bit) for i in range(count)])
            bit *= 2
    return [value], jnp.zeros((1,), jnp.int32)


def unpack_kernel(where, extent, *rest):
    parts, (taps, biases, heads, head_biases, loss, buf) = rest[:-6], rest[-6:]
    for n, part in enumerate(parts):
        size = part.shape[0]
        buf[pl.ds(pl.multiple_of(where[n] * size, 8), size), :] = part[...]
    ch = taps.shape[2]
    half = 3 * ch // 2
    for a in range(3):
        taps[a, 0] = buf[a * ch : (a + 1) * ch, 0:ch]
        taps[a, 1] = buf[a * ch : (a + 1) * ch, ch : 2 * ch]
        for o in range(0, ch, 32):
            at = a * ch + o
            lanes = slice(0, ch) if at < half else slice(ch, 2 * ch)
            row = 3 * ch + at % half
            taps[a, 2, o : o + 32] = buf[row : row + 32, lanes]
    small = buf[3 * ch + half :, :]
    turned = small.T
    heads[...] = small[: heads.shape[0], :ch]
    head_biases[...] = turned[ch : ch + 1, : heads.shape[0]]
    biases[...] = turned[ch + 1 : ch + 2, :]
    area = (extent[0] * extent[0]).astype(F32)
    loss[...] = turned[ch + 2 : ch + 3, 0:1] / area


def per_device(x, labels, lengths, conv_weight, conv_bias, head_weight, head_bias):
    channels, rows, width = x.shape
    nbins = head_weight.shape[0]
    nrow, ncol = lax.axis_size("row"), lax.axis_size("col")
    q = width // rows
    tiles = width // 128
    assert rows == 64 and channels == 64 and q == 2 * tiles and q & (q - 1) == 0
    assert q * ncol == nrow and 128 * tiles == width
    nb = -(-nbins // 8) * 8
    pairs = (nbins + 1) // 2
    wide = 3 * channels
    r, c = lax.axis_index("row"), lax.axis_index("col")

    scal = jnp.stack([r % q, r * rows, c * width, lengths[0], c]).astype(jnp.int32)
    w_fwd = conv_weight.transpose(2, 0, 1, 3).reshape(channels, 9 * channels)
    w_bwd = conv_weight[::-1, ::-1].transpose(3, 0, 1, 2).reshape(channels, 9 * channels)
    hw = jnp.pad(head_weight, ((0, nb - nbins), (0, 0)))

    field = (tiles, rows, channels, 128)
    strip = (tiles, DIL, channels, 128)
    xt, head, tail = pl.pallas_call(
        prep_kernel,
        grid=(channels // 8,),
        in_specs=[pl.BlockSpec((8, rows, width), lambda g: (g, 0, 0))],
        out_specs=[VM, VM, VM],
        out_shape=[shape(field), shape(strip), shape(strip)],
        scratch_shapes=[pltpu.VMEM((tiles * channels * rows, 128), F32)],
        compiler_params=grant(8),
        cost_estimate=cost(4),
        name="prep",
    )(x)
    above, below = row_halo(head, tail)
    xs = with_border(xt, above, below, side_columns(xt, above, below, scal), scal)

    band = labels.shape[0]
    mine = labels.astype(BF16).reshape(band, ncol, width)
    strips = jnp.zeros((ncol, band, width), BF16)
    for d in range(ncol):
        piece = lax.dynamic_index_in_dim(mine, (c + d) % ncol, axis=1, keepdims=False)
        if d:
            piece = lax.ppermute(piece, "col", [(i, (i + d) % ncol) for i in range(ncol)])
        strips = lax.dynamic_update_index_in_dim(strips, piece, (c - d) % ncol, axis=0)
    tile_labels = strips.reshape(rows, tiles, 128).transpose(1, 0, 2).astype(jnp.int32)

    kept, got = [], []
    for stage in range(tiles):
        block = shape((pairs, rows, 128))
        hid, slope, direct, *sends = call(
            functools.partial(forward_kernel, stage=stage),
            "forward",
            [shape(field[1:]), shape(field[1:]), shape((nb * rows, 128), F32), block, block],
            (scal, xs, w_fwd, conv_bias[:, None], hw),
            us=6,
            smem=1,
        )
        kept.append((hid, slope, direct))
        for e in range(2):
            t = 2 * stage + e
            perm = [
                (i * ncol + j, (q * j + (i % q ^ t)) * ncol + i // q)
                for i in range(nrow)
                for j in range(ncol)
            ]
            got.append(lax.ppermute(sends[e], ROWS, perm))

    dpre = small = ends = None
    for stage in range(tiles):
        hid, slope, direct = kept[stage]
        args = (
            scal,
            head_bias,
            direct.reshape(nb, rows, 128),
            tile_labels,
            hid,
            slope,
            hw.T,
            got[2 * stage],
            got[2 * stage + 1],
        )
        last = stage == tiles - 1
        dpre, small, *ends = call(
            functools.partial(middle_kernel, stage=stage, last=last, nbins=nbins),
            "middle",
            [shape(field), shape((channels, 128), F32)] + [shape(strip)] * (2 * last),
            args + ((dpre, small) if stage else ()),
            us=5,
            smem=2,
            scratch=[
                pltpu.VMEM((nb * rows, 128), F32),
                pltpu.VMEM((channels, 128), F32),
                pltpu.VMEM((nb * 8, 128), F32),
                pltpu.VMEM((channels, 128), F32),
                pltpu.VMEM((8, 128), F32),
            ],
            aliases={len(args): 0} if stage else None,
        )

    sums = call(
        weight_kernel,
        "weights",
        shape((wide + wide // 2 + channels, 128), F32),
        (xs, dpre, small),
        us=4,
        mib=8,
        scratch=[
            pltpu.VMEM((wide, wide), F32),
            pltpu.VMEM((tiles, rows + 16, channels, 128), BF16),
        ],
    )
    above, below = row_halo(*ends)
    sides = side_columns(dpre, above, below, scal)
    sides, sums = lax.optimization_barrier((sides, sums))
    ds = with_border(dpre, above, below, sides, scal)
    parts, where = total_over_tiles(sums)

    pair_gradient = pl.pallas_call(
        backward_kernel,
        grid=(rows // 8,),
        in_specs=[VM, VM],
        out_specs=pl.BlockSpec((channels, 8, width), lambda g: (0, g, 0)),
        out_shape=shape((channels, rows, width)),
        scratch_shapes=[pltpu.VMEM((tiles * channels * 8, 128), F32)],
        compiler_params=grant(8),
        cost_estimate=cost(6),
        name="backward",
    )(ds, w_bwd)

    conv_grad, biases, heads, head_biases, loss = pl.pallas_call(
        unpack_kernel,
        in_specs=[SM, SM] + [VM] * len(parts),
        out_shape=[
            shape((3, 3, channels, channels), F32),
            shape((1, channels), F32),
            shape((nbins, channels), F32),
            shape((1, nbins), F32),
            shape((1, 1), F32),
        ],
        scratch_shapes=[pltpu.VMEM(sums.shape, F32)],
        compiler_params=grant(4),
        cost_estimate=cost(1),
        name="unpack",
    )(where, lengths, *parts)
    return (
        pair_gradient,
        conv_grad,
        biases.reshape(channels),
        heads,
        head_biases.reshape(nbins),
        loss.reshape(1),
    )


def solution(mesh):
    return jax.shard_map(
        per_device,
        mesh=mesh,
        in_specs=(
            P(None, ("parts", "row"), "col"),
            P(("parts", "row", "col"), None),
            P("parts"),
            P(),
            P(),
            P(),
            P(),
        ),
        out_specs=(
            P(None, ("parts", "row"), "col"),
            P("parts", None, None, None),
            P("parts"),
            P("parts", None),
            P("parts"),
            P("parts"),
        ),
        check_vma=False,
    )
```

time: 418 us -> 129 us (0.31); the launches traced: 411 us -> 129 us
  matrix products: 113 us -> 0 us
  blocking collectives: 92.3 us -> 0 us
  local copies, waits for them, and re-layouts: 72.9 us -> 2.62 us
  Pallas kernels: 0 us -> 46.7 us
  waiting for transfers between devices: 68.1 us -> 39.6 us
  between operations: 17.4 us -> 1.67 us
  other arithmetic: 12.7 us -> 0.13 us
    dot_general x31 -> x0, matrix products: 113 us -> none  [the longest x9 44.2 us: per_device(): jnp.einsum('oc,cij->oij', conv_weight[offset_row, offset_column], sliding...]
    psum x1 -> x0, blocking collectives: 62.7 us -> none  [per_device(): lax.psum((conv_grad, conv_bias_grad, head_grad, head_bias_grad, loss_loca...]
    pallas_call x0 -> x12, Pallas kernels: none -> 46.7 us  [the longest x9 35.7 us: call(): pl.pallas_call(body, out_shape=out_shape, in_specs=[SM] * smem + [VM] * (...]
    all_to_all x2 -> x0, waiting for transfers between devices: 44.8 us -> none  [the longest x1 34 us: mirror_features(): lax.all_to_all(blocks, ('row', 'col'), split_axis=2, concat_axis=2, tiled...]
    ppermute x8 -> x20, waiting for transfers between devices: 0.02 us -> 39.6 us  [the longest x4 35.2 us: per_device(): got.append(lax.ppermute(sends[e], ROWS, perm))]
    all_to_all x1 -> x0, blocking collectives: 29.7 us -> none  [tile_to_band(): lax.all_to_all(split, 'col', split_axis=1, concat_axis=3, tiled=True)]
    unnamed x71 -> x15, local copies, waits for them, and re-layouts: 27.2 us -> 1.81 us
    psum x1 -> x0, waiting for transfers between devices: 23.2 us -> none  [per_device(): lax.psum((conv_grad, conv_bias_grad, head_grad, head_bias_grad, loss_loca...]
  transfers between devices with their start and end apart: 11 -> 20, of which waited for: 3 -> 5; matrix products, arithmetic and copies ran while one was open for 23% -> 1% of each run, Pallas kernels for 0% -> 20%
where the time goes in v2:
time: 129 us
  Pallas kernels  46.7 us (36%)
  waiting for transfers between devices  39.6 us (31%)
  starting transfers between devices  38.3 us (30%)
  local copies, waits for them, and re-layouts  2.62 us (2%)
  between operations  1.67 us (1%)
    pallas_call x9, Pallas kernels, call(): pl.pallas_call(body, out_shape=out_shape, in_specs=[SM] * smem + [VM] * (...  35.7 us
    ppermute x4, waiting for transfers between devices, per_device(): got.append(lax.ppermute(sends[e], ROWS, perm))  35.2 us
    ppermute x6, starting transfers between devices, near(): return lax.ppermute(v, ROWS, perm)  16.3 us
    pallas_call x1, Pallas kernels, per_device(): pl.pallas_call(backward_kernel, grid=(rows // 8,), in_specs=[VM, VM], out...  5.76 us
    ppermute x4, starting transfers between devices, per_device(): got.append(lax.ppermute(sends[e], ROWS, perm))  5.47 us
    ppermute x2, starting transfers between devices, row_halo(): above = lax.ppermute(tail, 'row', [(i, i + 1) for i in range(count - 1)])  4.39 us
    ppermute x3, starting transfers between devices, total_over_tiles(): summed = summed + lax.ppermute(own, 'row', perm)  3.88 us
    pallas_call x1, Pallas kernels, per_device(): pl.pallas_call(prep_kernel, grid=(channels // 8,), in_specs=[pl.BlockSpec...  3.8 us
  transfers between devices with their start and end apart: 20, of which 5 were waited for; matrix products, arithmetic and copies ran while one was open for 1% of the time, Pallas kernels for 20%

profile of v2, /device:TPU:0, one launch (start us, length us, event | category | flops | bytes accessed | tf_op | source)
XLA Modules:
  0.0 129.0 jit_solution(11855745764373227100)
XLA Ops:
  2.2 3.8 %prep.1 = (bf16[2,64,64,128]{3,2,1,0:T(8,128)(2,1)S(1)}, bf16[2,4,64,128]{3,2,1,0:T(8,128)(2,1)S(1)}, bf16[2,4,64,128]{3,2,1,0:T(8,128)(2,1)S(1)}) custom-call(bf16[64,64,256]{2,1,0:T(8,128)(2,1)S(1)} %copy-done), custom_call_target="tpu_custom_call" | custom-call | flops 4400000000 | tf_op jit(solution)/shard_map/prep/pallas_call | solution.py:466
  6.0 2.4 %collective-permute-start = (bf16[2,4,64,128]{3,2,1,0:T(8,128)(2,1)S(1)}, bf16[2,4,64,128]{3,2,1,0:T(8,128)(2,1)S(1)}, u32[]{:S(2)}, u32[]{:S(2)}) collective-permute-start(bf16[2,4,64,128]{3,2,1,0:T(8,128)(2,1)S(1)} %get-tuple-element.33), channel_id=1, source_target_pairs={{0,2},{2,4},{4,6},{6,8},{8,10},{10,12},{12,14},{1,3},{3,5},{5,7},{... | collective-permute-start | bytes 393224 | tf_op jit(solution)/shard_map/ppermute | solution.py:382
  9.9 2.4 %collective-permute-start.3 = (bf16[32,256]{1,0:T(8,128)(2,1)S(1)}, bf16[32,256]{1,0:T(8,128)(2,1)S(1)}, u32[]{:S(2)}, u32[]{:S(2)}) collective-permute-start(bf16[32,256]{1,0:T(8,128)(2,1)S(1)} %bitcast.53), channel_id=1, source_target_pairs={{0,1},{1,0},{2,3},{3,2},{4,5},{5,4},{6,7},{7,6},{8,9},{9,8},{10,11... | collective-permute-start | bytes 49160 | tf_op jit(solution)/shard_map/ppermute | solution.py:486
  13.8 2.1 %edges.2 = bf16[3,64,128]{2,1,0:T(8,128)(2,1)S(1)} custom-call(s32[5]{0:T(128)S(1)} %stack.34.scal, bf16[2,64,64,128]{3,2,1,0:T(8,128)(2,1)S(1)} %get-tuple-element.32.field, bf16[2,4,64,128]{3,2,1,0:T(8,128)(2,1)S(1)} %collective-permute-done.above, bf16[2,4,64,128]{3,2,1,0:T(8,128)(2,1)S(1)} %collective-permute-done.1.below), custom_call_target="tpu_custom_call" | custom-call | flops 1650000000 | tf_op jit(solution)/shard_map/edges/pallas_call | solution.py:28
  17.6 2.5 %collective-permute-done.2.rest_0_ = bf16[3,64,128]{2,1,0:T(8,128)(2,1)S(1)} collective-permute-done((bf16[3,64,128]{2,1,0:T(8,128)(2,1)S(1)}, bf16[3,64,128]{2,1,0:T(8,128)(2,1)S(1)}, u32[]{:S(2)}, u32[]{:S(2)}) %collective-permute-start.2) | collective-permute-done | bytes 49184 | tf_op jit(solution)/shard_map/ppermute | solution.py:362
  20.1 3.7 %border.2.xs = bf16[2,72,192,128]{3,2,1,0:T(8,128)(2,1)S(1)} custom-call(s32[5]{0:T(128)S(1)} %stack.34.scal, bf16[2,64,64,128]{3,2,1,0:T(8,128)(2,1)S(1)} %get-tuple-element.32.field, bf16[2,4,64,128]{3,2,1,0:T(8,128)(2,1)S(1)} %collective-permute-done.above, bf16[2,4,64,128]{3,2,1,0:T(8,128)(2,1)S(1)} %collective-permute-done.1.below, ...), custom_call_target="tpu_custom_call" | custom-call | flops 4400000000 | tf_op jit(solution)/shard_map/border/pallas_call | solution.py:28
  23.8 5.6 %forward.3 = (bf16[64,64,128]{2,1,0:T(8,128)(2,1)S(1)}, bf16[64,64,128]{2,1,0:T(8,128)(2,1)S(1)}, f32[2560,128]{1,0:T(8,128)S(1)}, bf16[19,64,128]{2,1,0:T(8,128)(2,1)S(1)}, bf16[19,64,128]{2,1,0:T(8,128)(2,1)S(1)}) custom-call(s32[5]{0:T(128)S(1)} %stack.34.scal, bf16[2,72,192,128]{3,2,1,0:T(8,128)(2,1)S(1)} %border.2.xs, bf16[64,576]{1,0:T(8,128)(2,1)S(1)} %copy.33.w, ...), custom_call_target="tpu_custom_call" | custom-call | flops 6600000000 | tf_op jit(solution)/shard_map/forward/pallas_call | solution.py:28
  30.1 2.5 %collective-permute-start.7 = (bf16[19,64,128]{2,1,0:T(8,128)(2,1)S(1)}, bf16[19,64,128]{2,1,0:T(8,128)(2,1)S(1)}, u32[]{:S(2)}, u32[]{:S(2)}) collective-permute-start(bf16[19,64,128]{2,1,0:T(8,128)(2,1)S(1)} %get-tuple-element.44), channel_id=1, source_target_pairs={{0,2},{1,10},{2,0},{3,8},{4,6},{5,14},{6,4},{7,12},{8,3},{9,11},{1... | collective-permute-start | bytes 933896 | tf_op jit(solution)/shard_map/ppermute | solution.py:509
  32.6 5.6 %forward.2 = (bf16[64,64,128]{2,1,0:T(8,128)(2,1)S(1)}, bf16[64,64,128]{2,1,0:T(8,128)(2,1)S(1)}, f32[2560,128]{1,0:T(8,128)S(1)}, bf16[19,64,128]{2,1,0:T(8,128)(2,1)S(1)}, bf16[19,64,128]{2,1,0:T(8,128)(2,1)S(1)}) custom-call(s32[5]{0:T(128)S(1)} %stack.34.scal, bf16[2,72,192,128]{3,2,1,0:T(8,128)(2,1)S(1)} %border.2.xs, bf16[64,576]{1,0:T(8,128)(2,1)S(1)} %copy.33.w, ...), custom_call_target="tpu_custom_call" | custom-call | flops 6600000000 | tf_op jit(solution)/shard_map/forward/pallas_call | solution.py:28
  38.2 2.3 %collective-permute-start.4 = (bf16[19,64,128]{2,1,0:T(8,128)(2,1)S(1)}, bf16[19,64,128]{2,1,0:T(8,128)(2,1)S(1)}, u32[]{:S(2)}, u32[]{:S(2)}) collective-permute-start(bf16[19,64,128]{2,1,0:T(8,128)(2,1)S(1)} %get-tuple-element.38), channel_id=1, source_target_pairs={{0,4},{1,12},{2,6},{3,14},{4,0},{5,8},{6,2},{7,10},{8,5},{9,13},{1... | collective-permute-start | bytes 933896 | tf_op jit(solution)/shard_map/ppermute | solution.py:509
  40.6 4.6 %middle.2 = (bf16[2,64,64,128]{3,2,1,0:T(8,128)(2,1)S(1)}, f32[64,128]{1,0:T(8,128)S(1)}) custom-call(s32[5]{0:T(128)S(1)} %stack.34.scal, f32[37]{0:T(128)S(1)} %copy-done.1, f32[40,64,128]{2,1,0:T(8,128)S(1)} %bitcast.49, s32[2,64,128]{2,1,0:T(8,128)S(1)} %bitcast.46, bf16[64,64,128]{2,1,0:T(8,128)(2,1)S(1)} %get-tuple-element.41.hid, ...), custom_call_target="tpu_custom_call" | custom-call | flops 5500000256 | tf_op jit(solution)/shard_map/middle/pallas_call | solution.py:28
  45.1 3.6 %collective-permute-done.4.one = bf16[19,64,128]{2,1,0:T(8,128)(2,1)S(1)} collective-permute-done((bf16[19,64,128]{2,1,0:T(8,128)(2,1)S(1)}, bf16[19,64,128]{2,1,0:T(8,128)(2,1)S(1)}, u32[]{:S(2)}, u32[]{:S(2)}) %collective-permute-start.4) | collective-permute-done | bytes 311328 | tf_op jit(solution)/shard_map/ppermute | solution.py:509
  48.7 31.6 %collective-permute-done.5.two = bf16[19,64,128]{2,1,0:T(8,128)(2,1)S(1)} collective-permute-done((bf16[19,64,128]{2,1,0:T(8,128)(2,1)S(1)}, bf16[19,64,128]{2,1,0:T(8,128)(2,1)S(1)}, u32[]{:S(2)}, u32[]{:S(2)}) %collective-permute-start.5) | collective-permute-done | bytes 311328 | tf_op jit(solution)/shard_map/ppermute | solution.py:509
  80.3 4.6 %middle.3 = (bf16[2,64,64,128]{3,2,1,0:T(8,128)(2,1)S(1)}, f32[64,128]{1,0:T(8,128)S(1)}, bf16[2,4,64,128]{3,2,1,0:T(8,128)(2,1)S(1)}, bf16[2,4,64,128]{3,2,1,0:T(8,128)(2,1)S(1)}) custom-call(s32[5]{0:T(128)S(1)} %stack.34.scal, f32[37]{0:T(128)S(1)} %copy-done.1, f32[40,64,128]{2,1,0:T(8,128)S(1)} %bitcast.48, ...), custom_call_target="tpu_custom_call", output_to_operand_aliasing={{0}: (9, {})} | custom-call | flops 5500000256 | tf_op jit(solution)/shard_map/middle/pallas_call | solution.py:28
  84.9 2.0 %collective-permute-start.8 = (bf16[2,4,64,128]{3,2,1,0:T(8,128)(2,1)S(1)}, bf16[2,4,64,128]{3,2,1,0:T(8,128)(2,1)S(1)}, u32[]{:S(2)}, u32[]{:S(2)}) collective-permute-start(bf16[2,4,64,128]{3,2,1,0:T(8,128)(2,1)S(1)} %get-tuple-element.48), channel_id=1, source_target_pairs={{0,2},{2,4},{4,6},{6,8},{8,10},{10,12},{12,14},{1,3},{3,5},{5,7},{... | collective-permute-start | bytes 393224 | tf_op jit(solution)/shard_map/ppermute | solution.py:382
  88.2 3.8 %weights.1 = f32[352,128]{1,0:T(8,128)S(1)} custom-call(bf16[2,72,192,128]{3,2,1,0:T(8,128)(2,1)S(1)} %border.2.xs, bf16[2,64,64,128]{3,2,1,0:T(8,128)(2,1)S(1)} %get-tuple-element.47.field.dpre, f32[64,128]{1,0:T(8,128)S(1)} %get-tuple-element.50.small), custom_call_target="tpu_custom_call" | custom-call | flops 4400000000 | tf_op jit(solution)/shard_map/weights/pallas_call | solution.py:28
  92.0 2.1 %edges.3 = bf16[3,64,128]{2,1,0:T(8,128)(2,1)S(1)} custom-call(s32[5]{0:T(128)S(1)} %stack.34.scal, bf16[2,64,64,128]{3,2,1,0:T(8,128)(2,1)S(1)} %get-tuple-element.47.field.dpre, bf16[2,4,64,128]{3,2,1,0:T(8,128)(2,1)S(1)} %collective-permute-done.8.above, bf16[2,4,64,128]{3,2,1,0:T(8,128)(2,1)S(1)} %collective-permute-done.9.below), custom_call_target="tpu_custom_call" | custom-call | flops 1650000000 | tf_op jit(solution)/shard_map/edges/pallas_call | solution.py:28
  94.1 10.8 %collective-permute-start.11 = (f32[88,128]{1,0:T(8,128)S(1)}, f32[88,128]{1,0:T(8,128)S(1)}, u32[]{:S(2)}, u32[]{:S(2)}) collective-permute-start(f32[88,128]{1,0:T(8,128)S(1)} %get-tuple-element.58), channel_id=1, source_target_pairs={{0,1},{1,0},{2,3},{3,2},{4,5},{5,4},{6,7},{7,6},{8,9},{9,8},{10,11... | collective-permute-start | bytes 135176 | tf_op jit(solution)/shard_map/ppermute | solution.py:400
  104.9 3.3 %collective-permute-start.12 = (f32[88,128]{1,0:T(8,128)S(1)}, f32[88,128]{1,0:T(8,128)S(1)}, u32[]{:S(2)}, u32[]{:S(2)}) collective-permute-start(f32[88,128]{1,0:T(8,128)S(1)} %get-tuple-element.60), channel_id=1, source_target_pairs={{0,2},{1,3},{2,0},{3,1},{4,6},{5,7},{6,4},{7,5},{8,10},{9,11},{10,... | collective-permute-start | bytes 135176 | tf_op jit(solution)/shard_map/ppermute | solution.py:400
  108.4 1.7 %collective-permute-start.10 = (bf16[3,64,128]{2,1,0:T(8,128)(2,1)S(1)}, bf16[3,64,128]{2,1,0:T(8,128)(2,1)S(1)}, u32[]{:S(2)}, u32[]{:S(2)}) collective-permute-start(bf16[3,64,128]{2,1,0:T(8,128)(2,1)S(1)} %edges.3), channel_id=1, source_target_pairs={{0,1},{1,0},{2,3},{3,2},{4,5},{5,4},{6,7},{7,6},{8,9},{9,8},{10,11... | collective-permute-start | bytes 147464 | tf_op jit(solution)/shard_map/ppermute | solution.py:362
  110.1 1.8 %collective-permute-done.13 = f32[88,128]{1,0:T(8,128)S(1)} collective-permute-done((f32[88,128]{1,0:T(8,128)S(1)}, f32[88,128]{1,0:T(8,128)S(1)}, u32[]{:S(2)}, u32[]{:S(2)}) %collective-permute-start.13) | collective-permute-done | bytes 45088 | tf_op jit(solution)/shard_map/ppermute | solution.py:400
  113.0 2.8 %collective-permute-start.16 = (f32[88,128]{1,0:T(8,128)S(1)}, f32[88,128]{1,0:T(8,128)S(1)}, u32[]{:S(2)}, u32[]{:S(2)}) collective-permute-start(f32[88,128]{1,0:T(8,128)S(1)} %fusion.1), channel_id=1, source_target_pairs={{0,12},{2,14},{4,0},{6,2},{8,4},{10,6},{12,8},{14,10},{1,13},{3,15... | collective-permute-start | bytes 135176 | tf_op jit(solution)/shard_map/ppermute | solution.py:408
  115.8 3.7 %border.3.ds = bf16[2,72,192,128]{3,2,1,0:T(8,128)(2,1)S(1)} custom-call(s32[5]{0:T(128)S(1)} %stack.34.scal, bf16[2,64,64,128]{3,2,1,0:T(8,128)(2,1)S(1)} %get-tuple-element.47.field.dpre, bf16[2,4,64,128]{3,2,1,0:T(8,128)(2,1)S(1)} %collective-permute-done.8.above, bf16[2,4,64,128]{3,2,1,0:T(8,128)(2,1)S(1)} %collective-permute-done.9.below, ...), custom_call_target="tpu_custom_call" | custom-call | flops 4400000000 | tf_op jit(solution)/shard_map/border/pallas_call | solution.py:28
  121.8 5.8 %backward.1 = bf16[64,64,256]{2,1,0:T(8,128)(2,1)} custom-call(bf16[2,72,192,128]{3,2,1,0:T(8,128)(2,1)S(1)} %border.3.ds, bf16[64,576]{1,0:T(8,128)(2,1)S(1)} %copy.40.w), custom_call_target="tpu_custom_call" | custom-call | flops 6600000000 | tf_op jit(solution)/shard_map/backward/pallas_call | solution.py:561
  (64 shorter events, 12.5 us)
Async XLA Ops:
  2.2 10.8 %copy-start.4 = (bf16[37,64]{1,0:T(8,128)(2,1)S(1)}, bf16[37,64]{1,0:T(8,128)(2,1)}, u32[]{:S(2)}) copy-start(bf16[37,64]{1,0:T(8,128)(2,1)} %param.12) | copy-start | bytes 14212
  2.2 11.0 %copy-start.2 = (bf16[3,3,64,64]{3,2,1,0:T(8,128)(2,1)S(1)}, bf16[3,3,64,64]{3,2,1,0:T(8,128)(2,1)}, u32[]{:S(2)}) copy-start(bf16[3,3,64,64]{3,2,1,0:T(8,128)(2,1)} %param.10) | copy-start | bytes 221188
  2.2 11.3 %copy-start.5 = (f32[64]{0:T(128)S(1)}, f32[64]{0:T(128)}, u32[]{:S(2)}) copy-start(f32[64]{0:T(128)} %param.11) | copy-start | bytes 772
  6.0 7.7 %collective-permute-start = (bf16[2,4,64,128]{3,2,1,0:T(8,128)(2,1)S(1)}, bf16[2,4,64,128]{3,2,1,0:T(8,128)(2,1)S(1)}, u32[]{:S(2)}, u32[]{:S(2)}) collective-permute-start(bf16[2,4,64,128]{3,2,1,0:T(8,128)(2,1)S(1)} %get-tuple-element.33), channel_id=1, source_target_pairs={{0,2},{2,4},{4,6},{6,8},{8,10},{10,12},{12,14},{1,3},{3,5},{5,7},{... | collective-permute-start | bytes 393224 | tf_op jit(solution)/shard_map/ppermute | solution.py:382
  8.4 5.4 %collective-permute-start.1 = (bf16[2,4,64,128]{3,2,1,0:T(8,128)(2,1)S(1)}, bf16[2,4,64,128]{3,2,1,0:T(8,128)(2,1)S(1)}, u32[]{:S(2)}, u32[]{:S(2)}) collective-permute-start(bf16[2,4,64,128]{3,2,1,0:T(8,128)(2,1)S(1)} %get-tuple-element.34), channel_id=1, source_target_pairs={{2,0},{4,2},{6,4},{8,6},{10,8},{12,10},{14,12},{3,1},{5,3},{7,5},{... | collective-permute-start | bytes 393224 | tf_op jit(solution)/shard_map/ppermute | solution.py:383
  9.9 7.6 %collective-permute-start.3 = (bf16[32,256]{1,0:T(8,128)(2,1)S(1)}, bf16[32,256]{1,0:T(8,128)(2,1)S(1)}, u32[]{:S(2)}, u32[]{:S(2)}) collective-permute-start(bf16[32,256]{1,0:T(8,128)(2,1)S(1)} %bitcast.53), channel_id=1, source_target_pairs={{0,1},{1,0},{2,3},{3,2},{4,5},{5,4},{6,7},{7,6},{8,9},{9,8},{10,11... | collective-permute-start | bytes 49160 | tf_op jit(solution)/shard_map/ppermute | solution.py:486
  15.9 4.2 %collective-permute-start.2 = (bf16[3,64,128]{2,1,0:T(8,128)(2,1)S(1)}, bf16[3,64,128]{2,1,0:T(8,128)(2,1)S(1)}, u32[]{:S(2)}, u32[]{:S(2)}) collective-permute-start(bf16[3,64,128]{2,1,0:T(8,128)(2,1)S(1)} %edges.2), channel_id=1, source_target_pairs={{0,1},{1,0},{2,3},{3,2},{4,5},{5,4},{6,7},{7,6},{8,9},{9,8},{10,11... | collective-permute-start | bytes 147464 | tf_op jit(solution)/shard_map/ppermute | solution.py:362
  29.4 11.1 %collective-permute-start.6 = (bf16[19,64,128]{2,1,0:T(8,128)(2,1)S(1)}, bf16[19,64,128]{2,1,0:T(8,128)(2,1)S(1)}, u32[]{:S(2)}, u32[]{:S(2)}) collective-permute-start(bf16[19,64,128]{2,1,0:T(8,128)(2,1)S(1)} %get-tuple-element.43), channel_id=1, source_target_pairs={{0,0},{1,8},{2,2},{3,10},{4,4},{5,12},{6,6},{7,14},{8,1},{9,9},{10... | collective-permute-start | bytes 933896 | tf_op jit(solution)/shard_map/ppermute | solution.py:509
  30.1 10.4 %copy-start.1 = (f32[37]{0:T(128)S(1)}, f32[37]{0:T(128)}, u32[]{:S(2)}) copy-start(f32[37]{0:T(128)} %hb.3) | copy-start | bytes 448
  30.1 10.4 %collective-permute-start.7 = (bf16[19,64,128]{2,1,0:T(8,128)(2,1)S(1)}, bf16[19,64,128]{2,1,0:T(8,128)(2,1)S(1)}, u32[]{:S(2)}, u32[]{:S(2)}) collective-permute-start(bf16[19,64,128]{2,1,0:T(8,128)(2,1)S(1)} %get-tuple-element.44), channel_id=1, source_target_pairs={{0,2},{1,10},{2,0},{3,8},{4,6},{5,14},{6,4},{7,12},{8,3},{9,11},{1... | collective-permute-start | bytes 933896 | tf_op jit(solution)/shard_map/ppermute | solution.py:509
  38.2 10.5 %collective-permute-start.4 = (bf16[19,64,128]{2,1,0:T(8,128)(2,1)S(1)}, bf16[19,64,128]{2,1,0:T(8,128)(2,1)S(1)}, u32[]{:S(2)}, u32[]{:S(2)}) collective-permute-start(bf16[19,64,128]{2,1,0:T(8,128)(2,1)S(1)} %get-tuple-element.38), channel_id=1, source_target_pairs={{0,4},{1,12},{2,6},{3,14},{4,0},{5,8},{6,2},{7,10},{8,5},{9,13},{1... | collective-permute-start | bytes 933896 | tf_op jit(solution)/shard_map/ppermute | solution.py:509
  40.5 39.8 %collective-permute-start.5 = (bf16[19,64,128]{2,1,0:T(8,128)(2,1)S(1)}, bf16[19,64,128]{2,1,0:T(8,128)(2,1)S(1)}, u32[]{:S(2)}, u32[]{:S(2)}) collective-permute-start(bf16[19,64,128]{2,1,0:T(8,128)(2,1)S(1)} %get-tuple-element.39), channel_id=1, source_target_pairs={{0,6},{1,14},{2,4},{3,12},{4,2},{5,10},{6,0},{7,8},{8,7},{9,15},{1... | collective-permute-start | bytes 933896 | tf_op jit(solution)/shard_map/ppermute | solution.py:509
  84.9 7.1 %collective-permute-start.8 = (bf16[2,4,64,128]{3,2,1,0:T(8,128)(2,1)S(1)}, bf16[2,4,64,128]{3,2,1,0:T(8,128)(2,1)S(1)}, u32[]{:S(2)}, u32[]{:S(2)}) collective-permute-start(bf16[2,4,64,128]{3,2,1,0:T(8,128)(2,1)S(1)} %get-tuple-element.48), channel_id=1, source_target_pairs={{0,2},{2,4},{4,6},{6,8},{8,10},{10,12},{12,14},{1,3},{3,5},{5,7},{... | collective-permute-start | bytes 393224 | tf_op jit(solution)/shard_map/ppermute | solution.py:382
  86.9 5.1 %collective-permute-start.9 = (bf16[2,4,64,128]{3,2,1,0:T(8,128)(2,1)S(1)}, bf16[2,4,64,128]{3,2,1,0:T(8,128)(2,1)S(1)}, u32[]{:S(2)}, u32[]{:S(2)}) collective-permute-start(bf16[2,4,64,128]{3,2,1,0:T(8,128)(2,1)S(1)} %get-tuple-element.49), channel_id=1, source_target_pairs={{2,0},{4,2},{6,4},{8,6},{10,8},{12,10},{14,12},{3,1},{5,3},{7,5},{... | collective-permute-start | bytes 393224 | tf_op jit(solution)/shard_map/ppermute | solution.py:383
  94.1 16.0 %collective-permute-start.11 = (f32[88,128]{1,0:T(8,128)S(1)}, f32[88,128]{1,0:T(8,128)S(1)}, u32[]{:S(2)}, u32[]{:S(2)}) collective-permute-start(f32[88,128]{1,0:T(8,128)S(1)} %get-tuple-element.58), channel_id=1, source_target_pairs={{0,1},{1,0},{2,3},{3,2},{4,5},{5,4},{6,7},{7,6},{8,9},{9,8},{10,11... | collective-permute-start | bytes 135176 | tf_op jit(solution)/shard_map/ppermute | solution.py:400
  104.9 5.2 %collective-permute-start.12 = (f32[88,128]{1,0:T(8,128)S(1)}, f32[88,128]{1,0:T(8,128)S(1)}, u32[]{:S(2)}, u32[]{:S(2)}) collective-permute-start(f32[88,128]{1,0:T(8,128)S(1)} %get-tuple-element.60), channel_id=1, source_target_pairs={{0,2},{1,3},{2,0},{3,1},{4,6},{5,7},{6,4},{7,5},{8,10},{9,11},{10,... | collective-permute-start | bytes 135176 | tf_op jit(solution)/shard_map/ppermute | solution.py:400
  108.2 3.8 %collective-permute-start.13 = (f32[88,128]{1,0:T(8,128)S(1)}, f32[88,128]{1,0:T(8,128)S(1)}, u32[]{:S(2)}, u32[]{:S(2)}) collective-permute-start(f32[88,128]{1,0:T(8,128)S(1)} %get-tuple-element.59), channel_id=1, source_target_pairs={{0,3},{1,2},{2,1},{3,0},{4,7},{5,6},{6,5},{7,4},{8,11},{9,10},{10,... | collective-permute-start | bytes 135176 | tf_op jit(solution)/shard_map/ppermute | solution.py:400
  108.4 7.4 %collective-permute-start.10 = (bf16[3,64,128]{2,1,0:T(8,128)(2,1)S(1)}, bf16[3,64,128]{2,1,0:T(8,128)(2,1)S(1)}, u32[]{:S(2)}, u32[]{:S(2)}) collective-permute-start(bf16[3,64,128]{2,1,0:T(8,128)(2,1)S(1)} %edges.3), channel_id=1, source_target_pairs={{0,1},{1,0},{2,3},{3,2},{4,5},{5,4},{6,7},{7,6},{8,9},{9,8},{10,11... | collective-permute-start | bytes 147464 | tf_op jit(solution)/shard_map/ppermute | solution.py:362
  111.9 7.6 %collective-permute-start.14 = (f32[88,128]{1,0:T(8,128)S(1)}, f32[88,128]{1,0:T(8,128)S(1)}, u32[]{:S(2)}, u32[]{:S(2)}) collective-permute-start(f32[88,128]{1,0:T(8,128)S(1)} %fusion.1), channel_id=1, source_target_pairs={{0,4},{2,6},{4,8},{6,10},{8,12},{10,14},{12,0},{14,2},{1,5},{3,7},... | collective-permute-start | bytes 135176 | tf_op jit(solution)/shard_map/ppermute | solution.py:408
  113.0 6.5 %collective-permute-start.15 = (f32[88,128]{1,0:T(8,128)S(1)}, f32[88,128]{1,0:T(8,128)S(1)}, u32[]{:S(2)}, u32[]{:S(2)}) collective-permute-start(f32[88,128]{1,0:T(8,128)S(1)} %fusion.1), channel_id=1, source_target_pairs={{0,8},{2,10},{4,12},{6,14},{8,0},{10,2},{12,4},{14,6},{1,9},{3,11}... | collective-permute-start | bytes 135176 | tf_op jit(solution)/shard_map/ppermute | solution.py:408
  113.0 6.5 %collective-permute-start.16 = (f32[88,128]{1,0:T(8,128)S(1)}, f32[88,128]{1,0:T(8,128)S(1)}, u32[]{:S(2)}, u32[]{:S(2)}) collective-permute-start(f32[88,128]{1,0:T(8,128)S(1)} %fusion.1), channel_id=1, source_target_pairs={{0,12},{2,14},{4,0},{6,2},{8,4},{10,6},{12,8},{14,10},{1,13},{3,15... | collective-permute-start | bytes 135176 | tf_op jit(solution)/shard_map/ppermute | solution.py:408
  119.6 8.0 %collective-permute-start.17 = (f32[88,128]{1,0:T(8,128)S(1)}, f32[88,128]{1,0:T(8,128)S(1)}, u32[]{:S(2)}, u32[]{:S(2)}) collective-permute-start(f32[88,128]{1,0:T(8,128)S(1)} %add_add_fusion.rest_0_), channel_id=1, source_target_pairs={{0,1},{1,0},{2,3},{3,2},{4,5},{5,4},{6,7},{7,6},{8,9},{9,8},{10,11... | collective-permute-start | bytes 135176 | tf_op jit(solution)/shard_map/ppermute | solution.py:400
  120.2 7.4 %collective-permute-start.18 = (f32[88,128]{1,0:T(8,128)S(1)}, f32[88,128]{1,0:T(8,128)S(1)}, u32[]{:S(2)}, u32[]{:S(2)}) collective-permute-start(f32[88,128]{1,0:T(8,128)S(1)} %add_add_fusion.rest_0_), channel_id=1, source_target_pairs={{0,2},{1,3},{2,0},{3,1},{4,6},{5,7},{6,4},{7,5},{8,10},{9,11},{10,... | collective-permute-start | bytes 135176 | tf_op jit(solution)/shard_map/ppermute | solution.py:400
  120.2 7.4 %collective-permute-start.19 = (f32[88,128]{1,0:T(8,128)S(1)}, f32[88,128]{1,0:T(8,128)S(1)}, u32[]{:S(2)}, u32[]{:S(2)}) collective-permute-start(f32[88,128]{1,0:T(8,128)S(1)} %add_add_fusion.rest_0_), channel_id=1, source_target_pairs={{0,3},{1,2},{2,1},{3,0},{4,7},{5,6},{6,5},{7,4},{8,11},{9,10},{10,... | collective-permute-start | bytes 135176 | tf_op jit(solution)/shard_map/ppermute | solution.py:400
  (2 other events, 9.1 us)

commit v3 on v2

--- a/solution.py
+++ b/solution.py
@@ -46,29 +46,58 @@
     return jnp.concatenate(tiles, axis=1)
 
 
-def prep_kernel(x, out, head, tail, main):
-    some, rows, width = x.shape
-    tiles, _, channels, _ = out.shape
-    step = pl.program_id(0)
-
-    for cc in range(some):
-        body = x[cc].astype(F32)
+def prep_kernel(_, x, out, head, tail, landed, main, sems):
+    channels, rows, width = x.shape
+    tiles = width // 128
+    some = channels // sems.shape[0]
+    copies = [
+        pltpu.make_async_copy(
+            x.at[pl.ds(n * some, some)], landed.at[pl.ds(n * some, some)], sems.at[n]
+        )
+        for n in range(sems.shape[0])
+    ]
+    for copy in copies:
+        copy.start()
+    for n, copy in enumerate(copies):
+        copy.wait()
+        for c in range(n * some, (n + 1) * some):
+            body = landed[c].astype(F32)
+            for u in range(tiles):
+                at = (u * channels + c) * rows
+                main[at : at + rows, :] = body[:, 128 * u : 128 * (u + 1)]
+
+    def turn(i, _):
         for u in range(tiles):
-            at = pl.multiple_of((u * channels + step * some + cc) * rows, 8)
-            main[pl.ds(at, rows), :] = body[:, 128 * u : 128 * (u + 1)]
-
-    @pl.when(step == pl.num_programs(0) - 1)
-    def _():
-        def turn(i, _):
-            for u in range(tiles):
-                at = u * channels * rows + i
-                out[u, i] = main[pl.ds(at, channels, stride=rows), :].astype(BF16)
-            return 0
-
-        lax.fori_loop(0, rows, turn, 0, unroll=8)
-        for u in range(tiles):
-            head[u] = out[u, :DIL]
-            tail[u] = out[u, rows - DIL :]
+            at = u * channels * rows + i
+            out[u, i] = main[pl.ds(at, channels, stride=rows), :].astype(BF16)
+        return 0
+
+    lax.fori_loop(0, rows, turn, 0, unroll=8)
+    for u in range(tiles):
+        head[u] = out[u, :DIL]
+        tail[u] = out[u, rows - DIL :]
+
+
+def setup_kernel(scal, cw, cb, hw, labels, _, fwd, bwd, bias, head, headt, *pieces):
+    ch = cw.shape[2]
+    nbins, nb = hw.shape[0], head.shape[0]
+    for a in range(3):
+        for b in range(3):
+            at = (3 * a + b) * ch
+            fwd[:, at : at + ch] = cw[a, b]
+            bwd[:, at : at + ch] = cw[2 - a, 2 - b].astype(F32).T.astype(BF16)
+    bias[...] = jnp.broadcast_to(cb[...], (ch, ch)).T[:, 0:1]
+    full = jnp.concatenate([hw[...].astype(F32), jnp.zeros((nb - nbins, ch), F32)], axis=0)
+    head[...] = full.astype(BF16)
+    headt[...] = full.T.astype(BF16)
+    ncol, width = len(pieces), pieces[0].shape[1]
+    blocks = [labels[:, width * n : width * (n + 1)] for n in range(ncol)]
+    for d, piece in enumerate(pieces):
+        want = lax.rem(scal[4] + d, ncol)
+        value = blocks[0]
+        for n in range(1, ncol):
+            value = jnp.where(want == n, blocks[n], value)
+        piece[...] = value.astype(F32).astype(BF16)
 
 
 def edges_kernel(scal, field, above, below, *sides, ncol):
@@ -83,7 +112,9 @@
     for (tile, extra), out in zip(picks, sides):
 
         def add(slot, row, acc):
-            moved = pltpu.roll(row.astype(F32), lax.rem(slot * DIL + extra, 128), 1)
+            turn = slot * DIL + extra
+            turn = turn % 128 if isinstance(turn, int) else lax.rem(turn, 128)
+            moved = pltpu.roll(row.astype(F32), turn, 1)
             return jnp.where(lane == slot, moved, acc)
 
         for part in range(out.shape[0]):
@@ -98,56 +129,71 @@
             def body(i, acc):
                 return add(i + DIL - part * per, field[tile, i], acc)
 
-            acc = lax.fori_loop(start, stop, body, acc, unroll=4)
+            for i in range(start, stop):
+                acc = body(i, acc)
             if part == out.shape[0] - 1:
                 for ii in range(DIL):
                     acc = add(rows + DIL + ii - part * per, below[tile, ii], acc)
             out[part] = acc.astype(BF16)
 
 
-def border_kernel(scal, field, above, below, *rest, ncol):
-    sides, (out, lefts, rights) = rest[:-3], rest[-3:]
-    tiles, rows, channels, _ = field.shape
-    for p in range(lefts.shape[0]):
-        if ncol == 2:
-            first = scal[4] == 0
-            v = sides[0][p].astype(F32)
-            lefts[p] = jnp.where(first, 0.0, v)
-            rights[p] = jnp.where(first, v, 0.0)
-        else:
-            lefts[p] = sides[0][p].astype(F32)
-            rights[p] = sides[1][p].astype(F32)
+def place(out, i, row):
+    tiles = len(row)
+    lane = lax.broadcasted_iota(jnp.int32, row[0].shape, 1)
+    whole = pairs_of([v.astype(F32) for v in row])
+    before = pltpu.roll(whole, DIL, 1)
+    after = pltpu.roll(whole, whole.shape[1] - DIL, 1)
+    for u in range(tiles):
+        b = before[:, 128 * u : 128 * (u + 1)]
+        a = after[:, 128 * u : 128 * (u + 1)]
+        if u == 0:
+            b = jnp.where(lane < DIL, 0.0, b)
+        if u == tiles - 1:
+            a = jnp.where(lane >= 128 - DIL, 0.0, a)
+        out[u, i] = jnp.concatenate([b.astype(BF16), row[u], a.astype(BF16)], axis=0)
+
+
+def inner_kernel(field, out):
+    tiles, rows = field.shape[:2]
+
+    def body(i, _):
+        place(out, i + DIL, [field[u, i] for u in range(tiles)])
+        return 0
+
+    lax.fori_loop(0, rows, body, 0, unroll=8)
+
+
+def border_kernel(scal, above, below, *rest, ncol):
+    sides, (_, out) = rest[:-2], rest[-2:]
+    tiles, high, wide, _ = out.shape
+    channels = wide // 3
+    for i in range(DIL):
+        place(out, i, [above[u, i] for u in range(tiles)])
+        place(out, i + high - DIL, [below[u, i] for u in range(tiles)])
     lane = lax.broadcasted_iota(jnp.int32, (channels, 128), 1)
     per = 128 // DIL
-
-    def place(i, row):
-        part, at = i // per, lax.rem(i, per) * DIL
-        left = pltpu.roll(lefts[part], lax.rem(128 - at, 128), 1)
-        right = pltpu.roll(rights[part], lax.rem(256 - DIL - at, 128), 1)
-        row = [v.astype(F32) for v in row]
-        whole = pairs_of(row)
-        before = pltpu.roll(whole, DIL, 1)
-        after = pltpu.roll(whole, whole.shape[1] - DIL, 1)
-        for u in range(tiles):
-            b = before[:, 128 * u : 128 * (u + 1)]
-            a = after[:, 128 * u : 128 * (u + 1)]
-            if u == 0:
-                b = jnp.where(lane < DIL, left, b)
-            if u == tiles - 1:
-                a = jnp.where(lane >= 128 - DIL, right, a)
-            out[u, i] = jnp.concatenate(
-                [b.astype(BF16), row[u].astype(BF16), a.astype(BF16)], axis=0
-            )
-
-    for i in range(DIL):
-        place(i, [above[u, i] for u in range(tiles)])
-        place(i + rows + DIL, [below[u, i] for u in range(tiles)])
-
-    def body(i, _):
-        place(i + DIL, [field[u, i] for u in range(tiles)])
-        return 0
-
-    lax.fori_loop(0, rows, body, 0, unroll=4)
+    if ncol == 2:
+        first = scal[4] == 0
+        tile = jnp.where(first, tiles - 1, 0)
+        block = pl.multiple_of(jnp.where(first, 2 * channels, 0), channels)
+        base = jnp.where(first, 128 - DIL, 0)
+        jobs = [(sides[0], tile, block, base)]
+    else:
+        jobs = [(sides[0], 0, 0, 0), (sides[1], tiles - 1, 2 * channels, 128 - DIL)]
+    for side, tile, block, base in jobs:
+        mine = (lane >= base) & (lane < base + DIL)
+        for part in range(side.shape[0]):
+
+            def patch(ii, _):
+                i = part * per + ii
+                moved = pltpu.roll(
+                    side[part].astype(F32), lax.rem(128 + base - ii * DIL, 128), 1
+                )
+                spot = (tile, i, pl.ds(block, channels))
+                out[spot] = jnp.where(mine, moved, out[spot].astype(F32)).astype(BF16)
+                return 0
+
+            lax.fori_loop(0, min(per, high - part * per), patch, 0, unroll=8)
 
 
 def forward_kernel(scal, xs, w, bias, hw, hid, slope, direct, one, two, *, stage):
@@ -194,15 +240,19 @@
         two[m] = jnp.where(flip, low, high).astype(BF16)
 
 
-def middle_kernel(scal, hb, direct, labels, hid, slope, hwt, one, two, *rest, stage, last, nbins):
-    if stage:
-        before, rest = rest[1], rest[2:]
+def middle_kernel(scal, hb, direct, hid, slope, hwt, *rest, stage, counts, ncol, first, last, nbins):
+    ones, twos, rest = rest[: counts[0]], rest[counts[0] : sum(counts)], rest[sum(counts) :]
+    strips, rest = rest[:ncol], rest[ncol:]
+    if not first:
+        before, rest = rest[1], rest[3:]
     dpre, small, *ends, dl, hacc, bacc, cacc, lacc = rest
     nb, rows, _ = direct.shape
+    band = rows // ncol
     channels = hwt.shape[0]
     rq, extent = scal[0], scal[3]
     u = (rq >> 1) ^ stage
     flip = (rq & 1) == 1
+    crossed = scal[5] == 1
     for ref in (hacc, bacc, cacc, lacc):
         ref[...] = jnp.zeros_like(ref)
     dl[nbins * rows :, :] = jnp.zeros((dl.shape[0] - nbins * rows, 128), F32)
@@ -216,11 +266,21 @@
         base = pl.multiple_of(g * 8, 8)
         row_ids = scal[1] + base + lax.broadcasted_iota(jnp.int32, (8, 128), 0)
         valid = jnp.where((row_ids < extent) & (col_ids < extent), 1.0, 0.0)
-        wanted = labels[u, pl.ds(base, 8), :]
+        strip, at = base // band, pl.multiple_of(lax.rem(base, band), 8)
+        wanted = jnp.zeros((8, 128), F32)
+        for d in range(ncol):
+            here = lax.rem(scal[4] + ncol - strip, ncol) == d
+            rows8 = strips[d][pl.ds(at, 8), :].astype(F32)
+            for v in range(rows8.shape[1] // 128):
+                lanes = rows8[:, 128 * v : 128 * (v + 1)]
+                wanted = jnp.where(here & (u == v), lanes, wanted)
         logits = []
         for m in range((nbins + 1) // 2):
-            a = one[m, pl.ds(base, 8), :].astype(F32)
-            b = two[m, pl.ds(base, 8), :].astype(F32)
+            a, b = (
+                [ref[m, pl.ds(base, 8), :].astype(F32) for ref in refs] for refs in (ones, twos)
+            )
+            a = a[0] if len(a) == 1 else jnp.where(crossed, a[1], a[0])
+            b = b[0] if len(b) == 1 else jnp.where(crossed, b[1], b[0])
             a, b = jnp.where(flip, b, a), jnp.where(flip, a, b)
             mirror = (
                 jnp.where(low, a, pltpu.roll(b, 64, 1)),
@@ -280,43 +340,59 @@
         hacc[...],
         jnp.where(spot == channels, sums, jnp.where(spot == channels + 1, biases, loss)),
     )
-    small[...] = value + before[...] if stage else value
+    small[...] = value if first else value + before[...]
     if last:
         for v in range(dpre.shape[0]):
             ends[0][v] = dpre[v, :DIL]
             ends[1][v] = dpre[v, rows - DIL :]
 
 
-def weight_kernel(xs, dpre, small, out, acc, padded):
-    tiles, rows, channels, _ = dpre.shape
+def sum_kernel(*refs):
+    refs[-1][...] = functools.reduce(lambda a, b: a + b, [ref[...] for ref in refs[:-1]])
+
+
+def sum_of(values):
+    return call(sum_kernel, "sum", shape(values[0].shape, F32), tuple(values), us=0.5, mib=2)
+
+
+def weight_kernel(scal, xs, dpre, small, *rest, stage, first):
+    if not first:
+        before, rest = rest[0], rest[1:]
+    padded, outs = rest[-1], rest[:-1]
+    _, rows, channels, _ = dpre.shape
     wide = 3 * channels
-    acc[...] = jnp.zeros_like(acc)
-    for u in range(tiles):
-        padded[u, 0:8] = jnp.zeros((8, channels, 128), BF16)
-        padded[u, 8 : 8 + rows] = dpre[u]
-        padded[u, 8 + rows : 16 + rows] = jnp.zeros((8, channels, 128), BF16)
-
-    def body(g, _):
+    u = (scal[0] >> 1) ^ stage
+    padded[0:8] = jnp.zeros((8, channels, 128), BF16)
+    padded[8 : 8 + rows] = dpre[u]
+    padded[8 + rows :] = jnp.zeros((8, channels, 128), BF16)
+
+    def body(g, acc):
         left, right = [], []
         for ii in range(8):
             i = g * 8 + ii
-            for u in range(tiles):
-                left.append(
-                    jnp.concatenate([padded[u, i + 8 - DIL * a] for a in range(3)], axis=0)
-                )
-                right.append(xs[u, i])
+            left.append(
+                jnp.concatenate([padded[i + 8 - DIL * a] for a in range(3)], axis=0)
+            )
+            right.append(xs[u, i])
         acc[...] += lax.dot_general(
             pairs_of(left), pairs_of(right), (((1,), (1,)), ((), ())),
             preferred_element_type=F32,
         )
-        return 0
-
-    lax.fori_loop(0, rows // 8 + 1, body, 0)
+
+    acc = outs[-1] if len(outs) == 1 else outs[-2]
+    acc[...] = jnp.zeros_like(acc) if first else before[...]
+    lax.fori_loop(0, rows // 8 + 1, lambda g, _: body(g, acc), None)
+    if len(outs) == 1:
+        return
+    out, outs = outs[-1], outs[:-2]
     half = wide // 2
     out[0:wide, :] = acc[:, 0:128]
     out[wide : wide + half, 0:64] = acc[0:half, 128:192]
     out[wide : wide + half, 64:128] = acc[half:wide, 128:192]
     out[wide + half :, :] = small[...]
+    for n, piece in enumerate(outs):
+        size = piece.shape[0]
+        piece[...] = out[pl.ds(pl.multiple_of((scal[6] ^ n) * size, 8), size), :]
 
 
 def backward_kernel(ds, w, out, turned):
@@ -355,8 +431,7 @@
     )
 
 
-def with_border(field, above, below, sides, scal):
-    tiles, rows, channels, _ = field.shape
+def with_border(inner, above, below, sides, scal):
     ncol = lax.axis_size("col")
     if ncol == 2:
         got = [lax.ppermute(sides[0], "col", [(0, 1), (1, 0)])]
@@ -369,11 +444,22 @@
     return call(
         functools.partial(border_kernel, ncol=ncol),
         "border",
+        shape(inner.shape),
+        (scal, above, below, *got, inner),
+        us=1.5,
+        smem=1,
+        aliases={3 + len(got): 0},
+    )
+
+
+def inner_of(field):
+    tiles, rows, channels, _ = field.shape
+    return call(
+        inner_kernel,
+        "inner",
         shape((tiles, rows + 2 * DIL, 3 * channels, 128)),
-        (scal, field, above, below, *got),
-        us=4,
-        smem=1,
-        scratch=[pltpu.VMEM(got[0].shape, F32)] * 2,
+        (field,),
+        us=3,
     )
 
 
@@ -384,13 +470,14 @@
     return above, below
 
 
-def total_over_tiles(value):
+def piece_count(total):
     nrow, ncol = lax.axis_size("row"), lax.axis_size("col")
-    if ncol == 2 and nrow % 2 == 0 and nrow <= 8 and value.shape[0] % 32 == 0:
-        r, c = lax.axis_index("row"), lax.axis_index("col")
-        me = (r % 2) * 2 + c
-        parts = value.reshape(4, value.shape[0] // 4, value.shape[1])
-
+    return 4 if ncol == 2 and nrow % 2 == 0 and nrow <= 8 and total % 32 == 0 else 1
+
+
+def total_over_tiles(pieces):
+    nrow, ncol = lax.axis_size("row"), lax.axis_size("col")
+    if len(pieces) == 4:
         def near(v, d):
             perm = [
                 (i * 2 + j, (i ^ (d >> 1)) * 2 + (j ^ (d & 1)))
@@ -399,15 +486,11 @@
             ]
             return lax.ppermute(v, ROWS, perm)
 
-        own = lax.dynamic_index_in_dim(parts, me, 0, False)
-        for d in (1, 2, 3):
-            own = own + near(lax.dynamic_index_in_dim(parts, me ^ d, 0, False), d)
-        summed = own
-        for d in range(1, nrow // 2):
-            perm = [(i, (i + 2 * d) % nrow) for i in range(nrow)]
-            summed = summed + lax.ppermute(own, "row", perm)
-        got = [summed] + [near(summed, d) for d in (1, 2, 3)]
-        return got, jnp.stack([me, me ^ 1, me ^ 2, me ^ 3]).astype(jnp.int32)
+        own = sum_of([pieces[0]] + [near(pieces[d], d) for d in (1, 2, 3)])
+        turns = [[(i, (i + 2 * d) % nrow) for i in range(nrow)] for d in range(1, nrow // 2)]
+        own = sum_of([own] + [lax.ppermute(own, "row", turn) for turn in turns])
+        return [own] + [near(own, d) for d in (1, 2, 3)]
+    value = pieces[0]
     for axis, count in (("col", ncol), ("row", nrow)):
         if count & (count - 1):
             value = lax.psum(value, axis)
@@ -416,14 +499,14 @@
         while bit < count:
             value = value + lax.ppermute(value, axis, [(i, i ^ bit) for i in range(count)])
             bit *= 2
-    return [value], jnp.zeros((1,), jnp.int32)
-
-
-def unpack_kernel(where, extent, *rest):
+    return [value]
+
+
+def unpack_kernel(scal, *rest):
     parts, (taps, biases, heads, head_biases, loss, buf) = rest[:-6], rest[-6:]
     for n, part in enumerate(parts):
         size = part.shape[0]
-        buf[pl.ds(pl.multiple_of(where[n] * size, 8), size), :] = part[...]
+        buf[pl.ds(pl.multiple_of((scal[6] ^ n) * size, 8), size), :] = part[...]
     ch = taps.shape[2]
     half = 3 * ch // 2
     for a in range(3):
@@ -439,7 +522,7 @@
     heads[...] = small[: heads.shape[0], :ch]
     head_biases[...] = turned[ch : ch + 1, : heads.shape[0]]
     biases[...] = turned[ch + 1 : ch + 2, :]
-    area = (extent[0] * extent[0]).astype(F32)
+    area = (scal[3] * scal[3]).astype(F32)
     loss[...] = turned[ch + 2 : ch + 3, 0:1] / area
 
 
@@ -454,38 +537,46 @@
     nb = -(-nbins // 8) * 8
     pairs = (nbins + 1) // 2
     wide = 3 * channels
+    total = wide + wide // 2 + channels
     r, c = lax.axis_index("row"), lax.axis_index("col")
 
-    scal = jnp.stack([r % q, r * rows, c * width, lengths[0], c]).astype(jnp.int32)
-    w_fwd = conv_weight.transpose(2, 0, 1, 3).reshape(channels, 9 * channels)
-    w_bwd = conv_weight[::-1, ::-1].transpose(3, 0, 1, 2).reshape(channels, 9 * channels)
-    hw = jnp.pad(head_weight, ((0, nb - nbins), (0, 0)))
-
+    count = piece_count(total)
+    mine = (r % 2) * 2 + c if count == 4 else 0 * r
+    crossed = (r // q != c).astype(jnp.int32)
+    scal = jnp.stack([r % q, r * rows, c * width, lengths[0], c, crossed, mine]).astype(jnp.int32)
     field = (tiles, rows, channels, 128)
     strip = (tiles, DIL, channels, 128)
     xt, head, tail = pl.pallas_call(
         prep_kernel,
-        grid=(channels // 8,),
-        in_specs=[pl.BlockSpec((8, rows, width), lambda g: (g, 0, 0))],
+        in_specs=[SM, pl.BlockSpec(memory_space=pltpu.HBM)],
         out_specs=[VM, VM, VM],
         out_shape=[shape(field), shape(strip), shape(strip)],
-        scratch_shapes=[pltpu.VMEM((tiles * channels * rows, 128), F32)],
+        scratch_shapes=[
+            pltpu.VMEM(x.shape, BF16),
+            pltpu.VMEM((tiles * channels * rows, 128), F32),
+            pltpu.SemaphoreType.DMA((8,)),
+        ],
         compiler_params=grant(8),
         cost_estimate=cost(4),
         name="prep",
-    )(x)
+    )(scal, pltpu.with_memory_space_constraint(x, pltpu.HBM))
     above, below = row_halo(head, tail)
-    xs = with_border(xt, above, below, side_columns(xt, above, below, scal), scal)
-
-    band = labels.shape[0]
-    mine = labels.astype(BF16).reshape(band, ncol, width)
-    strips = jnp.zeros((ncol, band, width), BF16)
-    for d in range(ncol):
-        piece = lax.dynamic_index_in_dim(mine, (c + d) % ncol, axis=1, keepdims=False)
-        if d:
-            piece = lax.ppermute(piece, "col", [(i, (i + d) % ncol) for i in range(ncol)])
-        strips = lax.dynamic_update_index_in_dim(strips, piece, (c - d) % ncol, axis=0)
-    tile_labels = strips.reshape(rows, tiles, 128).transpose(1, 0, 2).astype(jnp.int32)
+    sides = side_columns(xt, above, below, scal)
+    w_fwd, w_bwd, bias, hw, hwt, *mine = call(
+        setup_kernel,
+        "setup",
+        [shape((channels, 9 * channels))] * 2
+        + [shape((channels, 1), F32), shape((nb, channels)), shape((channels, nb))]
+        + [shape((labels.shape[0], width))] * ncol,
+        (scal, conv_weight, conv_bias[None], head_weight, labels, tail),
+        us=2,
+        smem=1,
+    )
+    strips = mine[:1] + [
+        lax.ppermute(mine[d], "col", [(i, (i + d) % ncol) for i in range(ncol)])
+        for d in range(1, ncol)
+    ]
+    xs = with_border(inner_of(xt), above, below, sides, scal)
 
     kept, got = [], []
     for stage in range(tiles):
@@ -494,7 +585,7 @@
             functools.partial(forward_kernel, stage=stage),
             "forward",
             [shape(field[1:]), shape(field[1:]), shape((nb * rows, 128), F32), block, block],
-            (scal, xs, w_fwd, conv_bias[:, None], hw),
+            (scal, xs, w_fwd, bias, hw),
             us=6,
             smem=1,
         )
@@ -506,28 +597,41 @@
                 for i in range(nrow)
                 for j in range(ncol)
             ]
-            got.append(lax.ppermute(sends[e], ROWS, perm))
-
-    dpre = small = ends = None
-    for stage in range(tiles):
+            if ncol > 2 or e == 0:
+                got.append([lax.ppermute(sends[e], ROWS, perm)])
+                continue
+            near = [(a, b) for a, b in perm if a % ncol == b % ncol]
+            far = [(a, b) for a, b in perm if a % ncol != b % ncol]
+            over = [(a, a + b % ncol - a % ncol) for a, b in far]
+            along = [(a + b % ncol - a % ncol, b) for a, b in far]
+            same = lax.ppermute(sends[e], ROWS, near)
+            relayed = lax.ppermute(sends[e], ROWS, over)
+            got.append([same, lax.ppermute(relayed, ROWS, along)])
+
+    dpre = small = ends = taps = None
+    order = list(range(tiles))
+    for stage in order:
         hid, slope, direct = kept[stage]
+        ones, twos = got[2 * stage : 2 * stage + 2]
         args = (
             scal,
             head_bias,
             direct.reshape(nb, rows, 128),
-            tile_labels,
             hid,
             slope,
-            hw.T,
-            got[2 * stage],
-            got[2 * stage + 1],
+            hwt,
+            *ones,
+            *twos,
+            *strips,
         )
-        last = stage == tiles - 1
+        first, last = stage == order[0], stage == order[-1]
         dpre, small, *ends = call(
-            functools.partial(middle_kernel, stage=stage, last=last, nbins=nbins),
+            functools.partial(
+                middle_kernel, stage=stage, counts=(len(ones), len(twos)), ncol=ncol, first=first, last=last, nbins=nbins
+            ),
             "middle",
             [shape(field), shape((channels, 128), F32)] + [shape(strip)] * (2 * last),
-            args + ((dpre, small) if stage else ()),
+            args + (() if first else (dpre, small, taps)),
             us=5,
             smem=2,
             scratch=[
@@ -537,26 +641,28 @@
                 pltpu.VMEM((channels, 128), F32),
                 pltpu.VMEM((8, 128), F32),
             ],
-            aliases={len(args): 0} if stage else None,
+            aliases=None if first else {len(args): 0},
         )
-
-    sums = call(
-        weight_kernel,
-        "weights",
-        shape((wide + wide // 2 + channels, 128), F32),
-        (xs, dpre, small),
-        us=4,
-        mib=8,
-        scratch=[
-            pltpu.VMEM((wide, wide), F32),
-            pltpu.VMEM((tiles, rows + 16, channels, 128), BF16),
-        ],
-    )
+        square = (wide, wide)
+        pieces = shape((total // count, 128), F32)
+        taps = call(
+            functools.partial(weight_kernel, stage=stage, first=first),
+            "weights",
+            [pieces] * count if last else shape(square, F32),
+            (scal, xs, dpre, small) + (() if first else (taps,)),
+            us=2.5,
+            mib=8,
+            smem=1,
+            scratch=[pltpu.VMEM(square, F32), pltpu.VMEM((total, 128), F32)] * last
+            + [pltpu.VMEM((rows + 16, channels, 128), BF16)],
+        )
+
+    pieces = taps
     above, below = row_halo(*ends)
     sides = side_columns(dpre, above, below, scal)
-    sides, sums = lax.optimization_barrier((sides, sums))
-    ds = with_border(dpre, above, below, sides, scal)
-    parts, where = total_over_tiles(sums)
+    sides, pieces = lax.optimization_barrier((sides, pieces))
+    ds = with_border(inner_of(dpre), above, below, sides, scal)
+    parts = total_over_tiles(pieces)
 
     pair_gradient = pl.pallas_call(
         backward_kernel,
@@ -572,7 +678,7 @@
 
     conv_grad, biases, heads, head_biases, loss = pl.pallas_call(
         unpack_kernel,
-        in_specs=[SM, SM] + [VM] * len(parts),
+        in_specs=[SM] + [VM] * len(parts),
         out_shape=[
             shape((3, 3, channels, channels), F32),
             shape((1, channels), F32),
@@ -580,11 +686,11 @@
             shape((1, nbins), F32),
             shape((1, 1), F32),
         ],
-        scratch_shapes=[pltpu.VMEM(sums.shape, F32)],
+        scratch_shapes=[pltpu.VMEM((total, 128), F32)],
         compiler_params=grant(4),
         cost_estimate=cost(1),
         name="unpack",
-    )(where, lengths, *parts)
+    )(scal, *parts)
     return (
         pair_gradient,
         conv_grad,

time: 129 us -> 111 us (0.86)
  waiting for transfers between devices: 39.6 us -> 23.1 us
  Pallas kernels: 46.7 us -> 49.3 us
  local copies, waits for them, and re-layouts: 2.62 us -> 0.12 us
  starting transfers between devices: 38.3 us -> 36.5 us
    ppermute x8 -> x12, waiting for transfers between devices: 35.2 us -> 21.4 us  [the longest x2 11.5 us: per_device(): got.append([lax.ppermute(sends[e], ROWS, perm)])]
    ppermute x6, starting transfers between devices: 16.3 us -> 5.57 us  [near(): return lax.ppermute(v, ROWS, perm)]
    ppermute x8 -> x12, starting transfers between devices: 11.8 us -> 18.5 us  [the longest x2 5.28 us: per_device(): same = lax.ppermute(sends[e], ROWS, near)]
    unnamed x15 -> x10, local copies, waits for them, and re-layouts: 1.81 us -> 0.03 us
    pallas_call x2, Pallas kernels: 5.18 us -> 6.93 us  [the longest x1 5.54 us: per_device(): pl.pallas_call(prep_kernel, in_specs=[SM, pl.BlockSpec(memory_space=pltpu...]
    ppermute x2, starting transfers between devices: 3.24 us -> 4.69 us  [with_border(): got = [lax.ppermute(sides[0], 'col', [(0, 1), (1, 0)])]]
    ppermute x6, waiting for transfers between devices: 1.84 us -> 0.4 us  [near(): return lax.ppermute(v, ROWS, perm)]
    pallas_call x9 -> x15, Pallas kernels: 35.7 us -> 36.6 us  [call(): pl.pallas_call(body, out_shape=out_shape, in_specs=[SM] * smem + [VM] * (...]
  transfers between devices with their start and end apart: 20 -> 24, of which waited for: 5 -> 6; matrix products, arithmetic and copies ran while one was open for 1% -> 0% of each run, Pallas kernels for 20% -> 26%
where the time goes in v3:
time: 111 us
  Pallas kernels  49.3 us (44%)
  starting transfers between devices  36.5 us (33%)
  waiting for transfers between devices  23.1 us (21%)
  between operations  1.62 us (1%)
    pallas_call x15, Pallas kernels, call(): pl.pallas_call(body, out_shape=out_shape, in_specs=[SM] * smem + [VM] * (...  36.6 us
    ppermute x2, waiting for transfers between devices, per_device(): got.append([lax.ppermute(sends[e], ROWS, perm)])  11.5 us
    pallas_call x1, Pallas kernels, per_device(): pl.pallas_call(backward_kernel, grid=(rows // 8,), in_specs=[VM, VM], out...  5.81 us
    ppermute x6, starting transfers between devices, near(): return lax.ppermute(v, ROWS, perm)  5.57 us
    pallas_call x1, Pallas kernels, per_device(): pl.pallas_call(prep_kernel, in_specs=[SM, pl.BlockSpec(memory_space=pltpu...  5.54 us
    ppermute x2, starting transfers between devices, per_device(): same = lax.ppermute(sends[e], ROWS, near)  5.28 us
    ppermute x2, starting transfers between devices, row_halo(): above = lax.ppermute(tail, 'row', [(i, i + 1) for i in range(count - 1)])  5.06 us
    ppermute x2, starting transfers between devices, with_border(): got = [lax.ppermute(sides[0], 'col', [(0, 1), (1, 0)])]  4.69 us
  transfers between devices with their start and end apart: 24, of which 6 were waited for; matrix products, arithmetic and copies ran while one was open for 0% of the time, Pallas kernels for 26%

profile of v3, /device:TPU:0, one launch (start us, length us, event | category | flops | bytes accessed | tf_op | source)
XLA Modules:
  0.0 110.6 jit_solution(1879271744403022914)
XLA Ops:
  1.4 5.5 %prep.1 = (bf16[2,64,64,128]{3,2,1,0:T(8,128)(2,1)S(1)}, bf16[2,4,64,128]{3,2,1,0:T(8,128)(2,1)S(1)}, bf16[2,4,64,128]{3,2,1,0:T(8,128)(2,1)S(1)}) custom-call(s32[7]{0:T(128)S(1)} %stack.31._.scal, bf16[64,64,256]{2,1,0:T(8,128)(2,1)} %x.1), custom_call_target="tpu_custom_call" | custom-call | flops 4400000000 | tf_op jit(solution)/shard_map/prep/pallas_call | solution.py:549
  8.2 3.0 %collective-permute-start = (bf16[2,4,64,128]{3,2,1,0:T(8,128)(2,1)S(1)}, bf16[2,4,64,128]{3,2,1,0:T(8,128)(2,1)S(1)}, u32[]{:S(2)}, u32[]{:S(2)}) collective-permute-start(bf16[2,4,64,128]{3,2,1,0:T(8,128)(2,1)S(1)} %get-tuple-element.46._), channel_id=1, source_target_pairs={{0,2},{2,4},{4,6},{6,8},{8,10},{10,12},{12,14},{1,3},{3,5},{5,7},{... | collective-permute-start | bytes 393224 | tf_op jit(solution)/shard_map/ppermute | solution.py:468
  11.3 1.7 %inner.2.rest_1_ = bf16[2,72,192,128]{3,2,1,0:T(8,128)(2,1)S(1)} custom-call(bf16[2,64,64,128]{3,2,1,0:T(8,128)(2,1)S(1)} %get-tuple-element.48.field), custom_call_target="tpu_custom_call" | custom-call | flops 3300000000 | tf_op jit(solution)/shard_map/inner/pallas_call | solution.py:28
  14.0 3.0 %collective-permute-start.2 = (bf16[3,64,128]{2,1,0:T(8,128)(2,1)S(1)}, bf16[3,64,128]{2,1,0:T(8,128)(2,1)S(1)}, u32[]{:S(2)}, u32[]{:S(2)}) collective-permute-start(bf16[3,64,128]{2,1,0:T(8,128)(2,1)S(1)} %edges.2), channel_id=1, source_target_pairs={{0,1},{1,0},{2,3},{3,2},{4,5},{5,4},{6,7},{7,6},{8,9},{9,8},{10,11... | collective-permute-start | bytes 147464 | tf_op jit(solution)/shard_map/ppermute | solution.py:437
  19.1 1.7 %border.2.xs = bf16[2,72,192,128]{3,2,1,0:T(8,128)(2,1)S(1)} custom-call(s32[7]{0:T(128)S(1)} %stack.31._.scal, bf16[2,4,64,128]{3,2,1,0:T(8,128)(2,1)S(1)} %collective-permute-done.above, bf16[2,4,64,128]{3,2,1,0:T(8,128)(2,1)S(1)} %collective-permute-done.1.below, ...), custom_call_target="tpu_custom_call", output_to_operand_aliasing={{}: (4, {})} | custom-call | flops 1650000000 | tf_op jit(solution)/shard_map/border/pallas_call | solution.py:28
  20.8 5.7 %forward.3 = (bf16[64,64,128]{2,1,0:T(8,128)(2,1)S(1)}, bf16[64,64,128]{2,1,0:T(8,128)(2,1)S(1)}, f32[2560,128]{1,0:T(8,128)S(1)}, bf16[19,64,128]{2,1,0:T(8,128)(2,1)S(1)}, bf16[19,64,128]{2,1,0:T(8,128)(2,1)S(1)}) custom-call(s32[7]{0:T(128)S(1)} %stack.31._.scal, bf16[2,72,192,128]{3,2,1,0:T(8,128)(2,1)S(1)} %border.2.xs, ...), custom_call_target="tpu_custom_call" | custom-call | flops 6600000000 | tf_op jit(solution)/shard_map/forward/pallas_call | solution.py:28
  28.5 5.7 %forward.2 = (bf16[64,64,128]{2,1,0:T(8,128)(2,1)S(1)}, bf16[64,64,128]{2,1,0:T(8,128)(2,1)S(1)}, f32[2560,128]{1,0:T(8,128)S(1)}, bf16[19,64,128]{2,1,0:T(8,128)(2,1)S(1)}, bf16[19,64,128]{2,1,0:T(8,128)(2,1)S(1)}) custom-call(s32[7]{0:T(128)S(1)} %stack.31._.scal, bf16[2,72,192,128]{3,2,1,0:T(8,128)(2,1)S(1)} %border.2.xs, ...), custom_call_target="tpu_custom_call" | custom-call | flops 6600000000 | tf_op jit(solution)/shard_map/forward/pallas_call | solution.py:28
  35.5 2.6 %collective-permute-start.9 = (bf16[19,64,128]{2,1,0:T(8,128)(2,1)S(1)}, bf16[19,64,128]{2,1,0:T(8,128)(2,1)S(1)}, u32[]{:S(2)}, u32[]{:S(2)}) collective-permute-start(bf16[19,64,128]{2,1,0:T(8,128)(2,1)S(1)} %get-tuple-element.64), channel_id=1, source_target_pairs={{0,2},{2,0},{4,6},{6,4},{9,11},{11,9},{13,15},{15,13},{16,18},{18,... | collective-permute-start | bytes 933896 | tf_op jit(solution)/shard_map/ppermute | solution.py:607
  38.1 3.6 %collective-permute-done.10 = bf16[19,64,128]{2,1,0:T(8,128)(2,1)S(1)} collective-permute-done((bf16[19,64,128]{2,1,0:T(8,128)(2,1)S(1)}, bf16[19,64,128]{2,1,0:T(8,128)(2,1)S(1)}, u32[]{:S(2)}, u32[]{:S(2)}) %collective-permute-start.10) | collective-permute-done | bytes 311328 | tf_op jit(solution)/shard_map/ppermute | solution.py:608
  41.7 1.7 %collective-permute-start.11 = (bf16[19,64,128]{2,1,0:T(8,128)(2,1)S(1)}, bf16[19,64,128]{2,1,0:T(8,128)(2,1)S(1)}, u32[]{:S(2)}, u32[]{:S(2)}) collective-permute-start(bf16[19,64,128]{2,1,0:T(8,128)(2,1)S(1)} %collective-permute-done.10), channel_id=1, source_target_pairs={{0,10},{2,8},{4,14},{6,12},{9,3},{11,1},{13,7},{15,5},{16,26},{18,... | collective-permute-start | bytes 933896 | tf_op jit(solution)/shard_map/ppermute | solution.py:609
  43.4 2.1 %collective-permute-start.7 = (bf16[32,256]{1,0:T(8,128)(2,1)S(1)}, bf16[32,256]{1,0:T(8,128)(2,1)S(1)}, u32[]{:S(2)}, u32[]{:S(2)}) collective-permute-start(bf16[32,256]{1,0:T(8,128)(2,1)S(1)} %get-tuple-element.59), channel_id=1, source_target_pairs={{0,1},{1,0},{2,3},{3,2},{4,5},{5,4},{6,7},{7,6},{8,9},{9,8},{10,11... | collective-permute-start | bytes 49160 | tf_op jit(solution)/shard_map/ppermute | solution.py:576
  45.5 3.6 %collective-permute-done.7.rest_4_ = bf16[32,256]{1,0:T(8,128)(2,1)S(1)} collective-permute-done((bf16[32,256]{1,0:T(8,128)(2,1)S(1)}, bf16[32,256]{1,0:T(8,128)(2,1)S(1)}, u32[]{:S(2)}, u32[]{:S(2)}) %collective-permute-start.7) | collective-permute-done | bytes 16416 | tf_op jit(solution)/shard_map/ppermute | solution.py:576
  49.0 2.7 %collective-permute-start.4 = (bf16[19,64,128]{2,1,0:T(8,128)(2,1)S(1)}, bf16[19,64,128]{2,1,0:T(8,128)(2,1)S(1)}, u32[]{:S(2)}, u32[]{:S(2)}) collective-permute-start(bf16[19,64,128]{2,1,0:T(8,128)(2,1)S(1)} %get-tuple-element.57), channel_id=1, source_target_pairs={{0,6},{2,4},{4,2},{6,0},{9,15},{11,13},{13,11},{15,9},{16,22},{18,... | collective-permute-start | bytes 933896 | tf_op jit(solution)/shard_map/ppermute | solution.py:607
  53.9 4.6 %middle.2 = (bf16[2,64,64,128]{3,2,1,0:T(8,128)(2,1)S(1)}, f32[64,128]{1,0:T(8,128)S(1)}) custom-call(s32[7]{0:T(128)S(1)} %stack.31._.scal, f32[37]{0:T(128)S(1)} %copy-done.4, f32[40,64,128]{2,1,0:T(8,128)S(1)} %bitcast.14, bf16[64,64,128]{2,1,0:T(8,128)(2,1)S(1)} %get-tuple-element.61.hid, bf16[64,64,128]{2,1,0:T(8,128)(2,1)S(1)} %get-tuple-element.62.slope, ...), custom_call_target="tpu_custom_call" | custom-call | flops 5500000256 | tf_op jit(solution)/shard_map/middle/pallas_call | solution.py:28
  58.4 3.3 %weights.2.rest_7_.rest_0_ = f32[192,192]{1,0:T(8,128)S(1)} custom-call(s32[7]{0:T(128)S(1)} %stack.31._.scal, bf16[2,72,192,128]{3,2,1,0:T(8,128)(2,1)S(1)} %border.2.xs, bf16[2,64,64,128]{3,2,1,0:T(8,128)(2,1)S(1)} %get-tuple-element.65.dpre.rest_5_, f32[64,128]{1,0:T(8,128)S(1)} %get-tuple-element.66.small.rest_6_), custom_call_target="tpu_custom_call" | custom-call | flops 2750000128 | tf_op jit(solution)/shard_map/weights/pallas_call | solution.py:28
  61.7 11.5 %collective-permute-done.3.rest_0_ = bf16[19,64,128]{2,1,0:T(8,128)(2,1)S(1)} collective-permute-done((bf16[19,64,128]{2,1,0:T(8,128)(2,1)S(1)}, bf16[19,64,128]{2,1,0:T(8,128)(2,1)S(1)}, u32[]{:S(2)}, u32[]{:S(2)}) %collective-permute-start.3) | collective-permute-done | bytes 311328 | tf_op jit(solution)/shard_map/ppermute | solution.py:601
  73.3 4.6 %middle.3 = (bf16[2,64,64,128]{3,2,1,0:T(8,128)(2,1)S(1)}, f32[64,128]{1,0:T(8,128)S(1)}, bf16[2,4,64,128]{3,2,1,0:T(8,128)(2,1)S(1)}, bf16[2,4,64,128]{3,2,1,0:T(8,128)(2,1)S(1)}) custom-call(s32[7]{0:T(128)S(1)} %stack.31._.scal, f32[37]{0:T(128)S(1)} %copy-done.4, f32[40,64,128]{2,1,0:T(8,128)S(1)} %bitcast.13, ...), custom_call_target="tpu_custom_call", output_to_operand_aliasing={{0}: (11, {})} | custom-call | flops 5500000256 | tf_op jit(solution)/shard_map/middle/pallas_call | solution.py:28
  77.9 2.0 %collective-permute-start.12 = (bf16[2,4,64,128]{3,2,1,0:T(8,128)(2,1)S(1)}, bf16[2,4,64,128]{3,2,1,0:T(8,128)(2,1)S(1)}, u32[]{:S(2)}, u32[]{:S(2)}) collective-permute-start(bf16[2,4,64,128]{3,2,1,0:T(8,128)(2,1)S(1)} %get-tuple-element.67), channel_id=1, source_target_pairs={{0,2},{2,4},{4,6},{6,8},{8,10},{10,12},{12,14},{1,3},{3,5},{5,7},{... | collective-permute-start | bytes 393224 | tf_op jit(solution)/shard_map/ppermute | solution.py:468
  81.2 3.3 %weights.3 = (f32[88,128]{1,0:T(8,128)S(1)}, f32[88,128]{1,0:T(8,128)S(1)}, f32[88,128]{1,0:T(8,128)S(1)}, f32[88,128]{1,0:T(8,128)S(1)}) custom-call(s32[7]{0:T(128)S(1)} %stack.31._.scal, bf16[2,72,192,128]{3,2,1,0:T(8,128)(2,1)S(1)} %border.2.xs, bf16[2,64,64,128]{3,2,1,0:T(8,128)(2,1)S(1)} %get-tuple-element.69.field.dpre, ...), custom_call_target="tpu_custom_call" | custom-call | flops 2750000128 | tf_op jit(solution)/shard_map/weights/pallas_call | solution.py:28
  85.5 2.0 %collective-permute-start.15 = (f32[88,128]{1,0:T(8,128)S(1)}, f32[88,128]{1,0:T(8,128)S(1)}, u32[]{:S(2)}, u32[]{:S(2)}) collective-permute-start(f32[88,128]{1,0:T(8,128)S(1)} %get-tuple-element.78), channel_id=1, source_target_pairs={{0,1},{1,0},{2,3},{3,2},{4,5},{5,4},{6,7},{7,6},{8,9},{9,8},{10,11... | collective-permute-start | bytes 135176 | tf_op jit(solution)/shard_map/ppermute | solution.py:487
  92.6 2.7 %collective-permute-start.20 = (f32[88,128]{1,0:T(8,128)S(1)}, f32[88,128]{1,0:T(8,128)S(1)}, u32[]{:S(2)}, u32[]{:S(2)}) collective-permute-start(f32[88,128]{1,0:T(8,128)S(1)} %sum.2.refs_0_), channel_id=1, source_target_pairs={{0,12},{2,14},{4,0},{6,2},{8,4},{10,6},{12,8},{14,10},{1,13},{3,15... | collective-permute-start | bytes 135176 | tf_op jit(solution)/shard_map/ppermute | solution.py:491
  96.7 1.7 %border.3.ds = bf16[2,72,192,128]{3,2,1,0:T(8,128)(2,1)S(1)} custom-call(s32[7]{0:T(128)S(1)} %stack.31._.scal, bf16[2,4,64,128]{3,2,1,0:T(8,128)(2,1)S(1)} %collective-permute-done.12.above, bf16[2,4,64,128]{3,2,1,0:T(8,128)(2,1)S(1)} %collective-permute-done.13.below, ...), custom_call_target="tpu_custom_call", output_to_operand_aliasing={{}: (4, {})} | custom-call | flops 1650000000 | tf_op jit(solution)/shard_map/border/pallas_call | solution.py:28
  98.4 2.7 %collective-permute-done.19.refs_2_ = f32[88,128]{1,0:T(8,128)S(1)} collective-permute-done((f32[88,128]{1,0:T(8,128)S(1)}, f32[88,128]{1,0:T(8,128)S(1)}, u32[]{:S(2)}, u32[]{:S(2)}) %collective-permute-start.19) | collective-permute-done | bytes 45088 | tf_op jit(solution)/shard_map/ppermute | solution.py:491
  103.4 5.8 %backward.1 = bf16[64,64,256]{2,1,0:T(8,128)(2,1)} custom-call(bf16[2,72,192,128]{3,2,1,0:T(8,128)(2,1)S(1)} %border.3.ds, bf16[64,576]{1,0:T(8,128)(2,1)S(1)} %get-tuple-element.76.w), custom_call_target="tpu_custom_call" | custom-call | flops 6600000000 | tf_op jit(solution)/shard_map/backward/pallas_call | solution.py:667
  (53 shorter events, 22.2 us)
Async XLA Ops:
  6.9 6.1 %collective-permute-start.1 = (bf16[2,4,64,128]{3,2,1,0:T(8,128)(2,1)S(1)}, bf16[2,4,64,128]{3,2,1,0:T(8,128)(2,1)S(1)}, u32[]{:S(2)}, u32[]{:S(2)}) collective-permute-start(bf16[2,4,64,128]{3,2,1,0:T(8,128)(2,1)S(1)} %get-tuple-element.47), channel_id=1, source_target_pairs={{2,0},{4,2},{6,4},{8,6},{10,8},{12,10},{14,12},{3,1},{5,3},{7,5},{... | collective-permute-start | bytes 393224 | tf_op jit(solution)/shard_map/ppermute | solution.py:469
  8.2 4.8 %collective-permute-start = (bf16[2,4,64,128]{3,2,1,0:T(8,128)(2,1)S(1)}, bf16[2,4,64,128]{3,2,1,0:T(8,128)(2,1)S(1)}, u32[]{:S(2)}, u32[]{:S(2)}) collective-permute-start(bf16[2,4,64,128]{3,2,1,0:T(8,128)(2,1)S(1)} %get-tuple-element.46._), channel_id=1, source_target_pairs={{0,2},{2,4},{4,6},{6,8},{8,10},{10,12},{12,14},{1,3},{3,5},{5,7},{... | collective-permute-start | bytes 393224 | tf_op jit(solution)/shard_map/ppermute | solution.py:468
  14.0 5.1 %collective-permute-start.2 = (bf16[3,64,128]{2,1,0:T(8,128)(2,1)S(1)}, bf16[3,64,128]{2,1,0:T(8,128)(2,1)S(1)}, u32[]{:S(2)}, u32[]{:S(2)}) collective-permute-start(bf16[3,64,128]{2,1,0:T(8,128)(2,1)S(1)} %edges.2), channel_id=1, source_target_pairs={{0,1},{1,0},{2,3},{3,2},{4,5},{5,4},{6,7},{7,6},{8,9},{9,8},{10,11... | collective-permute-start | bytes 147464 | tf_op jit(solution)/shard_map/ppermute | solution.py:437
  26.5 25.2 %collective-permute-start.8 = (bf16[19,64,128]{2,1,0:T(8,128)(2,1)S(1)}, bf16[19,64,128]{2,1,0:T(8,128)(2,1)S(1)}, u32[]{:S(2)}, u32[]{:S(2)}) collective-permute-start(bf16[19,64,128]{2,1,0:T(8,128)(2,1)S(1)} %get-tuple-element.63), channel_id=1, source_target_pairs={{0,0},{1,8},{2,2},{3,10},{4,4},{5,12},{6,6},{7,14},{8,1},{9,9},{10... | collective-permute-start | bytes 933896 | tf_op jit(solution)/shard_map/ppermute | solution.py:601
  27.2 14.5 %collective-permute-start.10 = (bf16[19,64,128]{2,1,0:T(8,128)(2,1)S(1)}, bf16[19,64,128]{2,1,0:T(8,128)(2,1)S(1)}, u32[]{:S(2)}, u32[]{:S(2)}) collective-permute-start(bf16[19,64,128]{2,1,0:T(8,128)(2,1)S(1)} %get-tuple-element.64), channel_id=1, source_target_pairs={{1,0},{3,2},{5,4},{7,6},{8,9},{10,11},{12,13},{14,15},{17,16},{19,... | collective-permute-start | bytes 933896 | tf_op jit(solution)/shard_map/ppermute | solution.py:608
  34.2 18.2 %collective-permute-start.5 = (bf16[19,64,128]{2,1,0:T(8,128)(2,1)S(1)}, bf16[19,64,128]{2,1,0:T(8,128)(2,1)S(1)}, u32[]{:S(2)}, u32[]{:S(2)}) collective-permute-start(bf16[19,64,128]{2,1,0:T(8,128)(2,1)S(1)} %get-tuple-element.57), channel_id=1, source_target_pairs={{1,0},{3,2},{5,4},{7,6},{8,9},{10,11},{12,13},{14,15},{17,16},{19,... | collective-permute-start | bytes 933896 | tf_op jit(solution)/shard_map/ppermute | solution.py:608
  35.5 18.4 %collective-permute-start.9 = (bf16[19,64,128]{2,1,0:T(8,128)(2,1)S(1)}, bf16[19,64,128]{2,1,0:T(8,128)(2,1)S(1)}, u32[]{:S(2)}, u32[]{:S(2)}) collective-permute-start(bf16[19,64,128]{2,1,0:T(8,128)(2,1)S(1)} %get-tuple-element.64), channel_id=1, source_target_pairs={{0,2},{2,0},{4,6},{6,4},{9,11},{11,9},{13,15},{15,13},{16,18},{18,... | collective-permute-start | bytes 933896 | tf_op jit(solution)/shard_map/ppermute | solution.py:607
  41.7 12.2 %collective-permute-start.11 = (bf16[19,64,128]{2,1,0:T(8,128)(2,1)S(1)}, bf16[19,64,128]{2,1,0:T(8,128)(2,1)S(1)}, u32[]{:S(2)}, u32[]{:S(2)}) collective-permute-start(bf16[19,64,128]{2,1,0:T(8,128)(2,1)S(1)} %collective-permute-done.10), channel_id=1, source_target_pairs={{0,10},{2,8},{4,14},{6,12},{9,3},{11,1},{13,7},{15,5},{16,26},{18,... | collective-permute-start | bytes 933896 | tf_op jit(solution)/shard_map/ppermute | solution.py:609
  43.4 5.6 %collective-permute-start.7 = (bf16[32,256]{1,0:T(8,128)(2,1)S(1)}, bf16[32,256]{1,0:T(8,128)(2,1)S(1)}, u32[]{:S(2)}, u32[]{:S(2)}) collective-permute-start(bf16[32,256]{1,0:T(8,128)(2,1)S(1)} %get-tuple-element.59), channel_id=1, source_target_pairs={{0,1},{1,0},{2,3},{3,2},{4,5},{5,4},{6,7},{7,6},{8,9},{9,8},{10,11... | collective-permute-start | bytes 49160 | tf_op jit(solution)/shard_map/ppermute | solution.py:576
  49.0 24.2 %collective-permute-start.4 = (bf16[19,64,128]{2,1,0:T(8,128)(2,1)S(1)}, bf16[19,64,128]{2,1,0:T(8,128)(2,1)S(1)}, u32[]{:S(2)}, u32[]{:S(2)}) collective-permute-start(bf16[19,64,128]{2,1,0:T(8,128)(2,1)S(1)} %get-tuple-element.57), channel_id=1, source_target_pairs={{0,6},{2,4},{4,2},{6,0},{9,15},{11,13},{13,11},{15,9},{16,22},{18,... | collective-permute-start | bytes 933896 | tf_op jit(solution)/shard_map/ppermute | solution.py:607
  51.7 21.5 %collective-permute-start.3 = (bf16[19,64,128]{2,1,0:T(8,128)(2,1)S(1)}, bf16[19,64,128]{2,1,0:T(8,128)(2,1)S(1)}, u32[]{:S(2)}, u32[]{:S(2)}) collective-permute-start(bf16[19,64,128]{2,1,0:T(8,128)(2,1)S(1)} %get-tuple-element.56), channel_id=1, source_target_pairs={{0,4},{1,12},{2,6},{3,14},{4,0},{5,8},{6,2},{7,10},{8,5},{9,13},{1... | collective-permute-start | bytes 933896 | tf_op jit(solution)/shard_map/ppermute | solution.py:601
  52.4 20.9 %collective-permute-start.6 = (bf16[19,64,128]{2,1,0:T(8,128)(2,1)S(1)}, bf16[19,64,128]{2,1,0:T(8,128)(2,1)S(1)}, u32[]{:S(2)}, u32[]{:S(2)}) collective-permute-start(bf16[19,64,128]{2,1,0:T(8,128)(2,1)S(1)} %collective-permute-done.5), channel_id=1, source_target_pairs={{0,14},{2,12},{4,10},{6,8},{9,7},{11,5},{13,3},{15,1},{16,30},{18,... | collective-permute-start | bytes 933896 | tf_op jit(solution)/shard_map/ppermute | solution.py:609
  77.9 6.7 %collective-permute-start.12 = (bf16[2,4,64,128]{3,2,1,0:T(8,128)(2,1)S(1)}, bf16[2,4,64,128]{3,2,1,0:T(8,128)(2,1)S(1)}, u32[]{:S(2)}, u32[]{:S(2)}) collective-permute-start(bf16[2,4,64,128]{3,2,1,0:T(8,128)(2,1)S(1)} %get-tuple-element.67), channel_id=1, source_target_pairs={{0,2},{2,4},{4,6},{6,8},{8,10},{10,12},{12,14},{1,3},{3,5},{5,7},{... | collective-permute-start | bytes 393224 | tf_op jit(solution)/shard_map/ppermute | solution.py:468
  79.9 4.7 %collective-permute-start.13 = (bf16[2,4,64,128]{3,2,1,0:T(8,128)(2,1)S(1)}, bf16[2,4,64,128]{3,2,1,0:T(8,128)(2,1)S(1)}, u32[]{:S(2)}, u32[]{:S(2)}) collective-permute-start(bf16[2,4,64,128]{3,2,1,0:T(8,128)(2,1)S(1)} %get-tuple-element.68), channel_id=1, source_target_pairs={{2,0},{4,2},{6,4},{8,6},{10,8},{12,10},{14,12},{3,1},{5,3},{7,5},{... | collective-permute-start | bytes 393224 | tf_op jit(solution)/shard_map/ppermute | solution.py:469
  85.5 6.7 %collective-permute-start.15 = (f32[88,128]{1,0:T(8,128)S(1)}, f32[88,128]{1,0:T(8,128)S(1)}, u32[]{:S(2)}, u32[]{:S(2)}) collective-permute-start(f32[88,128]{1,0:T(8,128)S(1)} %get-tuple-element.78), channel_id=1, source_target_pairs={{0,1},{1,0},{2,3},{3,2},{4,5},{5,4},{6,7},{7,6},{8,9},{9,8},{10,11... | collective-permute-start | bytes 135176 | tf_op jit(solution)/shard_map/ppermute | solution.py:487
  87.5 4.7 %collective-permute-start.16 = (f32[88,128]{1,0:T(8,128)S(1)}, f32[88,128]{1,0:T(8,128)S(1)}, u32[]{:S(2)}, u32[]{:S(2)}) collective-permute-start(f32[88,128]{1,0:T(8,128)S(1)} %get-tuple-element.79), channel_id=1, source_target_pairs={{0,2},{1,3},{2,0},{3,1},{4,6},{5,7},{6,4},{7,5},{8,10},{9,11},{10,... | collective-permute-start | bytes 135176 | tf_op jit(solution)/shard_map/ppermute | solution.py:487
  88.8 3.8 %collective-permute-start.17 = (f32[88,128]{1,0:T(8,128)S(1)}, f32[88,128]{1,0:T(8,128)S(1)}, u32[]{:S(2)}, u32[]{:S(2)}) collective-permute-start(f32[88,128]{1,0:T(8,128)S(1)} %get-tuple-element.80), channel_id=1, source_target_pairs={{0,3},{1,2},{2,1},{3,0},{4,7},{5,6},{6,5},{7,4},{8,11},{9,10},{10,... | collective-permute-start | bytes 135176 | tf_op jit(solution)/shard_map/ppermute | solution.py:487
  90.5 6.2 %collective-permute-start.14 = (bf16[3,64,128]{2,1,0:T(8,128)(2,1)S(1)}, bf16[3,64,128]{2,1,0:T(8,128)(2,1)S(1)}, u32[]{:S(2)}, u32[]{:S(2)}) collective-permute-start(bf16[3,64,128]{2,1,0:T(8,128)(2,1)S(1)} %edges.3), channel_id=1, source_target_pairs={{0,1},{1,0},{2,3},{3,2},{4,5},{5,4},{6,7},{7,6},{8,9},{9,8},{10,11... | collective-permute-start | bytes 147464 | tf_op jit(solution)/shard_map/ppermute | solution.py:437
  92.6 5.8 %collective-permute-start.20 = (f32[88,128]{1,0:T(8,128)S(1)}, f32[88,128]{1,0:T(8,128)S(1)}, u32[]{:S(2)}, u32[]{:S(2)}) collective-permute-start(f32[88,128]{1,0:T(8,128)S(1)} %sum.2.refs_0_), channel_id=1, source_target_pairs={{0,12},{2,14},{4,0},{6,2},{8,4},{10,6},{12,8},{14,10},{1,13},{3,15... | collective-permute-start | bytes 135176 | tf_op jit(solution)/shard_map/ppermute | solution.py:491
  95.3 5.9 %collective-permute-start.19 = (f32[88,128]{1,0:T(8,128)S(1)}, f32[88,128]{1,0:T(8,128)S(1)}, u32[]{:S(2)}, u32[]{:S(2)}) collective-permute-start(f32[88,128]{1,0:T(8,128)S(1)} %sum.2.refs_0_), channel_id=1, source_target_pairs={{0,8},{2,10},{4,12},{6,14},{8,0},{10,2},{12,4},{14,6},{1,9},{3,11}... | collective-permute-start | bytes 135176 | tf_op jit(solution)/shard_map/ppermute | solution.py:491
  95.3 5.9 %collective-permute-start.18 = (f32[88,128]{1,0:T(8,128)S(1)}, f32[88,128]{1,0:T(8,128)S(1)}, u32[]{:S(2)}, u32[]{:S(2)}) collective-permute-start(f32[88,128]{1,0:T(8,128)S(1)} %sum.2.refs_0_), channel_id=1, source_target_pairs={{0,4},{2,6},{4,8},{6,10},{8,12},{10,14},{12,0},{14,2},{1,5},{3,7},... | collective-permute-start | bytes 135176 | tf_op jit(solution)/shard_map/ppermute | solution.py:491
  101.2 8.0 %collective-permute-start.23 = (f32[88,128]{1,0:T(8,128)S(1)}, f32[88,128]{1,0:T(8,128)S(1)}, u32[]{:S(2)}, u32[]{:S(2)}) collective-permute-start(f32[88,128]{1,0:T(8,128)S(1)} %sum.3.rest_0_), channel_id=1, source_target_pairs={{0,3},{1,2},{2,1},{3,0},{4,7},{5,6},{6,5},{7,4},{8,11},{9,10},{10,... | collective-permute-start | bytes 135176 | tf_op jit(solution)/shard_map/ppermute | solution.py:487
  101.3 7.9 %collective-permute-start.22 = (f32[88,128]{1,0:T(8,128)S(1)}, f32[88,128]{1,0:T(8,128)S(1)}, u32[]{:S(2)}, u32[]{:S(2)}) collective-permute-start(f32[88,128]{1,0:T(8,128)S(1)} %sum.3.rest_0_), channel_id=1, source_target_pairs={{0,2},{1,3},{2,0},{3,1},{4,6},{5,7},{6,4},{7,5},{8,10},{9,11},{10,... | collective-permute-start | bytes 135176 | tf_op jit(solution)/shard_map/ppermute | solution.py:487
  102.9 6.3 %collective-permute-start.21 = (f32[88,128]{1,0:T(8,128)S(1)}, f32[88,128]{1,0:T(8,128)S(1)}, u32[]{:S(2)}, u32[]{:S(2)}) collective-permute-start(f32[88,128]{1,0:T(8,128)S(1)} %sum.3.rest_0_), channel_id=1, source_target_pairs={{0,1},{1,0},{2,3},{3,2},{4,5},{5,4},{6,7},{7,6},{8,9},{9,8},{10,11... | collective-permute-start | bytes 135176 | tf_op jit(solution)/shard_map/ppermute | solution.py:487
  (5 other events, 42.8 us)

commit v4 on v3

--- a/solution.py
+++ b/solution.py
@@ -24,7 +24,7 @@
     return pl.CostEstimate(flops=int(us * 1.1e9), transcendentals=0, bytes_accessed=0)
 
 
-def call(body, name, out_shape, args, us, smem=0, scratch=(), aliases=None, mib=4):
+def call(body, name, out_shape, args, us, smem=0, scratch=(), aliases=None, mib=12):
     return pl.pallas_call(
         body,
         out_shape=out_shape,
@@ -63,13 +63,13 @@
         for c in range(n * some, (n + 1) * some):
             body = landed[c].astype(F32)
             for u in range(tiles):
-                at = (u * channels + c) * rows
+                at = (u * channels + c) * (rows + 1)
                 main[at : at + rows, :] = body[:, 128 * u : 128 * (u + 1)]
 
     def turn(i, _):
         for u in range(tiles):
-            at = u * channels * rows + i
-            out[u, i] = main[pl.ds(at, channels, stride=rows), :].astype(BF16)
+            at = u * channels * (rows + 1) + i
+            out[u, i] = main[pl.ds(at, channels, stride=rows + 1), :].astype(BF16)
         return 0
 
     lax.fori_loop(0, rows, turn, 0, unroll=8)
@@ -199,6 +199,7 @@
 def forward_kernel(scal, xs, w, bias, hw, hid, slope, direct, one, two, *, stage):
     rows, channels, _ = hid.shape
     nb = hw.shape[0]
+    high = direct.shape[0] // nb
     rq = scal[0]
     u = (rq >> 1) ^ stage
 
@@ -206,38 +207,41 @@
         return jnp.concatenate([xs[u, i + DIL * a] for a in range(3)], axis=0)
 
     def conv(g, _):
-        for p in range(4):
-            i = g * 8 + 2 * p
+        for p in range(8):
+            i = g * 64 + 8 * p
             pre = jnp.dot(
-                w[...], pairs_of([window(i), window(i + 1)]), preferred_element_type=F32
+                w[...],
+                pairs_of([window(i + e) for e in range(8)]),
+                preferred_element_type=F32,
             )
             pre = pre + bias[...]
             grown = jnp.exp(jnp.minimum(pre, 0.0))
             h = jnp.where(pre > 0, pre, grown - 1.0).astype(BF16)
             s = jnp.where(pre > 0, 1.0, grown).astype(BF16)
-            for e in range(2):
+            for e in range(8):
                 hid[i + e] = h[:, 128 * e : 128 * (e + 1)]
                 slope[i + e] = s[:, 128 * e : 128 * (e + 1)]
         return 0
 
-    lax.fori_loop(0, rows // 8, conv, 0)
+    lax.fori_loop(0, rows // 64, conv, 0)
 
     def head(g, _):
-        for p in range(4):
-            i = g * 8 + 2 * p
-            d = jnp.dot(hw[...], pairs_of([hid[i], hid[i + 1]]), preferred_element_type=F32)
-            for e in range(2):
-                direct[pl.ds(i + e, nb, stride=rows), :] = d[:, 128 * e : 128 * (e + 1)]
+        for p in range(8):
+            i = g * 64 + 8 * p
+            d = jnp.dot(hw[...], pairs_of([hid[i + e] for e in range(8)]), preferred_element_type=F32)
+            for e in range(8):
+                direct[pl.ds(i + e, nb, stride=high), :] = d[:, 128 * e : 128 * (e + 1)]
         return 0
 
-    lax.fori_loop(0, rows // 8, head, 0)
+    lax.fori_loop(0, rows // 64, head, 0)
 
     flip = (rq & 1) == 1
     for m in range(one.shape[0]):
-        turned = direct[2 * rows * m : 2 * rows * (m + 1), :].T.astype(BF16)
-        low, high = turned[:rows].astype(F32), turned[rows:].astype(F32)
-        one[m] = jnp.where(flip, high, low).astype(BF16)
-        two[m] = jnp.where(flip, low, high).astype(BF16)
+        both = [direct[high * k : high * k + rows, :] for k in (2 * m, 2 * m + 1)]
+        turned = jnp.concatenate(both, axis=0).T.astype(BF16)
+        upper, lower = turned[:rows].astype(F32), turned[rows:].astype(F32)
+        one[m] = jnp.where(flip, lower, upper).astype(BF16)
+        two[m] = jnp.where(flip, upper, lower).astype(BF16)
 
 
 def middle_kernel(scal, hb, direct, hid, slope, hwt, *rest, stage, counts, ncol, first, last, nbins):
@@ -246,7 +250,8 @@
     if not first:
         before, rest = rest[1], rest[3:]
     dpre, small, *ends, dl, hacc, bacc, cacc, lacc = rest
-    nb, rows, _ = direct.shape
+    nb, high, _ = direct.shape
+    rows = hid.shape[0]
     band = rows // ncol
     channels = hwt.shape[0]
     rq, extent = scal[0], scal[3]
@@ -255,7 +260,7 @@
     crossed = scal[5] == 1
     for ref in (hacc, bacc, cacc, lacc):
         ref[...] = jnp.zeros_like(ref)
-    dl[nbins * rows :, :] = jnp.zeros((dl.shape[0] - nbins * rows, 128), F32)
+    dl[nbins * high :, :] = jnp.zeros((dl.shape[0] - nbins * high, 128), F32)
 
     lane = lax.broadcasted_iota(jnp.int32, (8, 128), 1)
     low = lane < 64
@@ -303,31 +308,35 @@
         for k in range(nbins):
             d = (powers[k] * inverse - jnp.where(wanted == k, 1.0, 0.0)) * scale
             d = d.astype(BF16).astype(F32)
-            dl[pl.ds(k * rows + base, 8), :] = d
+            dl[pl.ds(k * high + base, 8), :] = d
             bacc[8 * k : 8 * k + 8, :] += d
         return 0
 
-    lax.fori_loop(0, rows // 8, softmax, 0)
+    lax.fori_loop(0, rows // 8, softmax, 0, unroll=2)
 
     def back(g, _):
-        for p in range(4):
-            i = g * 8 + 2 * p
+        heads, shifts = [], []
+        for p in range(8):
+            i = g * 64 + 8 * p
             d = pairs_of(
-                [dl[pl.ds(i + e, nb, stride=rows), :].astype(BF16) for e in range(2)]
+                [dl[pl.ds(i + e, nb, stride=high), :].astype(BF16) for e in range(8)]
             )
-            h = pairs_of([hid[i], hid[i + 1]])
-            s = pairs_of([slope[i], slope[i + 1]])
+            h = pairs_of([hid[i + e] for e in range(8)])
+            s = pairs_of([slope[i + e] for e in range(8)])
             v = jnp.dot(hwt[...], d, preferred_element_type=F32) * s.astype(F32)
             v = v.astype(BF16)
-            dpre[u, i] = v[:, :128]
-            dpre[u, i + 1] = v[:, 128:]
-            cacc[...] += v[:, :128].astype(F32) + v[:, 128:].astype(F32)
-            hacc[0:nb, 0:channels] += lax.dot_general(
-                d, h, (((1,), (1,)), ((), ())), preferred_element_type=F32
-            )
+            for e in range(8):
+                dpre[u, i + e] = v[:, 128 * e : 128 * (e + 1)]
+                shifts.append(v[:, 128 * e : 128 * (e + 1)].astype(F32))
+            heads.append((d, h))
+        cacc[...] += functools.reduce(lambda a, b: a + b, shifts)
+        hacc[0:nb, 0:channels] += lax.dot_general(
+            pairs_of([d for d, _ in heads]), pairs_of([h for _, h in heads]),
+            (((1,), (1,)), ((), ())), preferred_element_type=F32,
+        )
         return 0
 
-    lax.fori_loop(0, rows // 8, back, 0)
+    lax.fori_loop(0, rows // 64, back, 0)
 
     spot = lax.broadcasted_iota(jnp.int32, small.shape, 1)
     sums = jnp.sum(bacc[...].reshape(nb, 8, 128), axis=1)
@@ -368,8 +377,8 @@
 
     def body(g, acc):
         left, right = [], []
-        for ii in range(8):
-            i = g * 8 + ii
+        for ii in range(3 * 24):
+            i = g * 72 + ii
             left.append(
                 jnp.concatenate([padded[i + 8 - DIL * a] for a in range(3)], axis=0)
             )
@@ -381,7 +390,7 @@
 
     acc = outs[-1] if len(outs) == 1 else outs[-2]
     acc[...] = jnp.zeros_like(acc) if first else before[...]
-    lax.fori_loop(0, rows // 8 + 1, lambda g, _: body(g, acc), None)
+    lax.fori_loop(0, (rows + 8) // 72, lambda g, _: body(g, acc), None)
     if len(outs) == 1:
         return
     out, outs = outs[-1], outs[:-2]
@@ -397,10 +406,10 @@
 
 def backward_kernel(ds, w, out, turned):
     step = pl.program_id(0)
-    channels, _, width = out.shape
+    channels, some, width = out.shape
     tiles = width // 128
-    for ii in range(8):
-        i = step * 8 + ii
+    for ii in range(some):
+        i = step * some + ii
         window = pairs_of(
             [
                 jnp.concatenate([ds[u, i + DIL * a] for a in range(3)], axis=0)
@@ -409,13 +418,13 @@
         )
         v = jnp.dot(w[...], window, preferred_element_type=F32)
         for u in range(tiles):
-            turned[pl.ds(u * channels * 8 + ii, channels, stride=8), :] = v[
+            turned[pl.ds(u * channels * (some + 8) + ii, channels, stride=some + 8), :] = v[
                 :, 128 * u : 128 * (u + 1)
             ]
     for u in range(tiles):
-        at = 8 * channels * u
-        block = turned[at : at + 8 * channels, :].reshape(channels, 8, 128)
-        out[:, :, 128 * u : 128 * (u + 1)] = block.astype(BF16)
+        at = (some + 8) * channels * u
+        block = turned[at : at + (some + 8) * channels, :].reshape(channels, some + 8, 128)
+        out[:, :, 128 * u : 128 * (u + 1)] = block[:, :some].astype(BF16)
 
 
 def side_columns(field, above, below, scal):
@@ -553,7 +562,7 @@
         out_shape=[shape(field), shape(strip), shape(strip)],
         scratch_shapes=[
             pltpu.VMEM(x.shape, BF16),
-            pltpu.VMEM((tiles * channels * rows, 128), F32),
+            pltpu.VMEM((tiles * channels * (rows + 1), 128), F32),
             pltpu.SemaphoreType.DMA((8,)),
         ],
         compiler_params=grant(8),
@@ -584,7 +593,7 @@
         hid, slope, direct, *sends = call(
             functools.partial(forward_kernel, stage=stage),
             "forward",
-            [shape(field[1:]), shape(field[1:]), shape((nb * rows, 128), F32), block, block],
+            [shape(field[1:]), shape(field[1:]), shape((nb * (rows + 8), 128), F32), block, block],
             (scal, xs, w_fwd, bias, hw),
             us=6,
             smem=1,
@@ -616,7 +625,7 @@
         args = (
             scal,
             head_bias,
-            direct.reshape(nb, rows, 128),
+            direct.reshape(nb, rows + 8, 128),
             hid,
             slope,
             hwt,
@@ -635,7 +644,7 @@
             us=5,
             smem=2,
             scratch=[
-                pltpu.VMEM((nb * rows, 128), F32),
+                pltpu.VMEM((nb * (rows + 8), 128), F32),
                 pltpu.VMEM((channels, 128), F32),
                 pltpu.VMEM((nb * 8, 128), F32),
                 pltpu.VMEM((channels, 128), F32),
@@ -651,7 +660,7 @@
             [pieces] * count if last else shape(square, F32),
             (scal, xs, dpre, small) + (() if first else (taps,)),
             us=2.5,
-            mib=8,
+            mib=12,
             smem=1,
             scratch=[pltpu.VMEM(square, F32), pltpu.VMEM((total, 128), F32)] * last
             + [pltpu.VMEM((rows + 16, channels, 128), BF16)],
@@ -666,11 +675,11 @@
 
     pair_gradient = pl.pallas_call(
         backward_kernel,
-        grid=(rows // 8,),
+        grid=(rows // 16,),
         in_specs=[VM, VM],
-        out_specs=pl.BlockSpec((channels, 8, width), lambda g: (0, g, 0)),
+        out_specs=pl.BlockSpec((channels, 16, width), lambda g: (0, g, 0)),
         out_shape=shape((channels, rows, width)),
-        scratch_shapes=[pltpu.VMEM((tiles * channels * 8, 128), F32)],
+        scratch_shapes=[pltpu.VMEM((tiles * channels * 24, 128), F32)],
         compiler_params=grant(8),
         cost_estimate=cost(6),
         name="backward",

time: 111 us -> 103 us (0.928)
  Pallas kernels: 49.3 us -> 33 us
  waiting for transfers between devices: 23.1 us -> 31.1 us
    pallas_call x15, Pallas kernels: 36.6 us -> 24.1 us  [call(): pl.pallas_call(body, out_shape=out_shape, in_specs=[SM] * smem + [VM] * (...]
    ppermute x2, waiting for transfers between devices: 3.59 us -> 8.58 us  [per_device(): relayed = lax.ppermute(sends[e], ROWS, over)]
    ppermute x2, waiting for transfers between devices: 11.5 us -> 14.8 us  [per_device(): got.append([lax.ppermute(sends[e], ROWS, perm)])]
    pallas_call x1, Pallas kernels: 5.54 us -> 2.43 us  [per_device(): pl.pallas_call(prep_kernel, in_specs=[SM, pl.BlockSpec(memory_space=pltpu...]
    ppermute x6, starting transfers between devices: 5.57 us -> 7.57 us  [near(): return lax.ppermute(v, ROWS, perm)]
    ppermute x1, starting transfers between devices: 2.05 us -> 0.07 us  [per_device(): lax.ppermute(mine[d], 'col', [(i, (i + d) % ncol) for i in range(ncol)])]
  transfers between devices with their start and end apart: 24 -> 24, of which waited for: 6 -> 8; matrix products, arithmetic and copies ran while one was open for 0% -> 0% of each run, Pallas kernels for 26% -> 20%
where the time goes in v4:
time: 103 us; the launch traced here: 102 us
  starting transfers between devices  36.3 us (35%)
  Pallas kernels  33 us (32%)
  waiting for transfers between devices  31.1 us (30%)
  between operations  1.63 us (2%)
    pallas_call x15, Pallas kernels, call(): pl.pallas_call(body, out_shape=out_shape, in_specs=[SM] * smem + [VM] * (...  24.1 us
    ppermute x2, waiting for transfers between devices, per_device(): got.append([lax.ppermute(sends[e], ROWS, perm)])  14.8 us
    ppermute x2, waiting for transfers between devices, per_device(): relayed = lax.ppermute(sends[e], ROWS, over)  8.58 us
    ppermute x6, starting transfers between devices, near(): return lax.ppermute(v, ROWS, perm)  7.57 us
    pallas_call x1, Pallas kernels, per_device(): pl.pallas_call(backward_kernel, grid=(rows // 16,), in_specs=[VM, VM], ou...  5.1 us
    ppermute x2, starting transfers between devices, row_halo(): above = lax.ppermute(tail, 'row', [(i, i + 1) for i in range(count - 1)])  5.04 us
    ppermute x2, starting transfers between devices, with_border(): got = [lax.ppermute(sides[0], 'col', [(0, 1), (1, 0)])]  4.69 us
    ppermute x2, starting transfers between devices, per_device(): same = lax.ppermute(sends[e], ROWS, near)  4.65 us
  transfers between devices with their start and end apart: 24, of which 8 were waited for; matrix products, arithmetic and copies ran while one was open for 0% of the time, Pallas kernels for 20%

profile of v4, /device:TPU:0, one launch (start us, length us, event | category | flops | bytes accessed | tf_op | source)
XLA Modules:
  0.0 102.2 jit_solution(14870445678204832890)
XLA Ops:
  1.4 2.4 %prep.1 = (bf16[2,64,64,128]{3,2,1,0:T(8,128)(2,1)S(1)}, bf16[2,4,64,128]{3,2,1,0:T(8,128)(2,1)S(1)}, bf16[2,4,64,128]{3,2,1,0:T(8,128)(2,1)S(1)}) custom-call(s32[7]{0:T(128)S(1)} %stack.31._.scal, bf16[64,64,256]{2,1,0:T(8,128)(2,1)} %x.1), custom_call_target="tpu_custom_call" | custom-call | flops 4400000000 | tf_op jit(solution)/shard_map/prep/pallas_call | solution.py:558
  5.1 3.0 %collective-permute-start = (bf16[2,4,64,128]{3,2,1,0:T(8,128)(2,1)S(1)}, bf16[2,4,64,128]{3,2,1,0:T(8,128)(2,1)S(1)}, u32[]{:S(2)}, u32[]{:S(2)}) collective-permute-start(bf16[2,4,64,128]{3,2,1,0:T(8,128)(2,1)S(1)} %get-tuple-element.46._), channel_id=1, source_target_pairs={{0,2},{2,4},{4,6},{6,8},{8,10},{10,12},{12,14},{1,3},{3,5},{5,7},{... | collective-permute-start | bytes 393224 | tf_op jit(solution)/shard_map/ppermute | solution.py:477
  8.2 1.7 %inner.2.rest_1_ = bf16[2,72,192,128]{3,2,1,0:T(8,128)(2,1)S(1)} custom-call(bf16[2,64,64,128]{3,2,1,0:T(8,128)(2,1)S(1)} %get-tuple-element.48.field), custom_call_target="tpu_custom_call" | custom-call | flops 3300000000 | tf_op jit(solution)/shard_map/inner/pallas_call | solution.py:28
  10.9 3.0 %collective-permute-start.2 = (bf16[3,64,128]{2,1,0:T(8,128)(2,1)S(1)}, bf16[3,64,128]{2,1,0:T(8,128)(2,1)S(1)}, u32[]{:S(2)}, u32[]{:S(2)}) collective-permute-start(bf16[3,64,128]{2,1,0:T(8,128)(2,1)S(1)} %edges.2), channel_id=1, source_target_pairs={{0,1},{1,0},{2,3},{3,2},{4,5},{5,4},{6,7},{7,6},{8,9},{9,8},{10,11... | collective-permute-start | bytes 147464 | tf_op jit(solution)/shard_map/ppermute | solution.py:446
  16.0 1.7 %border.2.xs = bf16[2,72,192,128]{3,2,1,0:T(8,128)(2,1)S(1)} custom-call(s32[7]{0:T(128)S(1)} %stack.31._.scal, bf16[2,4,64,128]{3,2,1,0:T(8,128)(2,1)S(1)} %collective-permute-done.above, bf16[2,4,64,128]{3,2,1,0:T(8,128)(2,1)S(1)} %collective-permute-done.1.below, ...), custom_call_target="tpu_custom_call", output_to_operand_aliasing={{}: (4, {})} | custom-call | flops 1650000000 | tf_op jit(solution)/shard_map/border/pallas_call | solution.py:28
  17.6 3.0 %forward.3 = (bf16[64,64,128]{2,1,0:T(8,128)(2,1)S(1)}, bf16[64,64,128]{2,1,0:T(8,128)(2,1)S(1)}, f32[2880,128]{1,0:T(8,128)S(1)}, bf16[19,64,128]{2,1,0:T(8,128)(2,1)S(1)}, bf16[19,64,128]{2,1,0:T(8,128)(2,1)S(1)}) custom-call(s32[7]{0:T(128)S(1)} %stack.31._.scal, bf16[2,72,192,128]{3,2,1,0:T(8,128)(2,1)S(1)} %border.2.xs, ...), custom_call_target="tpu_custom_call" | custom-call | flops 6600000000 | tf_op jit(solution)/shard_map/forward/pallas_call | solution.py:28
  22.7 3.0 %forward.2 = (bf16[64,64,128]{2,1,0:T(8,128)(2,1)S(1)}, bf16[64,64,128]{2,1,0:T(8,128)(2,1)S(1)}, f32[2880,128]{1,0:T(8,128)S(1)}, bf16[19,64,128]{2,1,0:T(8,128)(2,1)S(1)}, bf16[19,64,128]{2,1,0:T(8,128)(2,1)S(1)}) custom-call(s32[7]{0:T(128)S(1)} %stack.31._.scal, bf16[2,72,192,128]{3,2,1,0:T(8,128)(2,1)S(1)} %border.2.xs, ...), custom_call_target="tpu_custom_call" | custom-call | flops 6600000000 | tf_op jit(solution)/shard_map/forward/pallas_call | solution.py:28
  27.0 2.6 %collective-permute-start.9 = (bf16[19,64,128]{2,1,0:T(8,128)(2,1)S(1)}, bf16[19,64,128]{2,1,0:T(8,128)(2,1)S(1)}, u32[]{:S(2)}, u32[]{:S(2)}) collective-permute-start(bf16[19,64,128]{2,1,0:T(8,128)(2,1)S(1)} %get-tuple-element.64), channel_id=1, source_target_pairs={{0,2},{2,0},{4,6},{6,4},{9,11},{11,9},{13,15},{15,13},{16,18},{18,... | collective-permute-start | bytes 933896 | tf_op jit(solution)/shard_map/ppermute | solution.py:616
  29.6 8.6 %collective-permute-done.10 = bf16[19,64,128]{2,1,0:T(8,128)(2,1)S(1)} collective-permute-done((bf16[19,64,128]{2,1,0:T(8,128)(2,1)S(1)}, bf16[19,64,128]{2,1,0:T(8,128)(2,1)S(1)}, u32[]{:S(2)}, u32[]{:S(2)}) %collective-permute-start.10) | collective-permute-done | bytes 311328 | tf_op jit(solution)/shard_map/ppermute | solution.py:617
  39.5 3.7 %collective-permute-done.7.rest_4_ = bf16[32,256]{1,0:T(8,128)(2,1)S(1)} collective-permute-done((bf16[32,256]{1,0:T(8,128)(2,1)S(1)}, bf16[32,256]{1,0:T(8,128)(2,1)S(1)}, u32[]{:S(2)}, u32[]{:S(2)}) %collective-permute-start.7) | collective-permute-done | bytes 16416 | tf_op jit(solution)/shard_map/ppermute | solution.py:585
  43.3 2.0 %collective-permute-start.4 = (bf16[19,64,128]{2,1,0:T(8,128)(2,1)S(1)}, bf16[19,64,128]{2,1,0:T(8,128)(2,1)S(1)}, u32[]{:S(2)}, u32[]{:S(2)}) collective-permute-start(bf16[19,64,128]{2,1,0:T(8,128)(2,1)S(1)} %get-tuple-element.57), channel_id=1, source_target_pairs={{0,6},{2,4},{4,2},{6,0},{9,15},{11,13},{13,11},{15,9},{16,22},{18,... | collective-permute-start | bytes 933896 | tf_op jit(solution)/shard_map/ppermute | solution.py:616
  45.3 1.8 %collective-permute-start.3 = (bf16[19,64,128]{2,1,0:T(8,128)(2,1)S(1)}, bf16[19,64,128]{2,1,0:T(8,128)(2,1)S(1)}, u32[]{:S(2)}, u32[]{:S(2)}) collective-permute-start(bf16[19,64,128]{2,1,0:T(8,128)(2,1)S(1)} %get-tuple-element.56), channel_id=1, source_target_pairs={{0,4},{1,12},{2,6},{3,14},{4,0},{5,8},{6,2},{7,10},{8,5},{9,13},{1... | collective-permute-start | bytes 933896 | tf_op jit(solution)/shard_map/ppermute | solution.py:610
  48.4 2.6 %middle.2 = (bf16[2,64,64,128]{3,2,1,0:T(8,128)(2,1)S(1)}, f32[64,128]{1,0:T(8,128)S(1)}) custom-call(s32[7]{0:T(128)S(1)} %stack.31._.scal, f32[37]{0:T(128)S(1)} %copy-done.4, f32[40,72,128]{2,1,0:T(8,128)S(1)} %bitcast.14, bf16[64,64,128]{2,1,0:T(8,128)(2,1)S(1)} %get-tuple-element.61.hid, bf16[64,64,128]{2,1,0:T(8,128)(2,1)S(1)} %get-tuple-element.62.slope, ...), custom_call_target="tpu_custom_call" | custom-call | flops 5500000256 | tf_op jit(solution)/shard_map/middle/pallas_call | solution.py:28
  52.7 14.8 %collective-permute-done.3.rest_0_ = bf16[19,64,128]{2,1,0:T(8,128)(2,1)S(1)} collective-permute-done((bf16[19,64,128]{2,1,0:T(8,128)(2,1)S(1)}, bf16[19,64,128]{2,1,0:T(8,128)(2,1)S(1)}, u32[]{:S(2)}, u32[]{:S(2)}) %collective-permute-start.3) | collective-permute-done | bytes 311328 | tf_op jit(solution)/shard_map/ppermute | solution.py:610
  67.5 2.7 %middle.3 = (bf16[2,64,64,128]{3,2,1,0:T(8,128)(2,1)S(1)}, f32[64,128]{1,0:T(8,128)S(1)}, bf16[2,4,64,128]{3,2,1,0:T(8,128)(2,1)S(1)}, bf16[2,4,64,128]{3,2,1,0:T(8,128)(2,1)S(1)}) custom-call(s32[7]{0:T(128)S(1)} %stack.31._.scal, f32[37]{0:T(128)S(1)} %copy-done.4, f32[40,72,128]{2,1,0:T(8,128)S(1)} %bitcast.13, ...), custom_call_target="tpu_custom_call", output_to_operand_aliasing={{0}: (11, {})} | custom-call | flops 5500000256 | tf_op jit(solution)/shard_map/middle/pallas_call | solution.py:28
  70.1 2.0 %collective-permute-start.12 = (bf16[2,4,64,128]{3,2,1,0:T(8,128)(2,1)S(1)}, bf16[2,4,64,128]{3,2,1,0:T(8,128)(2,1)S(1)}, u32[]{:S(2)}, u32[]{:S(2)}) collective-permute-start(bf16[2,4,64,128]{3,2,1,0:T(8,128)(2,1)S(1)} %get-tuple-element.67), channel_id=1, source_target_pairs={{0,2},{2,4},{4,6},{6,8},{8,10},{10,12},{12,14},{1,3},{3,5},{5,7},{... | collective-permute-start | bytes 393224 | tf_op jit(solution)/shard_map/ppermute | solution.py:477
  73.5 1.8 %weights.3 = (f32[88,128]{1,0:T(8,128)S(1)}, f32[88,128]{1,0:T(8,128)S(1)}, f32[88,128]{1,0:T(8,128)S(1)}, f32[88,128]{1,0:T(8,128)S(1)}) custom-call(s32[7]{0:T(128)S(1)} %stack.31._.scal, bf16[2,72,192,128]{3,2,1,0:T(8,128)(2,1)S(1)} %border.2.xs, bf16[2,64,64,128]{3,2,1,0:T(8,128)(2,1)S(1)} %get-tuple-element.69.field.dpre, ...), custom_call_target="tpu_custom_call" | custom-call | flops 2750000128 | tf_op jit(solution)/shard_map/weights/pallas_call | solution.py:28
  76.3 2.6 %collective-permute-start.15 = (f32[88,128]{1,0:T(8,128)S(1)}, f32[88,128]{1,0:T(8,128)S(1)}, u32[]{:S(2)}, u32[]{:S(2)}) collective-permute-start(f32[88,128]{1,0:T(8,128)S(1)} %get-tuple-element.78), channel_id=1, source_target_pairs={{0,1},{1,0},{2,3},{3,2},{4,5},{5,4},{6,7},{7,6},{8,9},{9,8},{10,11... | collective-permute-start | bytes 135176 | tf_op jit(solution)/shard_map/ppermute | solution.py:496
  78.9 2.8 %collective-permute-start.16 = (f32[88,128]{1,0:T(8,128)S(1)}, f32[88,128]{1,0:T(8,128)S(1)}, u32[]{:S(2)}, u32[]{:S(2)}) collective-permute-start(f32[88,128]{1,0:T(8,128)S(1)} %get-tuple-element.79), channel_id=1, source_target_pairs={{0,2},{1,3},{2,0},{3,1},{4,6},{5,7},{6,4},{7,5},{8,10},{9,11},{10,... | collective-permute-start | bytes 135176 | tf_op jit(solution)/shard_map/ppermute | solution.py:496
  85.4 1.8 %collective-permute-start.20 = (f32[88,128]{1,0:T(8,128)S(1)}, f32[88,128]{1,0:T(8,128)S(1)}, u32[]{:S(2)}, u32[]{:S(2)}) collective-permute-start(f32[88,128]{1,0:T(8,128)S(1)} %sum.2.refs_0_), channel_id=1, source_target_pairs={{0,12},{2,14},{4,0},{6,2},{8,4},{10,6},{12,8},{14,10},{1,13},{3,15... | collective-permute-start | bytes 135176 | tf_op jit(solution)/shard_map/ppermute | solution.py:500
  87.6 1.9 %collective-permute-start.18 = (f32[88,128]{1,0:T(8,128)S(1)}, f32[88,128]{1,0:T(8,128)S(1)}, u32[]{:S(2)}, u32[]{:S(2)}) collective-permute-start(f32[88,128]{1,0:T(8,128)S(1)} %sum.2.refs_0_), channel_id=1, source_target_pairs={{0,4},{2,6},{4,8},{6,10},{8,12},{10,14},{12,0},{14,2},{1,5},{3,7},... | collective-permute-start | bytes 135176 | tf_op jit(solution)/shard_map/ppermute | solution.py:500
  89.5 1.7 %border.3.ds = bf16[2,72,192,128]{3,2,1,0:T(8,128)(2,1)S(1)} custom-call(s32[7]{0:T(128)S(1)} %stack.31._.scal, bf16[2,4,64,128]{3,2,1,0:T(8,128)(2,1)S(1)} %collective-permute-done.12.above, bf16[2,4,64,128]{3,2,1,0:T(8,128)(2,1)S(1)} %collective-permute-done.13.below, ...), custom_call_target="tpu_custom_call", output_to_operand_aliasing={{}: (4, {})} | custom-call | flops 1650000000 | tf_op jit(solution)/shard_map/border/pallas_call | solution.py:28
  93.5 1.8 %collective-permute-start.22 = (f32[88,128]{1,0:T(8,128)S(1)}, f32[88,128]{1,0:T(8,128)S(1)}, u32[]{:S(2)}, u32[]{:S(2)}) collective-permute-start(f32[88,128]{1,0:T(8,128)S(1)} %sum.3.rest_0_), channel_id=1, source_target_pairs={{0,2},{1,3},{2,0},{3,1},{4,6},{5,7},{6,4},{7,5},{8,10},{9,11},{10,... | collective-permute-start | bytes 135176 | tf_op jit(solution)/shard_map/ppermute | solution.py:496
  95.7 5.1 %backward.1 = bf16[64,64,256]{2,1,0:T(8,128)(2,1)} custom-call(bf16[2,72,192,128]{3,2,1,0:T(8,128)(2,1)S(1)} %border.3.ds, bf16[64,576]{1,0:T(8,128)(2,1)S(1)} %get-tuple-element.76.w), custom_call_target="tpu_custom_call" | custom-call | flops 6600000000 | tf_op jit(solution)/shard_map/backward/pallas_call | solution.py:676
  (53 shorter events, 22.5 us)
Async XLA Ops:
  3.8 6.1 %collective-permute-start.1 = (bf16[2,4,64,128]{3,2,1,0:T(8,128)(2,1)S(1)}, bf16[2,4,64,128]{3,2,1,0:T(8,128)(2,1)S(1)}, u32[]{:S(2)}, u32[]{:S(2)}) collective-permute-start(bf16[2,4,64,128]{3,2,1,0:T(8,128)(2,1)S(1)} %get-tuple-element.47), channel_id=1, source_target_pairs={{2,0},{4,2},{6,4},{8,6},{10,8},{12,10},{14,12},{3,1},{5,3},{7,5},{... | collective-permute-start | bytes 393224 | tf_op jit(solution)/shard_map/ppermute | solution.py:478
  5.1 4.8 %collective-permute-start = (bf16[2,4,64,128]{3,2,1,0:T(8,128)(2,1)S(1)}, bf16[2,4,64,128]{3,2,1,0:T(8,128)(2,1)S(1)}, u32[]{:S(2)}, u32[]{:S(2)}) collective-permute-start(bf16[2,4,64,128]{3,2,1,0:T(8,128)(2,1)S(1)} %get-tuple-element.46._), channel_id=1, source_target_pairs={{0,2},{2,4},{4,6},{6,8},{8,10},{10,12},{12,14},{1,3},{3,5},{5,7},{... | collective-permute-start | bytes 393224 | tf_op jit(solution)/shard_map/ppermute | solution.py:477
  10.9 5.1 %collective-permute-start.2 = (bf16[3,64,128]{2,1,0:T(8,128)(2,1)S(1)}, bf16[3,64,128]{2,1,0:T(8,128)(2,1)S(1)}, u32[]{:S(2)}, u32[]{:S(2)}) collective-permute-start(bf16[3,64,128]{2,1,0:T(8,128)(2,1)S(1)} %edges.2), channel_id=1, source_target_pairs={{0,1},{1,0},{2,3},{3,2},{4,5},{5,4},{6,7},{7,6},{8,9},{9,8},{10,11... | collective-permute-start | bytes 147464 | tf_op jit(solution)/shard_map/ppermute | solution.py:446
  20.7 24.7 %collective-permute-start.8 = (bf16[19,64,128]{2,1,0:T(8,128)(2,1)S(1)}, bf16[19,64,128]{2,1,0:T(8,128)(2,1)S(1)}, u32[]{:S(2)}, u32[]{:S(2)}) collective-permute-start(bf16[19,64,128]{2,1,0:T(8,128)(2,1)S(1)} %get-tuple-element.63), channel_id=1, source_target_pairs={{0,0},{1,8},{2,2},{3,10},{4,4},{5,12},{6,6},{7,14},{8,1},{9,9},{10... | collective-permute-start | bytes 933896 | tf_op jit(solution)/shard_map/ppermute | solution.py:610
  21.4 16.8 %collective-permute-start.10 = (bf16[19,64,128]{2,1,0:T(8,128)(2,1)S(1)}, bf16[19,64,128]{2,1,0:T(8,128)(2,1)S(1)}, u32[]{:S(2)}, u32[]{:S(2)}) collective-permute-start(bf16[19,64,128]{2,1,0:T(8,128)(2,1)S(1)} %get-tuple-element.64), channel_id=1, source_target_pairs={{1,0},{3,2},{5,4},{7,6},{8,9},{10,11},{12,13},{14,15},{17,16},{19,... | collective-permute-start | bytes 933896 | tf_op jit(solution)/shard_map/ppermute | solution.py:617
  25.7 21.4 %collective-permute-start.5 = (bf16[19,64,128]{2,1,0:T(8,128)(2,1)S(1)}, bf16[19,64,128]{2,1,0:T(8,128)(2,1)S(1)}, u32[]{:S(2)}, u32[]{:S(2)}) collective-permute-start(bf16[19,64,128]{2,1,0:T(8,128)(2,1)S(1)} %get-tuple-element.57), channel_id=1, source_target_pairs={{1,0},{3,2},{5,4},{7,6},{8,9},{10,11},{12,13},{14,15},{17,16},{19,... | collective-permute-start | bytes 933896 | tf_op jit(solution)/shard_map/ppermute | solution.py:617
  27.0 21.4 %collective-permute-start.9 = (bf16[19,64,128]{2,1,0:T(8,128)(2,1)S(1)}, bf16[19,64,128]{2,1,0:T(8,128)(2,1)S(1)}, u32[]{:S(2)}, u32[]{:S(2)}) collective-permute-start(bf16[19,64,128]{2,1,0:T(8,128)(2,1)S(1)} %get-tuple-element.64), channel_id=1, source_target_pairs={{0,2},{2,0},{4,6},{6,4},{9,11},{11,9},{13,15},{15,13},{16,18},{18,... | collective-permute-start | bytes 933896 | tf_op jit(solution)/shard_map/ppermute | solution.py:616
  38.2 10.2 %collective-permute-start.11 = (bf16[19,64,128]{2,1,0:T(8,128)(2,1)S(1)}, bf16[19,64,128]{2,1,0:T(8,128)(2,1)S(1)}, u32[]{:S(2)}, u32[]{:S(2)}) collective-permute-start(bf16[19,64,128]{2,1,0:T(8,128)(2,1)S(1)} %collective-permute-done.10), channel_id=1, source_target_pairs={{0,10},{2,8},{4,14},{6,12},{9,3},{11,1},{13,7},{15,5},{16,26},{18,... | collective-permute-start | bytes 933896 | tf_op jit(solution)/shard_map/ppermute | solution.py:618
  39.5 3.8 %collective-permute-start.7 = (bf16[32,256]{1,0:T(8,128)(2,1)S(1)}, bf16[32,256]{1,0:T(8,128)(2,1)S(1)}, u32[]{:S(2)}, u32[]{:S(2)}) collective-permute-start(bf16[32,256]{1,0:T(8,128)(2,1)S(1)} %get-tuple-element.59), channel_id=1, source_target_pairs={{0,1},{1,0},{2,3},{3,2},{4,5},{5,4},{6,7},{7,6},{8,9},{9,8},{10,11... | collective-permute-start | bytes 49160 | tf_op jit(solution)/shard_map/ppermute | solution.py:585
  43.3 24.2 %collective-permute-start.4 = (bf16[19,64,128]{2,1,0:T(8,128)(2,1)S(1)}, bf16[19,64,128]{2,1,0:T(8,128)(2,1)S(1)}, u32[]{:S(2)}, u32[]{:S(2)}) collective-permute-start(bf16[19,64,128]{2,1,0:T(8,128)(2,1)S(1)} %get-tuple-element.57), channel_id=1, source_target_pairs={{0,6},{2,4},{4,2},{6,0},{9,15},{11,13},{13,11},{15,9},{16,22},{18,... | collective-permute-start | bytes 933896 | tf_op jit(solution)/shard_map/ppermute | solution.py:616
  45.3 22.1 %collective-permute-start.3 = (bf16[19,64,128]{2,1,0:T(8,128)(2,1)S(1)}, bf16[19,64,128]{2,1,0:T(8,128)(2,1)S(1)}, u32[]{:S(2)}, u32[]{:S(2)}) collective-permute-start(bf16[19,64,128]{2,1,0:T(8,128)(2,1)S(1)} %get-tuple-element.56), channel_id=1, source_target_pairs={{0,4},{1,12},{2,6},{3,14},{4,0},{5,8},{6,2},{7,10},{8,5},{9,13},{1... | collective-permute-start | bytes 933896 | tf_op jit(solution)/shard_map/ppermute | solution.py:610
  47.1 20.4 %collective-permute-start.6 = (bf16[19,64,128]{2,1,0:T(8,128)(2,1)S(1)}, bf16[19,64,128]{2,1,0:T(8,128)(2,1)S(1)}, u32[]{:S(2)}, u32[]{:S(2)}) collective-permute-start(bf16[19,64,128]{2,1,0:T(8,128)(2,1)S(1)} %collective-permute-done.5), channel_id=1, source_target_pairs={{0,14},{2,12},{4,10},{6,8},{9,7},{11,5},{13,3},{15,1},{16,30},{18,... | collective-permute-start | bytes 933896 | tf_op jit(solution)/shard_map/ppermute | solution.py:618
  70.1 5.1 %collective-permute-start.12 = (bf16[2,4,64,128]{3,2,1,0:T(8,128)(2,1)S(1)}, bf16[2,4,64,128]{3,2,1,0:T(8,128)(2,1)S(1)}, u32[]{:S(2)}, u32[]{:S(2)}) collective-permute-start(bf16[2,4,64,128]{3,2,1,0:T(8,128)(2,1)S(1)} %get-tuple-element.67), channel_id=1, source_target_pairs={{0,2},{2,4},{4,6},{6,8},{8,10},{10,12},{12,14},{1,3},{3,5},{5,7},{... | collective-permute-start | bytes 393224 | tf_op jit(solution)/shard_map/ppermute | solution.py:477
  72.2 3.2 %collective-permute-start.13 = (bf16[2,4,64,128]{3,2,1,0:T(8,128)(2,1)S(1)}, bf16[2,4,64,128]{3,2,1,0:T(8,128)(2,1)S(1)}, u32[]{:S(2)}, u32[]{:S(2)}) collective-permute-start(bf16[2,4,64,128]{3,2,1,0:T(8,128)(2,1)S(1)} %get-tuple-element.68), channel_id=1, source_target_pairs={{2,0},{4,2},{6,4},{8,6},{10,8},{12,10},{14,12},{3,1},{5,3},{7,5},{... | collective-permute-start | bytes 393224 | tf_op jit(solution)/shard_map/ppermute | solution.py:478
  76.3 8.7 %collective-permute-start.15 = (f32[88,128]{1,0:T(8,128)S(1)}, f32[88,128]{1,0:T(8,128)S(1)}, u32[]{:S(2)}, u32[]{:S(2)}) collective-permute-start(f32[88,128]{1,0:T(8,128)S(1)} %get-tuple-element.78), channel_id=1, source_target_pairs={{0,1},{1,0},{2,3},{3,2},{4,5},{5,4},{6,7},{7,6},{8,9},{9,8},{10,11... | collective-permute-start | bytes 135176 | tf_op jit(solution)/shard_map/ppermute | solution.py:496
  78.9 6.2 %collective-permute-start.16 = (f32[88,128]{1,0:T(8,128)S(1)}, f32[88,128]{1,0:T(8,128)S(1)}, u32[]{:S(2)}, u32[]{:S(2)}) collective-permute-start(f32[88,128]{1,0:T(8,128)S(1)} %get-tuple-element.79), channel_id=1, source_target_pairs={{0,2},{1,3},{2,0},{3,1},{4,6},{5,7},{6,4},{7,5},{8,10},{9,11},{10,... | collective-permute-start | bytes 135176 | tf_op jit(solution)/shard_map/ppermute | solution.py:496
  81.7 3.8 %collective-permute-start.17 = (f32[88,128]{1,0:T(8,128)S(1)}, f32[88,128]{1,0:T(8,128)S(1)}, u32[]{:S(2)}, u32[]{:S(2)}) collective-permute-start(f32[88,128]{1,0:T(8,128)S(1)} %get-tuple-element.80), channel_id=1, source_target_pairs={{0,3},{1,2},{2,1},{3,0},{4,7},{5,6},{6,5},{7,4},{8,11},{9,10},{10,... | collective-permute-start | bytes 135176 | tf_op jit(solution)/shard_map/ppermute | solution.py:496
  83.4 6.2 %collective-permute-start.14 = (bf16[3,64,128]{2,1,0:T(8,128)(2,1)S(1)}, bf16[3,64,128]{2,1,0:T(8,128)(2,1)S(1)}, u32[]{:S(2)}, u32[]{:S(2)}) collective-permute-start(bf16[3,64,128]{2,1,0:T(8,128)(2,1)S(1)} %edges.3), channel_id=1, source_target_pairs={{0,1},{1,0},{2,3},{3,2},{4,5},{5,4},{6,7},{7,6},{8,9},{9,8},{10,11... | collective-permute-start | bytes 147464 | tf_op jit(solution)/shard_map/ppermute | solution.py:446
  85.4 5.8 %collective-permute-start.20 = (f32[88,128]{1,0:T(8,128)S(1)}, f32[88,128]{1,0:T(8,128)S(1)}, u32[]{:S(2)}, u32[]{:S(2)}) collective-permute-start(f32[88,128]{1,0:T(8,128)S(1)} %sum.2.refs_0_), channel_id=1, source_target_pairs={{0,12},{2,14},{4,0},{6,2},{8,4},{10,6},{12,8},{14,10},{1,13},{3,15... | collective-permute-start | bytes 135176 | tf_op jit(solution)/shard_map/ppermute | solution.py:500
  87.2 5.6 %collective-permute-start.19 = (f32[88,128]{1,0:T(8,128)S(1)}, f32[88,128]{1,0:T(8,128)S(1)}, u32[]{:S(2)}, u32[]{:S(2)}) collective-permute-start(f32[88,128]{1,0:T(8,128)S(1)} %sum.2.refs_0_), channel_id=1, source_target_pairs={{0,8},{2,10},{4,12},{6,14},{8,0},{10,2},{12,4},{14,6},{1,9},{3,11}... | collective-permute-start | bytes 135176 | tf_op jit(solution)/shard_map/ppermute | solution.py:500
  87.6 5.8 %collective-permute-start.18 = (f32[88,128]{1,0:T(8,128)S(1)}, f32[88,128]{1,0:T(8,128)S(1)}, u32[]{:S(2)}, u32[]{:S(2)}) collective-permute-start(f32[88,128]{1,0:T(8,128)S(1)} %sum.2.refs_0_), channel_id=1, source_target_pairs={{0,4},{2,6},{4,8},{6,10},{8,12},{10,14},{12,0},{14,2},{1,5},{3,7},... | collective-permute-start | bytes 135176 | tf_op jit(solution)/shard_map/ppermute | solution.py:500
  93.4 7.3 %collective-permute-start.23 = (f32[88,128]{1,0:T(8,128)S(1)}, f32[88,128]{1,0:T(8,128)S(1)}, u32[]{:S(2)}, u32[]{:S(2)}) collective-permute-start(f32[88,128]{1,0:T(8,128)S(1)} %sum.3.rest_0_), channel_id=1, source_target_pairs={{0,3},{1,2},{2,1},{3,0},{4,7},{5,6},{6,5},{7,4},{8,11},{9,10},{10,... | collective-permute-start | bytes 135176 | tf_op jit(solution)/shard_map/ppermute | solution.py:496
  93.5 7.2 %collective-permute-start.22 = (f32[88,128]{1,0:T(8,128)S(1)}, f32[88,128]{1,0:T(8,128)S(1)}, u32[]{:S(2)}, u32[]{:S(2)}) collective-permute-start(f32[88,128]{1,0:T(8,128)S(1)} %sum.3.rest_0_), channel_id=1, source_target_pairs={{0,2},{1,3},{2,0},{3,1},{4,6},{5,7},{6,4},{7,5},{8,10},{9,11},{10,... | collective-permute-start | bytes 135176 | tf_op jit(solution)/shard_map/ppermute | solution.py:496
  95.3 5.5 %collective-permute-start.21 = (f32[88,128]{1,0:T(8,128)S(1)}, f32[88,128]{1,0:T(8,128)S(1)}, u32[]{:S(2)}, u32[]{:S(2)}) collective-permute-start(f32[88,128]{1,0:T(8,128)S(1)} %sum.3.rest_0_), channel_id=1, source_target_pairs={{0,1},{1,0},{2,3},{3,2},{4,5},{5,4},{6,7},{7,6},{8,9},{9,8},{10,11... | collective-permute-start | bytes 135176 | tf_op jit(solution)/shard_map/ppermute | solution.py:496
  (5 other events, 43.1 us)

commit v5 on v4

--- a/solution.py
+++ b/solution.py
@@ -90,17 +90,20 @@
     full = jnp.concatenate([hw[...].astype(F32), jnp.zeros((nb - nbins, ch), F32)], axis=0)
     head[...] = full.astype(BF16)
     headt[...] = full.T.astype(BF16)
-    ncol, width = len(pieces), pieces[0].shape[1]
+    ncol = len(pieces)
+    band, width = labels.shape[0], labels.shape[1] // ncol
     blocks = [labels[:, width * n : width * (n + 1)] for n in range(ncol)]
     for d, piece in enumerate(pieces):
         want = lax.rem(scal[4] + d, ncol)
         value = blocks[0]
         for n in range(1, ncol):
             value = jnp.where(want == n, blocks[n], value)
-        piece[...] = value.astype(F32).astype(BF16)
-
-
-def edges_kernel(scal, field, above, below, *sides, ncol):
+        value = value.astype(F32).astype(BF16)
+        for u in range(width // 128):
+            piece[band * u : band * (u + 1), :] = value[:, 128 * u : 128 * (u + 1)]
+
+
+def edges_kernel(scal, field, above, below, *sides, ncol, extra):
     tiles, rows, channels, _ = field.shape
     lane = lax.broadcasted_iota(jnp.int32, (channels, 128), 1) // DIL
     if ncol == 2:
@@ -109,15 +112,19 @@
     else:
         picks = [(0, 0), (tiles - 1, DIL)]
     per = 128 // DIL
-    for (tile, extra), out in zip(picks, sides):
+    if extra:
+        sides[1][sides[1].shape[0] - 1] = sides[0][...]
+        sides = sides[1:]
+    for (tile, offset), out in zip(picks, sides):
 
         def add(slot, row, acc):
-            turn = slot * DIL + extra
+            turn = slot * DIL + offset
             turn = turn % 128 if isinstance(turn, int) else lax.rem(turn, 128)
             moved = pltpu.roll(row.astype(F32), turn, 1)
             return jnp.where(lane == slot, moved, acc)
 
-        for part in range(out.shape[0]):
+        parts = out.shape[0] - extra
+        for part in range(parts):
             acc = jnp.zeros((channels, 128), F32)
             start = part * per - DIL
             if part == 0:
@@ -131,7 +138,7 @@
 
             for i in range(start, stop):
                 acc = body(i, acc)
-            if part == out.shape[0] - 1:
+            if part == parts - 1:
                 for ii in range(DIL):
                     acc = add(rows + DIL + ii - part * per, below[tile, ii], acc)
             out[part] = acc.astype(BF16)
@@ -182,7 +189,7 @@
         jobs = [(sides[0], 0, 0, 0), (sides[1], tiles - 1, 2 * channels, 128 - DIL)]
     for side, tile, block, base in jobs:
         mine = (lane >= base) & (lane < base + DIL)
-        for part in range(side.shape[0]):
+        for part in range(-(-high // per)):
 
             def patch(ii, _):
                 i = part * per + ii
@@ -196,7 +203,7 @@
             lax.fori_loop(0, min(per, high - part * per), patch, 0, unroll=8)
 
 
-def forward_kernel(scal, xs, w, bias, hw, hid, slope, direct, one, two, *, stage):
+def forward_kernel(scal, xs, w, bias, hw, hid, slope, direct, one, two, *, stage, swap):
     rows, channels, _ = hid.shape
     nb = hw.shape[0]
     high = direct.shape[0] // nb
@@ -235,7 +242,7 @@
 
     lax.fori_loop(0, rows // 64, head, 0)
 
-    flip = (rq & 1) == 1
+    flip = ((rq & 1) ^ (1 - scal[5] if swap else 0)) == 1
     for m in range(one.shape[0]):
         both = [direct[high * k : high * k + rows, :] for k in (2 * m, 2 * m + 1)]
         turned = jnp.concatenate(both, axis=0).T.astype(BF16)
@@ -275,10 +282,12 @@
         wanted = jnp.zeros((8, 128), F32)
         for d in range(ncol):
             here = lax.rem(scal[4] + ncol - strip, ncol) == d
-            rows8 = strips[d][pl.ds(at, 8), :].astype(F32)
-            for v in range(rows8.shape[1] // 128):
-                lanes = rows8[:, 128 * v : 128 * (v + 1)]
-                wanted = jnp.where(here & (u == v), lanes, wanted)
+            rows8 = pl.ds(pl.multiple_of(u * band + at, 8), 8)
+            if len(strips[d].shape) == 3:
+                value = strips[d][strips[d].shape[0] - 1, rows8, :]
+            else:
+                value = strips[d][rows8, :]
+            wanted = jnp.where(here, value.astype(F32), wanted)
         logits = []
         for m in range((nbins + 1) // 2):
             a, b = (
@@ -427,14 +436,14 @@
         out[:, :, 128 * u : 128 * (u + 1)] = block[:, :some].astype(BF16)
 
 
-def side_columns(field, above, below, scal):
+def side_columns(field, above, below, scal, more=()):
     parts = -(-(field.shape[1] + 2 * DIL) * DIL // 128)
     ncol = lax.axis_size("col")
     return call(
-        functools.partial(edges_kernel, ncol=ncol),
+        functools.partial(edges_kernel, ncol=ncol, extra=len(more)),
         "edges",
-        [shape((parts, field.shape[2], 128))] * (1 if ncol == 2 else 2),
-        (scal, field, above, below),
+        [shape((parts + len(more), field.shape[2], 128))] * (1 if ncol == 2 else 2),
+        (scal, field, above, below, *more),
         us=1.5,
         smem=1,
     )
@@ -450,7 +459,7 @@
             lax.ppermute(to_right, "col", [(i, i + 1) for i in range(ncol - 1)]),
             lax.ppermute(to_left, "col", [(i + 1, i) for i in range(ncol - 1)]),
         ]
-    return call(
+    return got, call(
         functools.partial(border_kernel, ncol=ncol),
         "border",
         shape(inner.shape),
@@ -570,28 +579,33 @@
         name="prep",
     )(scal, pltpu.with_memory_space_constraint(x, pltpu.HBM))
     above, below = row_halo(head, tail)
-    sides = side_columns(xt, above, below, scal)
     w_fwd, w_bwd, bias, hw, hwt, *mine = call(
         setup_kernel,
         "setup",
         [shape((channels, 9 * channels))] * 2
         + [shape((channels, 1), F32), shape((nb, channels)), shape((channels, nb))]
-        + [shape((labels.shape[0], width))] * ncol,
+        + [shape((labels.shape[0] * tiles, 128))] * ncol,
         (scal, conv_weight, conv_bias[None], head_weight, labels, tail),
         us=2,
         smem=1,
     )
-    strips = mine[:1] + [
-        lax.ppermute(mine[d], "col", [(i, (i + d) % ncol) for i in range(ncol)])
-        for d in range(1, ncol)
-    ]
-    xs = with_border(inner_of(xt), above, below, sides, scal)
+    together = ncol == 2 and mine[1].shape == (channels, 128)
+    sides = side_columns(xt, above, below, scal, mine[1:] if together else ())
+    got, xs = with_border(inner_of(xt), above, below, sides, scal)
+    strips = mine[:1] + (
+        got
+        if together
+        else [
+            lax.ppermute(mine[d], "col", [(i, (i + d) % ncol) for i in range(ncol)])
+            for d in range(1, ncol)
+        ]
+    )
 
     kept, got = [], []
     for stage in range(tiles):
         block = shape((pairs, rows, 128))
         hid, slope, direct, *sends = call(
-            functools.partial(forward_kernel, stage=stage),
+            functools.partial(forward_kernel, stage=stage, swap=ncol == 2 and stage == 0),
             "forward",
             [shape(field[1:]), shape(field[1:]), shape((nb * (rows + 8), 128), F32), block, block],
             (scal, xs, w_fwd, bias, hw),
@@ -606,16 +620,23 @@
                 for i in range(nrow)
                 for j in range(ncol)
             ]
-            if ncol > 2 or e == 0:
-                got.append([lax.ppermute(sends[e], ROWS, perm)])
-                continue
             near = [(a, b) for a, b in perm if a % ncol == b % ncol]
             far = [(a, b) for a, b in perm if a % ncol != b % ncol]
-            over = [(a, a + b % ncol - a % ncol) for a, b in far]
-            along = [(a + b % ncol - a % ncol, b) for a, b in far]
-            same = lax.ppermute(sends[e], ROWS, near)
-            relayed = lax.ppermute(sends[e], ROWS, over)
-            got.append([same, lax.ppermute(relayed, ROWS, along)])
+            if ncol > 2 or t == 2 * stage and t > 0:
+                got.append([lax.ppermute(sends[e], ROWS, perm)])
+            elif t == 0:
+                first_far = far
+            else:
+                over = [(a, a + b % ncol - a % ncol) for a, b in far]
+                along = [(a + b % ncol - a % ncol, b) for a, b in far]
+                if t == 1:
+                    direct_in = lax.ppermute(sends[0], ROWS, first_far + near)
+                    got.append([sends[1], direct_in])
+                    same = direct_in
+                else:
+                    same = lax.ppermute(sends[e], ROWS, near)
+                relayed = lax.ppermute(sends[e], ROWS, over)
+                got.append([same, lax.ppermute(relayed, ROWS, along)])
 
     dpre = small = ends = taps = None
     order = list(range(tiles))
@@ -670,7 +691,7 @@
     above, below = row_halo(*ends)
     sides = side_columns(dpre, above, below, scal)
     sides, pieces = lax.optimization_barrier((sides, pieces))
-    ds = with_border(inner_of(dpre), above, below, sides, scal)
+    _, ds = with_border(inner_of(dpre), above, below, sides, scal)
     parts = total_over_tiles(pieces)
 
     pair_gradient = pl.pallas_call(

time: 103 us -> 101 us (0.981)
  waiting for transfers between devices: 31.1 us -> 26.8 us
  starting transfers between devices: 36.3 us -> 38.7 us
    ppermute x2 -> x1, starting transfers between devices: 4.65 us -> 8.75 us  [per_device(): same = lax.ppermute(sends[e], ROWS, near)]
    ppermute x2, waiting for transfers between devices: 8.58 us -> 4.49 us  [per_device(): relayed = lax.ppermute(sends[e], ROWS, over)]
    ppermute x1, waiting for transfers between devices: 3.73 us -> 0.01 us  [per_device(): direct_in = lax.ppermute(sends[0], ROWS, first_far + near)]
    ppermute x2 -> x1, waiting for transfers between devices: 14.8 us -> 17.9 us  [per_device(): got.append([lax.ppermute(sends[e], ROWS, perm)])]
    ppermute x2 -> x1, starting transfers between devices: 2.43 us -> 0.29 us  [per_device(): got.append([lax.ppermute(sends[e], ROWS, perm)])]
    ppermute x1, starting transfers between devices: 0.07 us -> 1.57 us  [per_device(): direct_in = lax.ppermute(sends[0], ROWS, first_far + near)]
    ppermute x3, starting transfers between devices: 4.09 us -> 2.65 us  [total_over_tiles(): own = sum_of([own] + [lax.ppermute(own, 'row', turn) for turn in turns])]
  transfers between devices with their start and end apart: 24 -> 22, of which waited for: 8 -> 9; matrix products, arithmetic and copies ran while one was open for 0% -> 0% of each run, Pallas kernels for 20% -> 20%
where the time goes in v5:
time: 101 us; the launch traced here: 100 us
  starting transfers between devices  38.7 us (38%)
  Pallas kernels  33.1 us (33%)
  waiting for transfers between devices  26.8 us (27%)
  between operations  1.6 us (2%)
    pallas_call x15, Pallas kernels, call(): pl.pallas_call(body, out_shape=out_shape, in_specs=[SM] * smem + [VM] * (...  24.2 us
    ppermute x1, waiting for transfers between devices, per_device(): got.append([lax.ppermute(sends[e], ROWS, perm)])  17.9 us
    ppermute x1, starting transfers between devices, per_device(): same = lax.ppermute(sends[e], ROWS, near)  8.75 us
    ppermute x6, starting transfers between devices, near(): return lax.ppermute(v, ROWS, perm)  7.78 us
    pallas_call x1, Pallas kernels, per_device(): pl.pallas_call(backward_kernel, grid=(rows // 16,), in_specs=[VM, VM], ou...  5.09 us
    ppermute x2, starting transfers between devices, row_halo(): above = lax.ppermute(tail, 'row', [(i, i + 1) for i in range(count - 1)])  5.02 us
    ppermute x2, starting transfers between devices, with_border(): got = [lax.ppermute(sides[0], 'col', [(0, 1), (1, 0)])]  4.69 us
    ppermute x2, waiting for transfers between devices, per_device(): relayed = lax.ppermute(sends[e], ROWS, over)  4.49 us
  transfers between devices with their start and end apart: 22, of which 9 were waited for; matrix products, arithmetic and copies ran while one was open for 0% of the time, Pallas kernels for 20%

profile of v5, /device:TPU:0, one launch (start us, length us, event | category | flops | bytes accessed | tf_op | source)
XLA Modules:
  0.0 100.3 jit_solution(2200678678189641146)
XLA Ops:
  1.4 2.4 %prep.1 = (bf16[2,64,64,128]{3,2,1,0:T(8,128)(2,1)S(1)}, bf16[2,4,64,128]{3,2,1,0:T(8,128)(2,1)S(1)}, bf16[2,4,64,128]{3,2,1,0:T(8,128)(2,1)S(1)}) custom-call(s32[7]{0:T(128)S(1)} %stack.31._.scal, bf16[64,64,256]{2,1,0:T(8,128)(2,1)} %x.1), custom_call_target="tpu_custom_call" | custom-call | flops 4400000000 | tf_op jit(solution)/shard_map/prep/pallas_call | solution.py:567
  5.2 3.0 %collective-permute-start = (bf16[2,4,64,128]{3,2,1,0:T(8,128)(2,1)S(1)}, bf16[2,4,64,128]{3,2,1,0:T(8,128)(2,1)S(1)}, u32[]{:S(2)}, u32[]{:S(2)}) collective-permute-start(bf16[2,4,64,128]{3,2,1,0:T(8,128)(2,1)S(1)} %get-tuple-element.46._), channel_id=1, source_target_pairs={{0,2},{2,4},{4,6},{6,8},{8,10},{10,12},{12,14},{1,3},{3,5},{5,7},{... | collective-permute-start | bytes 393224 | tf_op jit(solution)/shard_map/ppermute | solution.py:486
  10.1 3.0 %collective-permute-start.2 = (bf16[4,64,128]{2,1,0:T(8,128)(2,1)S(1)}, bf16[4,64,128]{2,1,0:T(8,128)(2,1)S(1)}, u32[]{:S(2)}, u32[]{:S(2)}) collective-permute-start(bf16[4,64,128]{2,1,0:T(8,128)(2,1)S(1)} %edges.2), channel_id=1, source_target_pairs={{0,1},{1,0},{2,3},{3,2},{4,5},{5,4},{6,7},{7,6},{8,9},{9,8},{10,11... | collective-permute-start | bytes 196616 | tf_op jit(solution)/shard_map/ppermute | solution.py:455
  13.1 1.7 %inner.2.rest_1_ = bf16[2,72,192,128]{3,2,1,0:T(8,128)(2,1)S(1)} custom-call(bf16[2,64,64,128]{3,2,1,0:T(8,128)(2,1)S(1)} %get-tuple-element.48.field), custom_call_target="tpu_custom_call" | custom-call | flops 3300000000 | tf_op jit(solution)/shard_map/inner/pallas_call | solution.py:28
  15.4 1.7 %border.2.xs = bf16[2,72,192,128]{3,2,1,0:T(8,128)(2,1)S(1)} custom-call(s32[7]{0:T(128)S(1)} %stack.31._.scal, bf16[2,4,64,128]{3,2,1,0:T(8,128)(2,1)S(1)} %collective-permute-done.above, bf16[2,4,64,128]{3,2,1,0:T(8,128)(2,1)S(1)} %collective-permute-done.1.below, ...), custom_call_target="tpu_custom_call", output_to_operand_aliasing={{}: (4, {})} | custom-call | flops 1650000000 | tf_op jit(solution)/shard_map/border/pallas_call | solution.py:28
  17.1 3.0 %forward.3 = (bf16[64,64,128]{2,1,0:T(8,128)(2,1)S(1)}, bf16[64,64,128]{2,1,0:T(8,128)(2,1)S(1)}, f32[2880,128]{1,0:T(8,128)S(1)}, bf16[19,64,128]{2,1,0:T(8,128)(2,1)S(1)}, bf16[19,64,128]{2,1,0:T(8,128)(2,1)S(1)}) custom-call(s32[7]{0:T(128)S(1)} %stack.31._.scal, bf16[2,72,192,128]{3,2,1,0:T(8,128)(2,1)S(1)} %border.2.xs, ...), custom_call_target="tpu_custom_call" | custom-call | flops 6600000000 | tf_op jit(solution)/shard_map/forward/pallas_call | solution.py:28
  21.4 3.0 %forward.2 = (bf16[64,64,128]{2,1,0:T(8,128)(2,1)S(1)}, bf16[64,64,128]{2,1,0:T(8,128)(2,1)S(1)}, f32[2880,128]{1,0:T(8,128)S(1)}, bf16[19,64,128]{2,1,0:T(8,128)(2,1)S(1)}, bf16[19,64,128]{2,1,0:T(8,128)(2,1)S(1)}) custom-call(s32[7]{0:T(128)S(1)} %stack.31._.scal, bf16[2,72,192,128]{3,2,1,0:T(8,128)(2,1)S(1)} %border.2.xs, ...), custom_call_target="tpu_custom_call" | custom-call | flops 6600000000 | tf_op jit(solution)/shard_map/forward/pallas_call | solution.py:28
  25.7 1.6 %collective-permute-start.7 = (bf16[19,64,128]{2,1,0:T(8,128)(2,1)S(1)}, bf16[19,64,128]{2,1,0:T(8,128)(2,1)S(1)}, u32[]{:S(2)}, u32[]{:S(2)}) collective-permute-start(bf16[19,64,128]{2,1,0:T(8,128)(2,1)S(1)} %get-tuple-element.64), channel_id=1, source_target_pairs={{1,8},{3,10},{5,12},{7,14},{8,1},{10,3},{12,5},{14,7},{0,2},{2,0},... | collective-permute-start | bytes 933896 | tf_op jit(solution)/shard_map/ppermute | solution.py:633
  27.2 4.5 %collective-permute-done.8 = bf16[19,64,128]{2,1,0:T(8,128)(2,1)S(1)} collective-permute-done((bf16[19,64,128]{2,1,0:T(8,128)(2,1)S(1)}, bf16[19,64,128]{2,1,0:T(8,128)(2,1)S(1)}, u32[]{:S(2)}, u32[]{:S(2)}) %collective-permute-start.8) | collective-permute-done | bytes 311328 | tf_op jit(solution)/shard_map/ppermute | solution.py:638
  33.3 8.7 %collective-permute-start.4 = (bf16[19,64,128]{2,1,0:T(8,128)(2,1)S(1)}, bf16[19,64,128]{2,1,0:T(8,128)(2,1)S(1)}, u32[]{:S(2)}, u32[]{:S(2)}) collective-permute-start(bf16[19,64,128]{2,1,0:T(8,128)(2,1)S(1)} %get-tuple-element.58), channel_id=1, source_target_pairs={{0,6},{2,4},{4,2},{6,0},{9,15},{11,13},{13,11},{15,9},{16,22},{18,... | collective-permute-start | bytes 933896 | tf_op jit(solution)/shard_map/ppermute | solution.py:637
  43.7 2.7 %middle.2 = (bf16[2,64,64,128]{3,2,1,0:T(8,128)(2,1)S(1)}, f32[64,128]{1,0:T(8,128)S(1)}) custom-call(s32[7]{0:T(128)S(1)} %stack.31._.scal, f32[37]{0:T(128)S(1)} %copy-done.4, f32[40,72,128]{2,1,0:T(8,128)S(1)} %bitcast.14, bf16[64,64,128]{2,1,0:T(8,128)(2,1)S(1)} %get-tuple-element.61.hid, bf16[64,64,128]{2,1,0:T(8,128)(2,1)S(1)} %get-tuple-element.62.slope, ...), custom_call_target="tpu_custom_call" | custom-call | flops 5500000256 | tf_op jit(solution)/shard_map/middle/pallas_call | solution.py:28
  46.4 1.7 %weights.2.rest_7_.rest_0_ = f32[192,192]{1,0:T(8,128)S(1)} custom-call(s32[7]{0:T(128)S(1)} %stack.31._.scal, bf16[2,72,192,128]{3,2,1,0:T(8,128)(2,1)S(1)} %border.2.xs, bf16[2,64,64,128]{3,2,1,0:T(8,128)(2,1)S(1)} %get-tuple-element.65.dpre.rest_5_, f32[64,128]{1,0:T(8,128)S(1)} %get-tuple-element.66.small.rest_6_), custom_call_target="tpu_custom_call" | custom-call | flops 2750000128 | tf_op jit(solution)/shard_map/weights/pallas_call | solution.py:28
  48.1 17.9 %collective-permute-done.3.rest_0_ = bf16[19,64,128]{2,1,0:T(8,128)(2,1)S(1)} collective-permute-done((bf16[19,64,128]{2,1,0:T(8,128)(2,1)S(1)}, bf16[19,64,128]{2,1,0:T(8,128)(2,1)S(1)}, u32[]{:S(2)}, u32[]{:S(2)}) %collective-permute-start.3) | collective-permute-done | bytes 311328 | tf_op jit(solution)/shard_map/ppermute | solution.py:626
  65.9 2.7 %middle.3 = (bf16[2,64,64,128]{3,2,1,0:T(8,128)(2,1)S(1)}, f32[64,128]{1,0:T(8,128)S(1)}, bf16[2,4,64,128]{3,2,1,0:T(8,128)(2,1)S(1)}, bf16[2,4,64,128]{3,2,1,0:T(8,128)(2,1)S(1)}) custom-call(s32[7]{0:T(128)S(1)} %stack.31._.scal, f32[37]{0:T(128)S(1)} %copy-done.4, f32[40,72,128]{2,1,0:T(8,128)S(1)} %bitcast.13, ...), custom_call_target="tpu_custom_call", output_to_operand_aliasing={{0}: (11, {})} | custom-call | flops 5500000256 | tf_op jit(solution)/shard_map/middle/pallas_call | solution.py:28
  68.6 2.0 %collective-permute-start.10 = (bf16[2,4,64,128]{3,2,1,0:T(8,128)(2,1)S(1)}, bf16[2,4,64,128]{3,2,1,0:T(8,128)(2,1)S(1)}, u32[]{:S(2)}, u32[]{:S(2)}) collective-permute-start(bf16[2,4,64,128]{3,2,1,0:T(8,128)(2,1)S(1)} %get-tuple-element.67), channel_id=1, source_target_pairs={{0,2},{2,4},{4,6},{6,8},{8,10},{10,12},{12,14},{1,3},{3,5},{5,7},{... | collective-permute-start | bytes 393224 | tf_op jit(solution)/shard_map/ppermute | solution.py:486
  71.9 1.8 %weights.3 = (f32[88,128]{1,0:T(8,128)S(1)}, f32[88,128]{1,0:T(8,128)S(1)}, f32[88,128]{1,0:T(8,128)S(1)}, f32[88,128]{1,0:T(8,128)S(1)}) custom-call(s32[7]{0:T(128)S(1)} %stack.31._.scal, bf16[2,72,192,128]{3,2,1,0:T(8,128)(2,1)S(1)} %border.2.xs, bf16[2,64,64,128]{3,2,1,0:T(8,128)(2,1)S(1)} %get-tuple-element.69.field.dpre, ...), custom_call_target="tpu_custom_call" | custom-call | flops 2750000128 | tf_op jit(solution)/shard_map/weights/pallas_call | solution.py:28
  74.8 2.8 %collective-permute-start.13 = (f32[88,128]{1,0:T(8,128)S(1)}, f32[88,128]{1,0:T(8,128)S(1)}, u32[]{:S(2)}, u32[]{:S(2)}) collective-permute-start(f32[88,128]{1,0:T(8,128)S(1)} %get-tuple-element.78), channel_id=1, source_target_pairs={{0,1},{1,0},{2,3},{3,2},{4,5},{5,4},{6,7},{7,6},{8,9},{9,8},{10,11... | collective-permute-start | bytes 135176 | tf_op jit(solution)/shard_map/ppermute | solution.py:505
  77.5 2.8 %collective-permute-start.14 = (f32[88,128]{1,0:T(8,128)S(1)}, f32[88,128]{1,0:T(8,128)S(1)}, u32[]{:S(2)}, u32[]{:S(2)}) collective-permute-start(f32[88,128]{1,0:T(8,128)S(1)} %get-tuple-element.79), channel_id=1, source_target_pairs={{0,2},{1,3},{2,0},{3,1},{4,6},{5,7},{6,4},{7,5},{8,10},{9,11},{10,... | collective-permute-start | bytes 135176 | tf_op jit(solution)/shard_map/ppermute | solution.py:505
  80.4 1.7 %inner.3.rest_1_ = bf16[2,72,192,128]{3,2,1,0:T(8,128)(2,1)S(1)} custom-call(bf16[2,64,64,128]{3,2,1,0:T(8,128)(2,1)S(1)} %get-tuple-element.69.field.dpre), custom_call_target="tpu_custom_call" | custom-call | flops 3300000000 | tf_op jit(solution)/shard_map/inner/pallas_call | solution.py:28
  82.0 1.7 %collective-permute-start.12 = (bf16[3,64,128]{2,1,0:T(8,128)(2,1)S(1)}, bf16[3,64,128]{2,1,0:T(8,128)(2,1)S(1)}, u32[]{:S(2)}, u32[]{:S(2)}) collective-permute-start(bf16[3,64,128]{2,1,0:T(8,128)(2,1)S(1)} %edges.3), channel_id=1, source_target_pairs={{0,1},{1,0},{2,3},{3,2},{4,5},{5,4},{6,7},{7,6},{8,9},{9,8},{10,11... | collective-permute-start | bytes 147464 | tf_op jit(solution)/shard_map/ppermute | solution.py:455
  86.8 1.7 %border.3.ds = bf16[2,72,192,128]{3,2,1,0:T(8,128)(2,1)S(1)} custom-call(s32[7]{0:T(128)S(1)} %stack.31._.scal, bf16[2,4,64,128]{3,2,1,0:T(8,128)(2,1)S(1)} %collective-permute-done.10.above, bf16[2,4,64,128]{3,2,1,0:T(8,128)(2,1)S(1)} %collective-permute-done.11.below, ...), custom_call_target="tpu_custom_call", output_to_operand_aliasing={{}: (4, {})} | custom-call | flops 1650000000 | tf_op jit(solution)/shard_map/border/pallas_call | solution.py:28
  88.7 2.0 %collective-permute-done.17.refs_2_ = f32[88,128]{1,0:T(8,128)S(1)} collective-permute-done((f32[88,128]{1,0:T(8,128)S(1)}, f32[88,128]{1,0:T(8,128)S(1)}, u32[]{:S(2)}, u32[]{:S(2)}) %collective-permute-start.17) | collective-permute-done | bytes 45088 | tf_op jit(solution)/shard_map/ppermute | solution.py:509
  92.3 1.6 %collective-permute-start.19 = (f32[88,128]{1,0:T(8,128)S(1)}, f32[88,128]{1,0:T(8,128)S(1)}, u32[]{:S(2)}, u32[]{:S(2)}) collective-permute-start(f32[88,128]{1,0:T(8,128)S(1)} %sum.3.rest_0_), channel_id=1, source_target_pairs={{0,1},{1,0},{2,3},{3,2},{4,5},{5,4},{6,7},{7,6},{8,9},{9,8},{10,11... | collective-permute-start | bytes 135176 | tf_op jit(solution)/shard_map/ppermute | solution.py:505
  93.9 5.1 %backward.1 = bf16[64,64,256]{2,1,0:T(8,128)(2,1)} custom-call(bf16[2,72,192,128]{3,2,1,0:T(8,128)(2,1)S(1)} %border.3.ds, bf16[64,576]{1,0:T(8,128)(2,1)S(1)} %get-tuple-element.76.w), custom_call_target="tpu_custom_call" | custom-call | flops 6600000000 | tf_op jit(solution)/shard_map/backward/pallas_call | solution.py:697
  (49 shorter events, 18.2 us)
Async XLA Ops:
  1.4 6.8 %copy-start.2 = (bf16[37,64]{1,0:T(8,128)(2,1)S(1)}, bf16[37,64]{1,0:T(8,128)(2,1)}, u32[]{:S(2)}) copy-start(bf16[37,64]{1,0:T(8,128)(2,1)} %hw.1) | copy-start | bytes 14212
  3.9 5.2 %collective-permute-start.1 = (bf16[2,4,64,128]{3,2,1,0:T(8,128)(2,1)S(1)}, bf16[2,4,64,128]{3,2,1,0:T(8,128)(2,1)S(1)}, u32[]{:S(2)}, u32[]{:S(2)}) collective-permute-start(bf16[2,4,64,128]{3,2,1,0:T(8,128)(2,1)S(1)} %get-tuple-element.47), channel_id=1, source_target_pairs={{2,0},{4,2},{6,4},{8,6},{10,8},{12,10},{14,12},{3,1},{5,3},{7,5},{... | collective-permute-start | bytes 393224 | tf_op jit(solution)/shard_map/ppermute | solution.py:487
  5.2 4.0 %collective-permute-start = (bf16[2,4,64,128]{3,2,1,0:T(8,128)(2,1)S(1)}, bf16[2,4,64,128]{3,2,1,0:T(8,128)(2,1)S(1)}, u32[]{:S(2)}, u32[]{:S(2)}) collective-permute-start(bf16[2,4,64,128]{3,2,1,0:T(8,128)(2,1)S(1)} %get-tuple-element.46._), channel_id=1, source_target_pairs={{0,2},{2,4},{4,6},{6,8},{8,10},{10,12},{12,14},{1,3},{3,5},{5,7},{... | collective-permute-start | bytes 393224 | tf_op jit(solution)/shard_map/ppermute | solution.py:486
  10.1 5.3 %collective-permute-start.2 = (bf16[4,64,128]{2,1,0:T(8,128)(2,1)S(1)}, bf16[4,64,128]{2,1,0:T(8,128)(2,1)S(1)}, u32[]{:S(2)}, u32[]{:S(2)}) collective-permute-start(bf16[4,64,128]{2,1,0:T(8,128)(2,1)S(1)} %edges.2), channel_id=1, source_target_pairs={{0,1},{1,0},{2,3},{3,2},{4,5},{5,4},{6,7},{7,6},{8,9},{9,8},{10,11... | collective-permute-start | bytes 196616 | tf_op jit(solution)/shard_map/ppermute | solution.py:455
  20.1 23.6 %copy-start.4 = (f32[37]{0:T(128)S(1)}, f32[37]{0:T(128)}, u32[]{:S(2)}) copy-start(f32[37]{0:T(128)} %hb.3) | copy-start | bytes 448
  20.1 11.7 %collective-permute-start.8 = (bf16[19,64,128]{2,1,0:T(8,128)(2,1)S(1)}, bf16[19,64,128]{2,1,0:T(8,128)(2,1)S(1)}, u32[]{:S(2)}, u32[]{:S(2)}) collective-permute-start(bf16[19,64,128]{2,1,0:T(8,128)(2,1)S(1)} %get-tuple-element.63.rest_0_), channel_id=1, source_target_pairs={{1,0},{3,2},{5,4},{7,6},{8,9},{10,11},{12,13},{14,15},{17,16},{19,... | collective-permute-start | bytes 933896 | tf_op jit(solution)/shard_map/ppermute | solution.py:638
  24.4 17.9 %collective-permute-start.5 = (bf16[19,64,128]{2,1,0:T(8,128)(2,1)S(1)}, bf16[19,64,128]{2,1,0:T(8,128)(2,1)S(1)}, u32[]{:S(2)}, u32[]{:S(2)}) collective-permute-start(bf16[19,64,128]{2,1,0:T(8,128)(2,1)S(1)} %get-tuple-element.58), channel_id=1, source_target_pairs={{1,0},{3,2},{5,4},{7,6},{8,9},{10,11},{12,13},{14,15},{17,16},{19,... | collective-permute-start | bytes 933896 | tf_op jit(solution)/shard_map/ppermute | solution.py:638
  25.7 17.9 %collective-permute-start.7 = (bf16[19,64,128]{2,1,0:T(8,128)(2,1)S(1)}, bf16[19,64,128]{2,1,0:T(8,128)(2,1)S(1)}, u32[]{:S(2)}, u32[]{:S(2)}) collective-permute-start(bf16[19,64,128]{2,1,0:T(8,128)(2,1)S(1)} %get-tuple-element.64), channel_id=1, source_target_pairs={{1,8},{3,10},{5,12},{7,14},{8,1},{10,3},{12,5},{14,7},{0,2},{2,0},... | collective-permute-start | bytes 933896 | tf_op jit(solution)/shard_map/ppermute | solution.py:633
  31.7 11.9 %collective-permute-start.9 = (bf16[19,64,128]{2,1,0:T(8,128)(2,1)S(1)}, bf16[19,64,128]{2,1,0:T(8,128)(2,1)S(1)}, u32[]{:S(2)}, u32[]{:S(2)}) collective-permute-start(bf16[19,64,128]{2,1,0:T(8,128)(2,1)S(1)} %collective-permute-done.8), channel_id=1, source_target_pairs={{0,10},{2,8},{4,14},{6,12},{9,3},{11,1},{13,7},{15,5},{16,26},{18,... | collective-permute-start | bytes 933896 | tf_op jit(solution)/shard_map/ppermute | solution.py:639
  33.3 32.7 %collective-permute-start.4 = (bf16[19,64,128]{2,1,0:T(8,128)(2,1)S(1)}, bf16[19,64,128]{2,1,0:T(8,128)(2,1)S(1)}, u32[]{:S(2)}, u32[]{:S(2)}) collective-permute-start(bf16[19,64,128]{2,1,0:T(8,128)(2,1)S(1)} %get-tuple-element.58), channel_id=1, source_target_pairs={{0,6},{2,4},{4,2},{6,0},{9,15},{11,13},{13,11},{15,9},{16,22},{18,... | collective-permute-start | bytes 933896 | tf_op jit(solution)/shard_map/ppermute | solution.py:637
  42.0 23.9 %collective-permute-start.3 = (bf16[19,64,128]{2,1,0:T(8,128)(2,1)S(1)}, bf16[19,64,128]{2,1,0:T(8,128)(2,1)S(1)}, u32[]{:S(2)}, u32[]{:S(2)}) collective-permute-start(bf16[19,64,128]{2,1,0:T(8,128)(2,1)S(1)} %get-tuple-element.57), channel_id=1, source_target_pairs={{0,4},{1,12},{2,6},{3,14},{4,0},{5,8},{6,2},{7,10},{8,5},{9,13},{1... | collective-permute-start | bytes 933896 | tf_op jit(solution)/shard_map/ppermute | solution.py:626
  42.3 23.6 %collective-permute-start.6 = (bf16[19,64,128]{2,1,0:T(8,128)(2,1)S(1)}, bf16[19,64,128]{2,1,0:T(8,128)(2,1)S(1)}, u32[]{:S(2)}, u32[]{:S(2)}) collective-permute-start(bf16[19,64,128]{2,1,0:T(8,128)(2,1)S(1)} %collective-permute-done.5), channel_id=1, source_target_pairs={{0,14},{2,12},{4,10},{6,8},{9,7},{11,5},{13,3},{15,1},{16,30},{18,... | collective-permute-start | bytes 933896 | tf_op jit(solution)/shard_map/ppermute | solution.py:639
  68.6 5.1 %collective-permute-start.10 = (bf16[2,4,64,128]{3,2,1,0:T(8,128)(2,1)S(1)}, bf16[2,4,64,128]{3,2,1,0:T(8,128)(2,1)S(1)}, u32[]{:S(2)}, u32[]{:S(2)}) collective-permute-start(bf16[2,4,64,128]{3,2,1,0:T(8,128)(2,1)S(1)} %get-tuple-element.67), channel_id=1, source_target_pairs={{0,2},{2,4},{4,6},{6,8},{8,10},{10,12},{12,14},{1,3},{3,5},{5,7},{... | collective-permute-start | bytes 393224 | tf_op jit(solution)/shard_map/ppermute | solution.py:486
  70.6 3.2 %collective-permute-start.11 = (bf16[2,4,64,128]{3,2,1,0:T(8,128)(2,1)S(1)}, bf16[2,4,64,128]{3,2,1,0:T(8,128)(2,1)S(1)}, u32[]{:S(2)}, u32[]{:S(2)}) collective-permute-start(bf16[2,4,64,128]{3,2,1,0:T(8,128)(2,1)S(1)} %get-tuple-element.68), channel_id=1, source_target_pairs={{2,0},{4,2},{6,4},{8,6},{10,8},{12,10},{14,12},{3,1},{5,3},{7,5},{... | collective-permute-start | bytes 393224 | tf_op jit(solution)/shard_map/ppermute | solution.py:487
  74.8 8.9 %collective-permute-start.13 = (f32[88,128]{1,0:T(8,128)S(1)}, f32[88,128]{1,0:T(8,128)S(1)}, u32[]{:S(2)}, u32[]{:S(2)}) collective-permute-start(f32[88,128]{1,0:T(8,128)S(1)} %get-tuple-element.78), channel_id=1, source_target_pairs={{0,1},{1,0},{2,3},{3,2},{4,5},{5,4},{6,7},{7,6},{8,9},{9,8},{10,11... | collective-permute-start | bytes 135176 | tf_op jit(solution)/shard_map/ppermute | solution.py:505
  77.5 6.2 %collective-permute-start.14 = (f32[88,128]{1,0:T(8,128)S(1)}, f32[88,128]{1,0:T(8,128)S(1)}, u32[]{:S(2)}, u32[]{:S(2)}) collective-permute-start(f32[88,128]{1,0:T(8,128)S(1)} %get-tuple-element.79), channel_id=1, source_target_pairs={{0,2},{1,3},{2,0},{3,1},{4,6},{5,7},{6,4},{7,5},{8,10},{9,11},{10,... | collective-permute-start | bytes 135176 | tf_op jit(solution)/shard_map/ppermute | solution.py:505
  80.3 3.8 %collective-permute-start.15 = (f32[88,128]{1,0:T(8,128)S(1)}, f32[88,128]{1,0:T(8,128)S(1)}, u32[]{:S(2)}, u32[]{:S(2)}) collective-permute-start(f32[88,128]{1,0:T(8,128)S(1)} %get-tuple-element.80), channel_id=1, source_target_pairs={{0,3},{1,2},{2,1},{3,0},{4,7},{5,6},{6,5},{7,4},{8,11},{9,10},{10,... | collective-permute-start | bytes 135176 | tf_op jit(solution)/shard_map/ppermute | solution.py:505
  82.0 4.7 %collective-permute-start.12 = (bf16[3,64,128]{2,1,0:T(8,128)(2,1)S(1)}, bf16[3,64,128]{2,1,0:T(8,128)(2,1)S(1)}, u32[]{:S(2)}, u32[]{:S(2)}) collective-permute-start(bf16[3,64,128]{2,1,0:T(8,128)(2,1)S(1)} %edges.3), channel_id=1, source_target_pairs={{0,1},{1,0},{2,3},{3,2},{4,5},{5,4},{6,7},{7,6},{8,9},{9,8},{10,11... | collective-permute-start | bytes 147464 | tf_op jit(solution)/shard_map/ppermute | solution.py:455
  84.1 4.6 %collective-permute-start.18 = (f32[88,128]{1,0:T(8,128)S(1)}, f32[88,128]{1,0:T(8,128)S(1)}, u32[]{:S(2)}, u32[]{:S(2)}) collective-permute-start(f32[88,128]{1,0:T(8,128)S(1)} %sum.2.refs_0_), channel_id=1, source_target_pairs={{0,12},{2,14},{4,0},{6,2},{8,4},{10,6},{12,8},{14,10},{1,13},{3,15... | collective-permute-start | bytes 135176 | tf_op jit(solution)/shard_map/ppermute | solution.py:509
  84.3 6.4 %collective-permute-start.17 = (f32[88,128]{1,0:T(8,128)S(1)}, f32[88,128]{1,0:T(8,128)S(1)}, u32[]{:S(2)}, u32[]{:S(2)}) collective-permute-start(f32[88,128]{1,0:T(8,128)S(1)} %sum.2.refs_0_), channel_id=1, source_target_pairs={{0,8},{2,10},{4,12},{6,14},{8,0},{10,2},{12,4},{14,6},{1,9},{3,11}... | collective-permute-start | bytes 135176 | tf_op jit(solution)/shard_map/ppermute | solution.py:509
  85.8 5.8 %collective-permute-start.16 = (f32[88,128]{1,0:T(8,128)S(1)}, f32[88,128]{1,0:T(8,128)S(1)}, u32[]{:S(2)}, u32[]{:S(2)}) collective-permute-start(f32[88,128]{1,0:T(8,128)S(1)} %sum.2.refs_0_), channel_id=1, source_target_pairs={{0,4},{2,6},{4,8},{6,10},{8,12},{10,14},{12,0},{14,2},{1,5},{3,7},... | collective-permute-start | bytes 135176 | tf_op jit(solution)/shard_map/ppermute | solution.py:509
  91.6 7.3 %collective-permute-start.21 = (f32[88,128]{1,0:T(8,128)S(1)}, f32[88,128]{1,0:T(8,128)S(1)}, u32[]{:S(2)}, u32[]{:S(2)}) collective-permute-start(f32[88,128]{1,0:T(8,128)S(1)} %sum.3.rest_0_), channel_id=1, source_target_pairs={{0,3},{1,2},{2,1},{3,0},{4,7},{5,6},{6,5},{7,4},{8,11},{9,10},{10,... | collective-permute-start | bytes 135176 | tf_op jit(solution)/shard_map/ppermute | solution.py:505
  91.7 7.2 %collective-permute-start.20 = (f32[88,128]{1,0:T(8,128)S(1)}, f32[88,128]{1,0:T(8,128)S(1)}, u32[]{:S(2)}, u32[]{:S(2)}) collective-permute-start(f32[88,128]{1,0:T(8,128)S(1)} %sum.3.rest_0_), channel_id=1, source_target_pairs={{0,2},{1,3},{2,0},{3,1},{4,6},{5,7},{6,4},{7,5},{8,10},{9,11},{10,... | collective-permute-start | bytes 135176 | tf_op jit(solution)/shard_map/ppermute | solution.py:505
  92.3 6.7 %collective-permute-start.19 = (f32[88,128]{1,0:T(8,128)S(1)}, f32[88,128]{1,0:T(8,128)S(1)}, u32[]{:S(2)}, u32[]{:S(2)}) collective-permute-start(f32[88,128]{1,0:T(8,128)S(1)} %sum.3.rest_0_), channel_id=1, source_target_pairs={{0,1},{1,0},{2,3},{3,2},{4,5},{5,4},{6,7},{7,6},{8,9},{9,8},{10,11... | collective-permute-start | bytes 135176 | tf_op jit(solution)/shard_map/ppermute | solution.py:505
  (3 other events, 20.5 us)

commit v6 on v5

--- a/solution.py
+++ b/solution.py
@@ -83,9 +83,9 @@
     nbins, nb = hw.shape[0], head.shape[0]
     for a in range(3):
         for b in range(3):
-            at = (3 * a + b) * ch
-            fwd[:, at : at + ch] = cw[a, b]
-            bwd[:, at : at + ch] = cw[2 - a, 2 - b].astype(F32).T.astype(BF16)
+            spot = (slice(ch * a, ch * (a + 1)), slice(ch * b, ch * (b + 1)))
+            fwd[spot] = cw[a, b]
+            bwd[spot] = cw[2 - a, 2 - b].astype(F32).T.astype(BF16)
     bias[...] = jnp.broadcast_to(cb[...], (ch, ch)).T[:, 0:1]
     full = jnp.concatenate([hw[...].astype(F32), jnp.zeros((nb - nbins, ch), F32)], axis=0)
     head[...] = full.astype(BF16)
@@ -167,7 +167,7 @@
         place(out, i + DIL, [field[u, i] for u in range(tiles)])
         return 0
 
-    lax.fori_loop(0, rows, body, 0, unroll=8)
+    lax.fori_loop(0, rows, body, 0, unroll=64)
 
 
 def border_kernel(scal, above, below, *rest, ncol):
@@ -203,6 +203,23 @@
             lax.fori_loop(0, min(per, high - part * per), patch, 0, unroll=8)
 
 
+def convolved(w, row, starts, count):
+    out = w.shape[0] // 3
+    last = count // DIL - 1
+    for m in starts:
+        parts = []
+        for k in range(last + 3):
+            low, high = max(0, k - last), min(2, k)
+            v = jnp.dot(
+                w[out * low : out * (high + 1)],
+                row(m + DIL * k),
+                preferred_element_type=F32,
+            )
+            parts.append({a: v[out * (a - low) : out * (a - low + 1)] for a in range(low, high + 1)})
+            if k >= 2:
+                yield m + DIL * (k - 2), parts[k - 2][0] + parts[k - 1][1] + parts[k][2]
+
+
 def forward_kernel(scal, xs, w, bias, hw, hid, slope, direct, one, two, *, stage, swap):
     rows, channels, _ = hid.shape
     nb = hw.shape[0]
@@ -210,27 +227,17 @@
     rq = scal[0]
     u = (rq >> 1) ^ stage
 
-    def window(i):
-        return jnp.concatenate([xs[u, i + DIL * a] for a in range(3)], axis=0)
-
-    def conv(g, _):
-        for p in range(8):
-            i = g * 64 + 8 * p
-            pre = jnp.dot(
-                w[...],
-                pairs_of([window(i + e) for e in range(8)]),
-                preferred_element_type=F32,
-            )
-            pre = pre + bias[...]
-            grown = jnp.exp(jnp.minimum(pre, 0.0))
-            h = jnp.where(pre > 0, pre, grown - 1.0).astype(BF16)
-            s = jnp.where(pre > 0, 1.0, grown).astype(BF16)
-            for e in range(8):
-                hid[i + e] = h[:, 128 * e : 128 * (e + 1)]
-                slope[i + e] = s[:, 128 * e : 128 * (e + 1)]
-        return 0
-
-    lax.fori_loop(0, rows // 64, conv, 0)
+    def row(i):
+        return pairs_of([xs[u, i], xs[u, i + 1]])
+
+    for i, pre in convolved(w, row, range(0, DIL, 2), rows):
+        pre = pre + bias[...]
+        grown = jnp.exp(jnp.minimum(pre, 0.0))
+        h = jnp.where(pre > 0, pre, grown - 1.0).astype(BF16)
+        s = jnp.where(pre > 0, 1.0, grown).astype(BF16)
+        for e in range(2):
+            hid[i + e] = h[:, 128 * e : 128 * (e + 1)]
+            slope[i + e] = s[:, 128 * e : 128 * (e + 1)]
 
     def head(g, _):
         for p in range(8):
@@ -417,19 +424,13 @@
     step = pl.program_id(0)
     channels, some, width = out.shape
     tiles = width // 128
-    for ii in range(some):
-        i = step * some + ii
-        window = pairs_of(
-            [
-                jnp.concatenate([ds[u, i + DIL * a] for a in range(3)], axis=0)
-                for u in range(tiles)
-            ]
-        )
-        v = jnp.dot(w[...], window, preferred_element_type=F32)
+    def row(i):
+        return pairs_of([ds[u, step * some + i] for u in range(tiles)])
+
+    for i, v in convolved(w, row, range(DIL), some):
         for u in range(tiles):
-            turned[pl.ds(u * channels * (some + 8) + ii, channels, stride=some + 8), :] = v[
-                :, 128 * u : 128 * (u + 1)
-            ]
+            at = u * channels * (some + 8) + i
+            turned[pl.ds(at, channels, stride=some + 8), :] = v[:, 128 * u : 128 * (u + 1)]
     for u in range(tiles):
         at = (some + 8) * channels * u
         block = turned[at : at + (some + 8) * channels, :].reshape(channels, some + 8, 128)
@@ -582,7 +583,7 @@
     w_fwd, w_bwd, bias, hw, hwt, *mine = call(
         setup_kernel,
         "setup",
-        [shape((channels, 9 * channels))] * 2
+        [shape((wide, wide))] * 2
         + [shape((channels, 1), F32), shape((nb, channels)), shape((channels, nb))]
         + [shape((labels.shape[0] * tiles, 128))] * ncol,
         (scal, conv_weight, conv_bias[None], head_weight, labels, tail),

time: 101 us -> 97.8 us (0.968)
  Pallas kernels: 33.1 us -> 29 us
  starting transfers between devices: 38.7 us -> 40.1 us
    pallas_call x15, Pallas kernels: 24.2 us -> 21.5 us  [call(): pl.pallas_call(body, out_shape=out_shape, in_specs=[SM] * smem + [VM] * (...]
    ppermute x1, waiting for transfers between devices: 17.9 us -> 16.4 us  [per_device(): got.append([lax.ppermute(sends[e], ROWS, perm)])]
    ppermute x1, starting transfers between devices: 0.29 us -> 1.81 us  [per_device(): got.append([lax.ppermute(sends[e], ROWS, perm)])]
    pallas_call x1, Pallas kernels: 5.09 us -> 3.66 us  [per_device(): pl.pallas_call(backward_kernel, grid=(rows // 16,), in_specs=[VM, VM], ou...]
  transfers between devices with their start and end apart: 22 -> 22, of which waited for: 9 -> 8; matrix products, arithmetic and copies ran while one was open for 0% -> 0% of each run, Pallas kernels for 20% -> 17%
where the time goes in v6:
time: 97.8 us; the launch traced here: 97.4 us
  starting transfers between devices  40.1 us (41%)
  Pallas kernels  29 us (30%)
  waiting for transfers between devices  26.7 us (27%)
  between operations  1.61 us (2%)
    pallas_call x15, Pallas kernels, call(): pl.pallas_call(body, out_shape=out_shape, in_specs=[SM] * smem + [VM] * (...  21.5 us
    ppermute x1, waiting for transfers between devices, per_device(): got.append([lax.ppermute(sends[e], ROWS, perm)])  16.4 us
    ppermute x6, starting transfers between devices, near(): return lax.ppermute(v, ROWS, perm)  8.52 us
    ppermute x1, starting transfers between devices, per_device(): same = lax.ppermute(sends[e], ROWS, near)  8.06 us
    ppermute x2, waiting for transfers between devices, per_device(): relayed = lax.ppermute(sends[e], ROWS, over)  5.36 us
    ppermute x2, starting transfers between devices, row_halo(): above = lax.ppermute(tail, 'row', [(i, i + 1) for i in range(count - 1)])  4.96 us
    ppermute x2, starting transfers between devices, with_border(): got = [lax.ppermute(sides[0], 'col', [(0, 1), (1, 0)])]  4.69 us
    pallas_call x1, Pallas kernels, per_device(): pl.pallas_call(backward_kernel, grid=(rows // 16,), in_specs=[VM, VM], ou...  3.66 us
  transfers between devices with their start and end apart: 22, of which 8 were waited for; matrix products, arithmetic and copies ran while one was open for 0% of the time, Pallas kernels for 17%

profile of v6, /device:TPU:0, one launch (start us, length us, event | category | flops | bytes accessed | tf_op | source)
XLA Modules:
  0.0 97.4 jit_solution(17432309895026951045)
XLA Ops:
  1.4 2.4 %prep.1 = (bf16[2,64,64,128]{3,2,1,0:T(8,128)(2,1)S(1)}, bf16[2,4,64,128]{3,2,1,0:T(8,128)(2,1)S(1)}, bf16[2,4,64,128]{3,2,1,0:T(8,128)(2,1)S(1)}) custom-call(s32[7]{0:T(128)S(1)} %stack.31._.scal, bf16[64,64,256]{2,1,0:T(8,128)(2,1)} %x.1), custom_call_target="tpu_custom_call" | custom-call | flops 4400000000 | tf_op jit(solution)/shard_map/prep/pallas_call | solution.py:568
  5.2 3.0 %collective-permute-start = (bf16[2,4,64,128]{3,2,1,0:T(8,128)(2,1)S(1)}, bf16[2,4,64,128]{3,2,1,0:T(8,128)(2,1)S(1)}, u32[]{:S(2)}, u32[]{:S(2)}) collective-permute-start(bf16[2,4,64,128]{3,2,1,0:T(8,128)(2,1)S(1)} %get-tuple-element.46._), channel_id=1, source_target_pairs={{0,2},{2,4},{4,6},{6,8},{8,10},{10,12},{12,14},{1,3},{3,5},{5,7},{... | collective-permute-start | bytes 393224 | tf_op jit(solution)/shard_map/ppermute | solution.py:487
  10.1 3.0 %collective-permute-start.2 = (bf16[4,64,128]{2,1,0:T(8,128)(2,1)S(1)}, bf16[4,64,128]{2,1,0:T(8,128)(2,1)S(1)}, u32[]{:S(2)}, u32[]{:S(2)}) collective-permute-start(bf16[4,64,128]{2,1,0:T(8,128)(2,1)S(1)} %edges.2), channel_id=1, source_target_pairs={{0,1},{1,0},{2,3},{3,2},{4,5},{5,4},{6,7},{7,6},{8,9},{9,8},{10,11... | collective-permute-start | bytes 196616 | tf_op jit(solution)/shard_map/ppermute | solution.py:456
  15.4 1.7 %border.2.xs = bf16[2,72,192,128]{3,2,1,0:T(8,128)(2,1)S(1)} custom-call(s32[7]{0:T(128)S(1)} %stack.31._.scal, bf16[2,4,64,128]{3,2,1,0:T(8,128)(2,1)S(1)} %collective-permute-done.above, bf16[2,4,64,128]{3,2,1,0:T(8,128)(2,1)S(1)} %collective-permute-done.1.below, ...), custom_call_target="tpu_custom_call", output_to_operand_aliasing={{}: (4, {})} | custom-call | flops 1650000000 | tf_op jit(solution)/shard_map/border/pallas_call | solution.py:28
  17.1 2.1 %forward.3 = (bf16[64,64,128]{2,1,0:T(8,128)(2,1)S(1)}, bf16[64,64,128]{2,1,0:T(8,128)(2,1)S(1)}, f32[2880,128]{1,0:T(8,128)S(1)}, bf16[19,64,128]{2,1,0:T(8,128)(2,1)S(1)}, bf16[19,64,128]{2,1,0:T(8,128)(2,1)S(1)}) custom-call(s32[7]{0:T(128)S(1)} %stack.31._.scal, bf16[2,72,192,128]{3,2,1,0:T(8,128)(2,1)S(1)} %border.2.xs, ...), custom_call_target="tpu_custom_call" | custom-call | flops 6600000000 | tf_op jit(solution)/shard_map/forward/pallas_call | solution.py:28
  20.5 2.1 %forward.2 = (bf16[64,64,128]{2,1,0:T(8,128)(2,1)S(1)}, bf16[64,64,128]{2,1,0:T(8,128)(2,1)S(1)}, f32[2880,128]{1,0:T(8,128)S(1)}, bf16[19,64,128]{2,1,0:T(8,128)(2,1)S(1)}, bf16[19,64,128]{2,1,0:T(8,128)(2,1)S(1)}) custom-call(s32[7]{0:T(128)S(1)} %stack.31._.scal, bf16[2,72,192,128]{3,2,1,0:T(8,128)(2,1)S(1)} %border.2.xs, ...), custom_call_target="tpu_custom_call" | custom-call | flops 6600000000 | tf_op jit(solution)/shard_map/forward/pallas_call | solution.py:28
  23.9 1.6 %collective-permute-start.7 = (bf16[19,64,128]{2,1,0:T(8,128)(2,1)S(1)}, bf16[19,64,128]{2,1,0:T(8,128)(2,1)S(1)}, u32[]{:S(2)}, u32[]{:S(2)}) collective-permute-start(bf16[19,64,128]{2,1,0:T(8,128)(2,1)S(1)} %get-tuple-element.64), channel_id=1, source_target_pairs={{1,8},{3,10},{5,12},{7,14},{8,1},{10,3},{12,5},{14,7},{0,2},{2,0},... | collective-permute-start | bytes 933896 | tf_op jit(solution)/shard_map/ppermute | solution.py:634
  25.5 5.4 %collective-permute-done.8 = bf16[19,64,128]{2,1,0:T(8,128)(2,1)S(1)} collective-permute-done((bf16[19,64,128]{2,1,0:T(8,128)(2,1)S(1)}, bf16[19,64,128]{2,1,0:T(8,128)(2,1)S(1)}, u32[]{:S(2)}, u32[]{:S(2)}) %collective-permute-start.8) | collective-permute-done | bytes 311328 | tf_op jit(solution)/shard_map/ppermute | solution.py:639
  32.2 8.1 %collective-permute-start.4 = (bf16[19,64,128]{2,1,0:T(8,128)(2,1)S(1)}, bf16[19,64,128]{2,1,0:T(8,128)(2,1)S(1)}, u32[]{:S(2)}, u32[]{:S(2)}) collective-permute-start(bf16[19,64,128]{2,1,0:T(8,128)(2,1)S(1)} %get-tuple-element.58), channel_id=1, source_target_pairs={{0,6},{2,4},{4,2},{6,0},{9,15},{11,13},{13,11},{15,9},{16,22},{18,... | collective-permute-start | bytes 933896 | tf_op jit(solution)/shard_map/ppermute | solution.py:638
  40.3 1.8 %collective-permute-start.3 = (bf16[19,64,128]{2,1,0:T(8,128)(2,1)S(1)}, bf16[19,64,128]{2,1,0:T(8,128)(2,1)S(1)}, u32[]{:S(2)}, u32[]{:S(2)}) collective-permute-start(bf16[19,64,128]{2,1,0:T(8,128)(2,1)S(1)} %get-tuple-element.57), channel_id=1, source_target_pairs={{0,4},{1,12},{2,6},{3,14},{4,0},{5,8},{6,2},{7,10},{8,5},{9,13},{1... | collective-permute-start | bytes 933896 | tf_op jit(solution)/shard_map/ppermute | solution.py:627
  43.4 2.7 %middle.2 = (bf16[2,64,64,128]{3,2,1,0:T(8,128)(2,1)S(1)}, f32[64,128]{1,0:T(8,128)S(1)}) custom-call(s32[7]{0:T(128)S(1)} %stack.31._.scal, f32[37]{0:T(128)S(1)} %copy-done.4, f32[40,72,128]{2,1,0:T(8,128)S(1)} %bitcast.14, bf16[64,64,128]{2,1,0:T(8,128)(2,1)S(1)} %get-tuple-element.61.hid, bf16[64,64,128]{2,1,0:T(8,128)(2,1)S(1)} %get-tuple-element.62.slope, ...), custom_call_target="tpu_custom_call" | custom-call | flops 5500000256 | tf_op jit(solution)/shard_map/middle/pallas_call | solution.py:28
  46.1 1.7 %weights.2.rest_7_.rest_0_ = f32[192,192]{1,0:T(8,128)S(1)} custom-call(s32[7]{0:T(128)S(1)} %stack.31._.scal, bf16[2,72,192,128]{3,2,1,0:T(8,128)(2,1)S(1)} %border.2.xs, bf16[2,64,64,128]{3,2,1,0:T(8,128)(2,1)S(1)} %get-tuple-element.65.dpre.rest_5_, f32[64,128]{1,0:T(8,128)S(1)} %get-tuple-element.66.small.rest_6_), custom_call_target="tpu_custom_call" | custom-call | flops 2750000128 | tf_op jit(solution)/shard_map/weights/pallas_call | solution.py:28
  47.8 16.4 %collective-permute-done.3.rest_0_ = bf16[19,64,128]{2,1,0:T(8,128)(2,1)S(1)} collective-permute-done((bf16[19,64,128]{2,1,0:T(8,128)(2,1)S(1)}, bf16[19,64,128]{2,1,0:T(8,128)(2,1)S(1)}, u32[]{:S(2)}, u32[]{:S(2)}) %collective-permute-start.3) | collective-permute-done | bytes 311328 | tf_op jit(solution)/shard_map/ppermute | solution.py:627
  64.2 2.7 %middle.3 = (bf16[2,64,64,128]{3,2,1,0:T(8,128)(2,1)S(1)}, f32[64,128]{1,0:T(8,128)S(1)}, bf16[2,4,64,128]{3,2,1,0:T(8,128)(2,1)S(1)}, bf16[2,4,64,128]{3,2,1,0:T(8,128)(2,1)S(1)}) custom-call(s32[7]{0:T(128)S(1)} %stack.31._.scal, f32[37]{0:T(128)S(1)} %copy-done.4, f32[40,72,128]{2,1,0:T(8,128)S(1)} %bitcast.13, ...), custom_call_target="tpu_custom_call", output_to_operand_aliasing={{0}: (11, {})} | custom-call | flops 5500000256 | tf_op jit(solution)/shard_map/middle/pallas_call | solution.py:28
  66.8 1.9 %collective-permute-start.10 = (bf16[2,4,64,128]{3,2,1,0:T(8,128)(2,1)S(1)}, bf16[2,4,64,128]{3,2,1,0:T(8,128)(2,1)S(1)}, u32[]{:S(2)}, u32[]{:S(2)}) collective-permute-start(bf16[2,4,64,128]{3,2,1,0:T(8,128)(2,1)S(1)} %get-tuple-element.67), channel_id=1, source_target_pairs={{0,2},{2,4},{4,6},{6,8},{8,10},{10,12},{12,14},{1,3},{3,5},{5,7},{... | collective-permute-start | bytes 393224 | tf_op jit(solution)/shard_map/ppermute | solution.py:487
  68.8 1.5 %collective-permute-start.11 = (bf16[2,4,64,128]{3,2,1,0:T(8,128)(2,1)S(1)}, bf16[2,4,64,128]{3,2,1,0:T(8,128)(2,1)S(1)}, u32[]{:S(2)}, u32[]{:S(2)}) collective-permute-start(bf16[2,4,64,128]{3,2,1,0:T(8,128)(2,1)S(1)} %get-tuple-element.68), channel_id=1, source_target_pairs={{2,0},{4,2},{6,4},{8,6},{10,8},{12,10},{14,12},{3,1},{5,3},{7,5},{... | collective-permute-start | bytes 393224 | tf_op jit(solution)/shard_map/ppermute | solution.py:488
  70.3 1.8 %weights.3 = (f32[88,128]{1,0:T(8,128)S(1)}, f32[88,128]{1,0:T(8,128)S(1)}, f32[88,128]{1,0:T(8,128)S(1)}, f32[88,128]{1,0:T(8,128)S(1)}) custom-call(s32[7]{0:T(128)S(1)} %stack.31._.scal, bf16[2,72,192,128]{3,2,1,0:T(8,128)(2,1)S(1)} %border.2.xs, bf16[2,64,64,128]{3,2,1,0:T(8,128)(2,1)S(1)} %get-tuple-element.69.field.dpre, ...), custom_call_target="tpu_custom_call" | custom-call | flops 2750000128 | tf_op jit(solution)/shard_map/weights/pallas_call | solution.py:28
  73.0 3.5 %collective-permute-start.13 = (f32[88,128]{1,0:T(8,128)S(1)}, f32[88,128]{1,0:T(8,128)S(1)}, u32[]{:S(2)}, u32[]{:S(2)}) collective-permute-start(f32[88,128]{1,0:T(8,128)S(1)} %get-tuple-element.78), channel_id=1, source_target_pairs={{0,1},{1,0},{2,3},{3,2},{4,5},{5,4},{6,7},{7,6},{8,9},{9,8},{10,11... | collective-permute-start | bytes 135176 | tf_op jit(solution)/shard_map/ppermute | solution.py:506
  76.5 2.7 %collective-permute-start.14 = (f32[88,128]{1,0:T(8,128)S(1)}, f32[88,128]{1,0:T(8,128)S(1)}, u32[]{:S(2)}, u32[]{:S(2)}) collective-permute-start(f32[88,128]{1,0:T(8,128)S(1)} %get-tuple-element.79), channel_id=1, source_target_pairs={{0,2},{1,3},{2,0},{3,1},{4,6},{5,7},{6,4},{7,5},{8,10},{9,11},{10,... | collective-permute-start | bytes 135176 | tf_op jit(solution)/shard_map/ppermute | solution.py:506
  80.5 1.7 %collective-permute-start.12 = (bf16[3,64,128]{2,1,0:T(8,128)(2,1)S(1)}, bf16[3,64,128]{2,1,0:T(8,128)(2,1)S(1)}, u32[]{:S(2)}, u32[]{:S(2)}) collective-permute-start(bf16[3,64,128]{2,1,0:T(8,128)(2,1)S(1)} %edges.3), channel_id=1, source_target_pairs={{0,1},{1,0},{2,3},{3,2},{4,5},{5,4},{6,7},{7,6},{8,9},{9,8},{10,11... | collective-permute-start | bytes 147464 | tf_op jit(solution)/shard_map/ppermute | solution.py:456
  85.5 1.7 %border.3.ds = bf16[2,72,192,128]{3,2,1,0:T(8,128)(2,1)S(1)} custom-call(s32[7]{0:T(128)S(1)} %stack.31._.scal, bf16[2,4,64,128]{3,2,1,0:T(8,128)(2,1)S(1)} %collective-permute-done.10.above, bf16[2,4,64,128]{3,2,1,0:T(8,128)(2,1)S(1)} %collective-permute-done.11.below, ...), custom_call_target="tpu_custom_call", output_to_operand_aliasing={{}: (4, {})} | custom-call | flops 1650000000 | tf_op jit(solution)/shard_map/border/pallas_call | solution.py:28
  88.6 1.5 %collective-permute-done.16.refs_1_ = f32[88,128]{1,0:T(8,128)S(1)} collective-permute-done((f32[88,128]{1,0:T(8,128)S(1)}, f32[88,128]{1,0:T(8,128)S(1)}, u32[]{:S(2)}, u32[]{:S(2)}) %collective-permute-start.16) | collective-permute-done | bytes 45088 | tf_op jit(solution)/shard_map/ppermute | solution.py:510
  92.4 3.7 %backward.1 = bf16[64,64,256]{2,1,0:T(8,128)(2,1)} custom-call(bf16[2,72,192,128]{3,2,1,0:T(8,128)(2,1)S(1)} %border.3.ds, bf16[192,192]{1,0:T(8,128)(2,1)S(1)} %get-tuple-element.76.w), custom_call_target="tpu_custom_call" | custom-call | flops 6600000000 | tf_op jit(solution)/shard_map/backward/pallas_call | solution.py:698
  96.1 1.4 %unpack.1 = (f32[3,3,64,64]{3,2,1,0:T(8,128)}, f32[1,64]{1,0:T(1,128)}, f32[37,64]{1,0:T(8,128)}, f32[1,37]{1,0:T(1,128)}, f32[1,1]{1,0:T(1,128)}) custom-call(s32[7]{0:T(128)S(1)} %stack.31._.scal, f32[88,128]{1,0:T(8,128)S(1)} %sum.3.rest_0_, f32[88,128]{1,0:T(8,128)S(1)} %collective-permute-done.19.rest_1_, ...), custom_call_target="tpu_custom_call" | custom-call | flops 1100000000 | tf_op jit(solution)/shard_map/unpack/pallas_call | solution.py:710
  (49 shorter events, 19.8 us)
Async XLA Ops:
  1.4 6.8 %copy-start.2 = (bf16[37,64]{1,0:T(8,128)(2,1)S(1)}, bf16[37,64]{1,0:T(8,128)(2,1)}, u32[]{:S(2)}) copy-start(bf16[37,64]{1,0:T(8,128)(2,1)} %hw.1) | copy-start | bytes 14212
  3.9 5.2 %collective-permute-start.1 = (bf16[2,4,64,128]{3,2,1,0:T(8,128)(2,1)S(1)}, bf16[2,4,64,128]{3,2,1,0:T(8,128)(2,1)S(1)}, u32[]{:S(2)}, u32[]{:S(2)}) collective-permute-start(bf16[2,4,64,128]{3,2,1,0:T(8,128)(2,1)S(1)} %get-tuple-element.47), channel_id=1, source_target_pairs={{2,0},{4,2},{6,4},{8,6},{10,8},{12,10},{14,12},{3,1},{5,3},{7,5},{... | collective-permute-start | bytes 393224 | tf_op jit(solution)/shard_map/ppermute | solution.py:488
  5.2 4.0 %collective-permute-start = (bf16[2,4,64,128]{3,2,1,0:T(8,128)(2,1)S(1)}, bf16[2,4,64,128]{3,2,1,0:T(8,128)(2,1)S(1)}, u32[]{:S(2)}, u32[]{:S(2)}) collective-permute-start(bf16[2,4,64,128]{3,2,1,0:T(8,128)(2,1)S(1)} %get-tuple-element.46._), channel_id=1, source_target_pairs={{0,2},{2,4},{4,6},{6,8},{8,10},{10,12},{12,14},{1,3},{3,5},{5,7},{... | collective-permute-start | bytes 393224 | tf_op jit(solution)/shard_map/ppermute | solution.py:487
  10.1 5.3 %collective-permute-start.2 = (bf16[4,64,128]{2,1,0:T(8,128)(2,1)S(1)}, bf16[4,64,128]{2,1,0:T(8,128)(2,1)S(1)}, u32[]{:S(2)}, u32[]{:S(2)}) collective-permute-start(bf16[4,64,128]{2,1,0:T(8,128)(2,1)S(1)} %edges.2), channel_id=1, source_target_pairs={{0,1},{1,0},{2,3},{3,2},{4,5},{5,4},{6,7},{7,6},{8,9},{9,8},{10,11... | collective-permute-start | bytes 196616 | tf_op jit(solution)/shard_map/ppermute | solution.py:456
  19.2 24.2 %copy-start.4 = (f32[37]{0:T(128)S(1)}, f32[37]{0:T(128)}, u32[]{:S(2)}) copy-start(f32[37]{0:T(128)} %hb.3) | copy-start | bytes 448
  19.2 11.7 %collective-permute-start.8 = (bf16[19,64,128]{2,1,0:T(8,128)(2,1)S(1)}, bf16[19,64,128]{2,1,0:T(8,128)(2,1)S(1)}, u32[]{:S(2)}, u32[]{:S(2)}) collective-permute-start(bf16[19,64,128]{2,1,0:T(8,128)(2,1)S(1)} %get-tuple-element.63.rest_0_), channel_id=1, source_target_pairs={{1,0},{3,2},{5,4},{7,6},{8,9},{10,11},{12,13},{14,15},{17,16},{19,... | collective-permute-start | bytes 933896 | tf_op jit(solution)/shard_map/ppermute | solution.py:639
  22.6 19.5 %collective-permute-start.5 = (bf16[19,64,128]{2,1,0:T(8,128)(2,1)S(1)}, bf16[19,64,128]{2,1,0:T(8,128)(2,1)S(1)}, u32[]{:S(2)}, u32[]{:S(2)}) collective-permute-start(bf16[19,64,128]{2,1,0:T(8,128)(2,1)S(1)} %get-tuple-element.58), channel_id=1, source_target_pairs={{1,0},{3,2},{5,4},{7,6},{8,9},{10,11},{12,13},{14,15},{17,16},{19,... | collective-permute-start | bytes 933896 | tf_op jit(solution)/shard_map/ppermute | solution.py:639
  23.9 19.5 %collective-permute-start.7 = (bf16[19,64,128]{2,1,0:T(8,128)(2,1)S(1)}, bf16[19,64,128]{2,1,0:T(8,128)(2,1)S(1)}, u32[]{:S(2)}, u32[]{:S(2)}) collective-permute-start(bf16[19,64,128]{2,1,0:T(8,128)(2,1)S(1)} %get-tuple-element.64), channel_id=1, source_target_pairs={{1,8},{3,10},{5,12},{7,14},{8,1},{10,3},{12,5},{14,7},{0,2},{2,0},... | collective-permute-start | bytes 933896 | tf_op jit(solution)/shard_map/ppermute | solution.py:634
  30.8 12.5 %collective-permute-start.9 = (bf16[19,64,128]{2,1,0:T(8,128)(2,1)S(1)}, bf16[19,64,128]{2,1,0:T(8,128)(2,1)S(1)}, u32[]{:S(2)}, u32[]{:S(2)}) collective-permute-start(bf16[19,64,128]{2,1,0:T(8,128)(2,1)S(1)} %collective-permute-done.8), channel_id=1, source_target_pairs={{0,10},{2,8},{4,14},{6,12},{9,3},{11,1},{13,7},{15,5},{16,26},{18,... | collective-permute-start | bytes 933896 | tf_op jit(solution)/shard_map/ppermute | solution.py:640
  32.2 32.0 %collective-permute-start.4 = (bf16[19,64,128]{2,1,0:T(8,128)(2,1)S(1)}, bf16[19,64,128]{2,1,0:T(8,128)(2,1)S(1)}, u32[]{:S(2)}, u32[]{:S(2)}) collective-permute-start(bf16[19,64,128]{2,1,0:T(8,128)(2,1)S(1)} %get-tuple-element.58), channel_id=1, source_target_pairs={{0,6},{2,4},{4,2},{6,0},{9,15},{11,13},{13,11},{15,9},{16,22},{18,... | collective-permute-start | bytes 933896 | tf_op jit(solution)/shard_map/ppermute | solution.py:638
  40.3 23.9 %collective-permute-start.3 = (bf16[19,64,128]{2,1,0:T(8,128)(2,1)S(1)}, bf16[19,64,128]{2,1,0:T(8,128)(2,1)S(1)}, u32[]{:S(2)}, u32[]{:S(2)}) collective-permute-start(bf16[19,64,128]{2,1,0:T(8,128)(2,1)S(1)} %get-tuple-element.57), channel_id=1, source_target_pairs={{0,4},{1,12},{2,6},{3,14},{4,0},{5,8},{6,2},{7,10},{8,5},{9,13},{1... | collective-permute-start | bytes 933896 | tf_op jit(solution)/shard_map/ppermute | solution.py:627
  42.1 22.1 %collective-permute-start.6 = (bf16[19,64,128]{2,1,0:T(8,128)(2,1)S(1)}, bf16[19,64,128]{2,1,0:T(8,128)(2,1)S(1)}, u32[]{:S(2)}, u32[]{:S(2)}) collective-permute-start(bf16[19,64,128]{2,1,0:T(8,128)(2,1)S(1)} %collective-permute-done.5), channel_id=1, source_target_pairs={{0,14},{2,12},{4,10},{6,8},{9,7},{11,5},{13,3},{15,1},{16,30},{18,... | collective-permute-start | bytes 933896 | tf_op jit(solution)/shard_map/ppermute | solution.py:640
  66.8 5.2 %collective-permute-start.10 = (bf16[2,4,64,128]{3,2,1,0:T(8,128)(2,1)S(1)}, bf16[2,4,64,128]{3,2,1,0:T(8,128)(2,1)S(1)}, u32[]{:S(2)}, u32[]{:S(2)}) collective-permute-start(bf16[2,4,64,128]{3,2,1,0:T(8,128)(2,1)S(1)} %get-tuple-element.67), channel_id=1, source_target_pairs={{0,2},{2,4},{4,6},{6,8},{8,10},{10,12},{12,14},{1,3},{3,5},{5,7},{... | collective-permute-start | bytes 393224 | tf_op jit(solution)/shard_map/ppermute | solution.py:487
  68.8 3.3 %collective-permute-start.11 = (bf16[2,4,64,128]{3,2,1,0:T(8,128)(2,1)S(1)}, bf16[2,4,64,128]{3,2,1,0:T(8,128)(2,1)S(1)}, u32[]{:S(2)}, u32[]{:S(2)}) collective-permute-start(bf16[2,4,64,128]{3,2,1,0:T(8,128)(2,1)S(1)} %get-tuple-element.68), channel_id=1, source_target_pairs={{2,0},{4,2},{6,4},{8,6},{10,8},{12,10},{14,12},{3,1},{5,3},{7,5},{... | collective-permute-start | bytes 393224 | tf_op jit(solution)/shard_map/ppermute | solution.py:488
  73.0 9.2 %collective-permute-start.13 = (f32[88,128]{1,0:T(8,128)S(1)}, f32[88,128]{1,0:T(8,128)S(1)}, u32[]{:S(2)}, u32[]{:S(2)}) collective-permute-start(f32[88,128]{1,0:T(8,128)S(1)} %get-tuple-element.78), channel_id=1, source_target_pairs={{0,1},{1,0},{2,3},{3,2},{4,5},{5,4},{6,7},{7,6},{8,9},{9,8},{10,11... | collective-permute-start | bytes 135176 | tf_op jit(solution)/shard_map/ppermute | solution.py:506
  76.5 5.7 %collective-permute-start.14 = (f32[88,128]{1,0:T(8,128)S(1)}, f32[88,128]{1,0:T(8,128)S(1)}, u32[]{:S(2)}, u32[]{:S(2)}) collective-permute-start(f32[88,128]{1,0:T(8,128)S(1)} %get-tuple-element.79), channel_id=1, source_target_pairs={{0,2},{1,3},{2,0},{3,1},{4,6},{5,7},{6,4},{7,5},{8,10},{9,11},{10,... | collective-permute-start | bytes 135176 | tf_op jit(solution)/shard_map/ppermute | solution.py:506
  79.3 3.8 %collective-permute-start.15 = (f32[88,128]{1,0:T(8,128)S(1)}, f32[88,128]{1,0:T(8,128)S(1)}, u32[]{:S(2)}, u32[]{:S(2)}) collective-permute-start(f32[88,128]{1,0:T(8,128)S(1)} %get-tuple-element.80), channel_id=1, source_target_pairs={{0,3},{1,2},{2,1},{3,0},{4,7},{5,6},{6,5},{7,4},{8,11},{9,10},{10,... | collective-permute-start | bytes 135176 | tf_op jit(solution)/shard_map/ppermute | solution.py:506
  80.5 5.0 %collective-permute-start.12 = (bf16[3,64,128]{2,1,0:T(8,128)(2,1)S(1)}, bf16[3,64,128]{2,1,0:T(8,128)(2,1)S(1)}, u32[]{:S(2)}, u32[]{:S(2)}) collective-permute-start(bf16[3,64,128]{2,1,0:T(8,128)(2,1)S(1)} %edges.3), channel_id=1, source_target_pairs={{0,1},{1,0},{2,3},{3,2},{4,5},{5,4},{6,7},{7,6},{8,9},{9,8},{10,11... | collective-permute-start | bytes 147464 | tf_op jit(solution)/shard_map/ppermute | solution.py:456
  83.1 4.6 %collective-permute-start.18 = (f32[88,128]{1,0:T(8,128)S(1)}, f32[88,128]{1,0:T(8,128)S(1)}, u32[]{:S(2)}, u32[]{:S(2)}) collective-permute-start(f32[88,128]{1,0:T(8,128)S(1)} %sum.2.refs_0_), channel_id=1, source_target_pairs={{0,12},{2,14},{4,0},{6,2},{8,4},{10,6},{12,8},{14,10},{1,13},{3,15... | collective-permute-start | bytes 135176 | tf_op jit(solution)/shard_map/ppermute | solution.py:510
  83.1 5.5 %collective-permute-start.17 = (f32[88,128]{1,0:T(8,128)S(1)}, f32[88,128]{1,0:T(8,128)S(1)}, u32[]{:S(2)}, u32[]{:S(2)}) collective-permute-start(f32[88,128]{1,0:T(8,128)S(1)} %sum.2.refs_0_), channel_id=1, source_target_pairs={{0,8},{2,10},{4,12},{6,14},{8,0},{10,2},{12,4},{14,6},{1,9},{3,11}... | collective-permute-start | bytes 135176 | tf_op jit(solution)/shard_map/ppermute | solution.py:510
  84.3 5.8 %collective-permute-start.16 = (f32[88,128]{1,0:T(8,128)S(1)}, f32[88,128]{1,0:T(8,128)S(1)}, u32[]{:S(2)}, u32[]{:S(2)}) collective-permute-start(f32[88,128]{1,0:T(8,128)S(1)} %sum.2.refs_0_), channel_id=1, source_target_pairs={{0,4},{2,6},{4,8},{6,10},{8,12},{10,14},{12,0},{14,2},{1,5},{3,7},... | collective-permute-start | bytes 135176 | tf_op jit(solution)/shard_map/ppermute | solution.py:510
  90.2 5.9 %collective-permute-start.21 = (f32[88,128]{1,0:T(8,128)S(1)}, f32[88,128]{1,0:T(8,128)S(1)}, u32[]{:S(2)}, u32[]{:S(2)}) collective-permute-start(f32[88,128]{1,0:T(8,128)S(1)} %sum.3.rest_0_), channel_id=1, source_target_pairs={{0,3},{1,2},{2,1},{3,0},{4,7},{5,6},{6,5},{7,4},{8,11},{9,10},{10,... | collective-permute-start | bytes 135176 | tf_op jit(solution)/shard_map/ppermute | solution.py:506
  90.3 5.8 %collective-permute-start.20 = (f32[88,128]{1,0:T(8,128)S(1)}, f32[88,128]{1,0:T(8,128)S(1)}, u32[]{:S(2)}, u32[]{:S(2)}) collective-permute-start(f32[88,128]{1,0:T(8,128)S(1)} %sum.3.rest_0_), channel_id=1, source_target_pairs={{0,2},{1,3},{2,0},{3,1},{4,6},{5,7},{6,4},{7,5},{8,10},{9,11},{10,... | collective-permute-start | bytes 135176 | tf_op jit(solution)/shard_map/ppermute | solution.py:506
  91.2 4.8 %collective-permute-start.19 = (f32[88,128]{1,0:T(8,128)S(1)}, f32[88,128]{1,0:T(8,128)S(1)}, u32[]{:S(2)}, u32[]{:S(2)}) collective-permute-start(f32[88,128]{1,0:T(8,128)S(1)} %sum.3.rest_0_), channel_id=1, source_target_pairs={{0,1},{1,0},{2,3},{3,2},{4,5},{5,4},{6,7},{7,6},{8,9},{9,8},{10,11... | collective-permute-start | bytes 135176 | tf_op jit(solution)/shard_map/ppermute | solution.py:506
  (3 other events, 20.5 us)
